TPU v7x, 512 devices: a whole 4x8x8 slice. The times are simulated.
512 devices in a mesh: ex: 16 (over z, x_hi), feat: 32 (over x_lo, y, core).
Axes of the slice: x: 4 (x_hi: 2, x_lo: 2; x = x_hi * 2 + x_lo), y: 8, z: 8, core: 2. Of those that a mesh axis runs over, the one named last changes fastest.
Arguments:
- features: bfloat16 [16384, 2048], P('ex', 'feat')
- centre_index: int32 [32, 16, 16], P(None, 'ex'), may hold values from 0 to 16383, as said below
- labels: int32 [16384], P('ex'), may hold values from 0 to 15
- precond: float32 [8192, 256], P('feat'), as said below
Outputs:
- predictions: float32 [16384, 16], P('ex')
Inputs may be any that keep to these rules, and one draw needn't show every extreme that they name: centre_index[j, i, c] lies among the examples i * 1024 to (i + 1) * 1024 - 1, and all entries are different. Each 256 x 256 block of precond is symmetric, and its diagonal entry exceeds the sum of the magnitudes of the other entries of its row by at least half of itself.
All inputs are finite; a program needn't handle non-finite values.
Results may differ from a plain program's by a relative error of at most 0.0003.
Values may be sent and summed in bfloat16 or wider, within the bound.
No kernel may reach another device: no remote copies, remote signals or barrier semaphores. Data moves between devices by JAX's collectives and lax.ppermute only.
A program may use at most 64 MiB of HBM per device.

v0:
```python
import jax
import jax.numpy as jnp
from jax import lax
from jax.sharding import PartitionSpec as P

CLASS_COUNT = 16
ITERS = 2


GAMMA = 4.0
LAMBDA = 0.05
EPS = 1e-06
HIGH = lax.Precision.HIGHEST


def assemble(picked):
    whole = lax.all_gather(picked, "ex", axis=0, tiled=True)
    return whole.reshape(whole.shape[0] * whole.shape[1], whole.shape[2])


def mean_squares(block):
    return jnp.sum(jnp.square(block.astype(jnp.float32)), axis=1)


def residual_sum(residual, precon_res):
    return lax.psum(jnp.sum(residual * precon_res, axis=0), "feat")


def per_device(features, centre_index, labels, precond):
    rows_dev = features.shape[0]
    feat_count = lax.axis_size("feat")
    ex_count = lax.axis_size("ex")
    ex_index = lax.axis_index("ex")
    feat_index = lax.axis_index("feat")
    full_width = features.shape[1] * feat_count
    examples = rows_dev * ex_count
    classes = CLASS_COUNT
    local_all = centre_index[:, 0, :] - ex_index * rows_dev
    own_rows = lax.dynamic_index_in_dim(local_all, feat_index, 0, keepdims=False)
    block_size = precond.shape[0]
    gathered = lax.all_gather(features, "feat", axis=1, tiled=True)
    centres = assemble(jnp.take(gathered, own_rows, axis=0)[None])
    row_sq = mean_squares(gathered)
    dots = jnp.dot(gathered, centres.T, preferred_element_type=jnp.float32)
    row_scale = lax.rsqrt(row_sq / full_width + EPS)
    centre_scale = lax.rsqrt(mean_squares(centres) / full_width + EPS)
    cosine = jnp.clip(dots * row_scale[:, None] * centre_scale[None, :], -1.0, 1.0)
    panel = jnp.exp(GAMMA * (cosine - 1.0))
    onehot = (labels[:, None] == jnp.arange(classes, dtype=jnp.int32)[None, :]).astype(jnp.float32)
    targets = classes * onehot - 1.0
    rhs = lax.psum(jnp.dot(panel.T, targets, precision=HIGH) / examples, "ex")
    slot_mask = (lax.iota(jnp.int32, ex_count) == ex_index)[:, None, None]

    def apply_pre(residual_vector):
        return jnp.dot(precond, residual_vector, precision=HIGH)

    fitted = jnp.zeros((rows_dev, classes), jnp.float32)
    residual = rhs
    precon_res = apply_pre(residual)
    direction = precon_res
    rz_now = residual_sum(residual, precon_res)
    for step in range(ITERS):
        part_prod = jnp.dot(panel, direction, precision=HIGH)
        kvec = lax.psum(part_prod, "feat")
        own_vals = jnp.take(kvec, own_rows, axis=0)
        placed = jnp.where(slot_mask, own_vals[None, :, :], 0.0).reshape(block_size, classes)
        term = jnp.dot(panel.T, kvec, precision=HIGH) / examples + LAMBDA * placed
        image = lax.psum(term, "ex")
        alpha = rz_now / lax.psum(jnp.sum(direction * image, axis=0), "feat")
        fitted = fitted + alpha * kvec
        residual = residual - alpha * image
        precon_res = apply_pre(residual)
        rz_next = residual_sum(residual, precon_res)
        direction = precon_res + rz_next / rz_now * direction
        rz_now = rz_next
    return fitted


def solution(mesh):
    in_specs = (P("ex", "feat"), P(None, "ex", None), P("ex"), P("feat", None))
    out_specs = P("ex", None)
    return jax.shard_map(
        per_device, mesh=mesh, in_specs=in_specs, out_specs=out_specs, check_vma=False
    )
```

profile of v0, /device:TPU:1, one launch (start us, length us, event | category | flops | bytes accessed | tf_op | source)
XLA Modules:
  0.0 982.6 jit_solution(15239277550528236983)
XLA Ops:
  7.3 0.9 fusion.16
  8.2 76.4 %all-gather.3.cloned.1.call-done = bf16[1024,2048]{0,1:T(8,128)(2,1)} async-done(((bf16[1024,64]{0,1:T(8,128)(2,1)}), bf16[1024,2048]{0,1:T(8,128)(2,1)}) %all-gather.3.cloned.1.call-update) | async-done | bytes 4194320 | tf_op jit(solution)/shard_map/all_gather | solution.py:41
  84.6 6.5 copy.15
  91.1 3.4 gather_fusion
  95.5 3.1 multiply_reduce_fusion
  98.6 77.7 %all-gather.5.cloned.1.call-done = bf16[16,16,2048]{2,1,0:T(8,128)(2,1)} async-done(((bf16[1,16,2048]{2,1,0:T(8,128)(2,1)}), bf16[16,16,2048]{2,1,0:T(8,128)(2,1)}) %all-gather.5.cloned.1.call-update) | async-done | bytes 1048592 | tf_op jit(solution)/shard_map/all_gather | solution.py:17
  176.3 1.5 multiply_reduce_fusion.1
  177.9 3.9 fusion.4
  181.8 1.2 convolution_multiply_fusion.1
  182.9 59.1 %psum.63 = f32[256,16]{0,1:T(8,128)S(1)} all-reduce(f32[256,16]{0,1:T(8,128)S(1)} %convolution_multiply_fusion.1), channel_id=1, replica_groups=mesh['ex'=16,'feat'=32] {'ex'}, use_global_device_ids=true, to_apply=%region_2.3 | all-reduce | flops 4096 | bytes 32768 | tf_op jit(solution)/shard_map/psum | solution.py:51
  242.3 1.3 fusion.24
  243.7 214.6 %all-reduce.4.cloned.1.call-done = f32[1024,16]{0,1:T(8,128)} async-done(((f32[1024,16]{0,1:T(8,128)}), f32[1024,16]{0,1:T(8,128)}) %all-reduce.4.cloned.1.call-update) | async-done | bytes 65552 | tf_op jit(solution)/shard_map/psum | solution.py:64
  458.4 1.1 copy.16
  460.3 1.8 fusion.6
  462.1 63.3 %psum.66 = f32[256,16]{0,1:T(8,128)S(1)} all-reduce(f32[256,16]{0,1:T(8,128)S(1)} %fusion.6), channel_id=1, replica_groups=mesh['ex'=16,'feat'=32] {'ex'}, use_global_device_ids=true, to_apply=%region_6.8 | all-reduce | flops 4096 | bytes 32768 | tf_op jit(solution)/shard_map/psum | solution.py:68
  525.5 68.5 %all-reduce = (f32[16]{0:T(128)S(1)}, f32[16]{0:T(128)S(1)}) all-reduce(f32[16]{0:T(128)S(1)} %get-tuple-element.7, f32[16]{0:T(128)S(1)} %get-tuple-element.6), channel_id=1, replica_groups=mesh['ex'=16,'feat'=32] {'feat'}, use_global_device_ids=true, to_apply=%region_4.5 | all-reduce | flops 32 | bytes 256 | tf_op jit(solution)/shard_map/psum | solution.py:26
  594.5 53.0 %psum.68 = f32[16]{0:T(128)S(1)} all-reduce(f32[16]{0:T(128)S(1)} %get-tuple-element.10), channel_id=1, replica_groups=mesh['ex'=16,'feat'=32] {'feat'}, use_global_device_ids=true, to_apply=%region_10.12 | all-reduce | flops 16 | bytes 128 | tf_op jit(solution)/shard_map/psum | solution.py:26
  647.5 1.3 fusion.17
  648.9 190.0 %all-reduce.6.cloned.1.call-done = f32[1024,16]{0,1:T(8,128)} async-done(((f32[1024,16]{0,1:T(8,128)}), f32[1024,16]{0,1:T(8,128)}) %all-reduce.6.cloned.1.call-update) | async-done | bytes 65552 | tf_op jit(solution)/shard_map/psum | solution.py:64
  838.8 1.0 copy.18
  840.7 1.8 fusion.5
  842.5 63.3 %psum.70 = f32[256,16]{0,1:T(8,128)S(1)} all-reduce(f32[256,16]{0,1:T(8,128)S(1)} %fusion.5), channel_id=1, replica_groups=mesh['ex'=16,'feat'=32] {'ex'}, use_global_device_ids=true, to_apply=%region_12.14 | all-reduce | flops 4096 | bytes 32768 | tf_op jit(solution)/shard_map/psum | solution.py:68
  906.0 68.5 %psum.71 = f32[16]{0:T(128)S(1)} all-reduce(f32[16]{0:T(128)S(1)} %multiply_reduce_fusion.2), channel_id=1, replica_groups=mesh['ex'=16,'feat'=32] {'feat'}, use_global_device_ids=true, to_apply=%region_14.16 | all-reduce | flops 16 | bytes 128 | tf_op jit(solution)/shard_map/psum | solution.py:69
  974.5 1.6 multiply_add_fusion
  (43 shorter events, 4.6 us)
Async XLA Ops:
  6.5 235.5 %copy-start = (f32[256,256]{1,0:T(8,128)S(1)}, f32[256,256]{1,0:T(8,128)}, u32[]{:S(2)}) copy-start(f32[256,256]{1,0:T(8,128)} %param.9) | copy-start | bytes 786436
  6.5 78.1 %all-gather.3.cloned.1.call-start = ((), (), s32[]{:S(2)}) async-start(), calls=%async_computation | async-start | bytes 4325376 | tf_op jit(solution)/shard_map/all_gather | solution.py:41
  7.3 169.0 %all-gather.5.cloned.1.call-start = ((), (), s32[]{:S(2)}) async-start(), calls=%async_computation.1 | async-start | bytes 1114112 | tf_op jit(solution)/shard_map/all_gather | solution.py:17
  95.2 363.1 %all-reduce.4.cloned.1.call-start = ((), (), s32[]{:S(2)}) async-start(), calls=%async_computation.2 | async-start | bytes 131072 | tf_op jit(solution)/shard_map/psum | solution.py:64
  177.8 4.0 copy-start.2
  243.6 595.2 %all-reduce.6.cloned.1.call-start = ((), (), s32[]{:S(2)}) async-start(), calls=%async_computation.3 | async-start | bytes 131072 | tf_op jit(solution)/shard_map/psum | solution.py:64
  458.3 516.2 %copy-start.1 = (f32[1024,16]{0,1:T(8,128)S(1)}, f32[1024,16]{0,1:T(8,128)}, u32[]{:S(2)}) copy-start(f32[1024,16]{0,1:T(8,128)} %all-reduce.4.cloned.1.call-done) | copy-start | bytes 196612
Sparse Core Ops, SparseCore 0:
  9.5 75.0 all-gather.2
  95.4 80.8 all-gather.4
  243.8 214.5 all-reduce.3
  649.0 189.7 all-reduce.5
where the time goes:
time: 983 us
  waiting for transfers between devices  559 us (57%)
  blocking collectives  376 us (38%)
  local copies, waits for them, and re-layouts  13.8 us (1%)
  between operations  13.3 us (1%)
  matrix products  11.9 us (1%)
    psum x2, waiting for transfers between devices, per_device(): kvec = lax.psum(part_prod, 'feat')  405 us
    psum x2, blocking collectives, per_device(): image = lax.psum(term, 'ex')  127 us
    psum x2, blocking collectives, residual_sum(): return lax.psum(jnp.sum(residual * precon_res, axis=0), 'feat')  122 us
    all_gather x1, waiting for transfers between devices, assemble(): whole = lax.all_gather(picked, 'ex', axis=0, tiled=True)  77.7 us
    all_gather x1, waiting for transfers between devices, per_device(): gathered = lax.all_gather(features, 'feat', axis=1, tiled=True)  76.4 us
    psum x1, blocking collectives, per_device(): alpha = rz_now / lax.psum(jnp.sum(direction * image, axis=0), 'feat')  68.5 us
    psum x1, blocking collectives, per_device(): rhs = lax.psum(jnp.dot(panel.T, targets, precision=HIGH) / examples, 'ex')  59.1 us
  transfers between devices with their start and end apart: 4, of which 4 were waited for; matrix products, arithmetic and copies ran while one was open for 0% of the time, Pallas kernels for 0%

commit v1 on v0

v1 whole, which is shorter than its diff:
```python
import functools

import jax
import jax.numpy as jnp
from jax import lax
from jax.experimental import pallas as pl
from jax.experimental.pallas import tpu as pltpu
from jax.sharding import Mesh, PartitionSpec as P

CLASSES = 16
GAMMA = 4.0
LAMBDA = 0.05
EPS = 1e-06
HIGH = lax.Precision.HIGHEST
F32 = jnp.float32
BF16 = jnp.bfloat16

ROWS = 1024
BLOCK = 256
OWN = 16
N_EX = 16
N_FEAT = 32
N_PLANE = 16
SLICE = 64
WIDTH = N_PLANE * SLICE
F = 2048
EXAMPLES = ROWS * N_EX

EX = ("z", "xh")
PLANE = ("xl", "y")
FEAT = ("xl", "y", "c")

LANES = (((1,), (1,)), ((), ()))


def dot_t(a, b, precision=HIGH):
    return lax.dot_general(a, b, LANES, precision=precision, preferred_element_type=F32)


def iota(shape, dim):
    return lax.broadcasted_iota(jnp.int32, shape, dim)


def to_row(col, offset=0):
    n = col.shape[0]
    place = iota((n, 128), 1) == iota((n, 128), 0) + offset
    return jnp.sum(jnp.where(place, col, 0.0), axis=0, keepdims=True)


def to_col(row, n, offset=0):
    place = iota((n, 128), 1) == iota((n, 128), 0) + offset
    return jnp.sum(jnp.where(place, row, 0.0), axis=1, keepdims=True)


def call(kernel, outs, *args, name, smem=0):
    spec = [pl.BlockSpec(memory_space=pltpu.SMEM)] * smem
    spec += [pl.BlockSpec(memory_space=pltpu.VMEM)] * (len(args) - smem)
    many = isinstance(outs, list)
    out_spec = pl.BlockSpec(memory_space=pltpu.VMEM)
    return pl.pallas_call(
        kernel,
        out_shape=[jax.ShapeDtypeStruct(s, d) for s, d in outs] if many else jax.ShapeDtypeStruct(*outs),
        in_specs=spec,
        out_specs=[out_spec] * len(outs) if many else out_spec,
        name=name,
    )(*args)


def pick_kernel(ft_ref, own_ref, other_ref, out_ref):
    ft = ft_ref[...]
    zero = jnp.zeros_like(ft)
    n = N_PLANE * OWN
    lane = iota((n, ROWS), 1)

    def chosen(index_ref, table):
        mask = (lane == index_ref[...]).astype(F32).astype(BF16)
        return lax.dot_general(mask, table, LANES, preferred_element_type=F32)

    both = chosen(own_ref, jnp.concatenate([ft, zero], axis=0))
    both = both + chosen(other_ref, jnp.concatenate([zero, ft], axis=0))
    out_ref[...] = both.astype(BF16).reshape(N_PLANE, OWN, 2 * SLICE)


def spread_kernel(in_ref, out_ref):
    low = iota((OWN, 128), 1) < SLICE
    for t in range(N_PLANE // 2):
        a = in_ref[2 * t].astype(F32)
        b = in_ref[2 * t + 1].astype(F32)
        own = jnp.where(low, a, pltpu.roll(b, SLICE, 1)).astype(BF16)
        other = jnp.where(low, pltpu.roll(a, SLICE, 1), b).astype(BF16)
        cols = slice(128 * t, 128 * t + 128)
        for i in range(N_EX):
            out_ref[i, 0:OWN, cols] = own
            out_ref[i, OWN : 2 * OWN, cols] = other


def half_dots(ft_ref, cen_ref, first):
    block = cen_ref[:, first : first + OWN, :].reshape(BLOCK, WIDTH)
    dots = jnp.dot(block, ft_ref[...], preferred_element_type=F32)
    squares = jnp.sum(jnp.square(block.astype(F32)), axis=1, keepdims=True)
    return dots, squares


def other_kernel(ft_ref, cen_ref, out_ref):
    dots, squares = half_dots(ft_ref, cen_ref, OWN)
    out_ref[0:BLOCK, :] = dots
    out_ref[BLOCK : BLOCK + 8, :] = jnp.zeros((8, ROWS), F32)
    out_ref[BLOCK : BLOCK + 1, :] = jnp.sum(jnp.square(ft_ref[...].astype(F32)), axis=0, keepdims=True)
    same = iota((BLOCK, BLOCK), 0) == iota((BLOCK, BLOCK), 1)
    out_ref[BLOCK + 1 : BLOCK + 2, 0:BLOCK] = jnp.sum(jnp.where(same, squares, 0.0), axis=0, keepdims=True)


def own_kernel(ft_ref, cen_ref, dots_ref, squares_ref):
    dots, squares = half_dots(ft_ref, cen_ref, 0)
    dots_ref[...] = dots
    squares_ref[...] = jnp.broadcast_to(squares, (BLOCK, 128))


def panel_kernel(dots_ref, squares_ref, sent_ref, recv_ref, labels_ref, loc_ref, panel_ref, normal_ref, out_ref):
    row_sq = sent_ref[BLOCK : BLOCK + 1, :] + recv_ref[BLOCK : BLOCK + 1, :]
    same = iota((BLOCK, BLOCK), 0) == iota((BLOCK, BLOCK), 1)
    got = jnp.sum(jnp.where(same, recv_ref[BLOCK + 1 : BLOCK + 2, 0:BLOCK], 0.0), axis=1, keepdims=True)
    row_scale = lax.rsqrt(row_sq / F + EPS)
    centre_scale = lax.rsqrt((squares_ref[:, 0:1] + got) / F + EPS)
    dots = dots_ref[...] + recv_ref[0:BLOCK, :]
    cosine = jnp.clip(dots * row_scale * centre_scale, -1.0, 1.0)
    panel = jnp.exp(GAMMA * (cosine - 1.0))
    panel_ref[...] = panel
    placed = iota((BLOCK, ROWS), 1) == loc_ref[...]
    normal_ref[...] = panel / EXAMPLES + jnp.where(placed, LAMBDA, 0.0)
    hit = iota((CLASSES, ROWS), 0) == labels_ref[...]
    targets = jnp.where(hit, CLASSES - 1.0, -1.0)
    rhs = dot_t(targets, panel) / EXAMPLES
    for i in range(N_EX):
        out_ref[i] = rhs


def total(ref):
    acc = ref[0]
    for i in range(1, ref.shape[0]):
        acc = acc + ref[i]
    return acc


def put_chunks(out_ref, vec, stride, slot):
    for s in range(N_FEAT):
        g, l = s // 8, s % 8
        out_ref[s * stride + slot] = vec[4 * g : 4 * g + 4, 128 * l : 128 * l + 128]


def take_chunks(in_ref, stride, out_ref):
    for s in range(N_FEAT):
        g, l = s // 8, s % 8
        out_ref[4 * g : 4 * g + 4, 128 * l : 128 * l + 128] = in_ref[s * stride]


def sum_slot(ref, stride, slot):
    acc = ref[slot]
    for s in range(1, N_FEAT):
        acc = acc + ref[s * stride + slot]
    return acc


def first_kernel(recv_ref, pre_ref, panel_ref, normal_ref, rhs_ref, u_ref, out_ref):
    rhs = total(recv_ref)
    u = dot_t(rhs, pre_ref[...])
    rhs_ref[...] = rhs
    u_ref[...] = u
    put_chunks(out_ref, jnp.dot(u, panel_ref[...], precision=HIGH, preferred_element_type=F32), 2, 0)
    put_chunks(out_ref, jnp.dot(u, normal_ref[...], precision=HIGH, preferred_element_type=F32), 2, 1)


def chunk_kernel(recv_ref, chunk_ref, out_ref):
    k = sum_slot(recv_ref, 2, 0)
    chunk_ref[0] = k
    chunk_ref[1] = sum_slot(recv_ref, 2, 1)
    for s in range(N_FEAT):
        out_ref[s] = k


def normal_kernel(recv_ref, normal_ref, k_ref, out_ref):
    take_chunks(recv_ref, 1, k_ref)
    image = dot_t(k_ref[...], normal_ref[...])
    for i in range(N_EX):
        out_ref[i] = image


def second_kernel(recv_ref, pre_ref, panel_ref, normal_ref, rhs_ref, u_ref, image_ref, v_ref, out_ref):
    image = total(recv_ref)
    v = dot_t(image, pre_ref[...])
    image_ref[...] = image
    v_ref[...] = v
    put_chunks(out_ref, jnp.dot(v, panel_ref[...], precision=HIGH, preferred_element_type=F32), 3, 0)
    put_chunks(out_ref, jnp.dot(v, normal_ref[...], precision=HIGH, preferred_element_type=F32), 3, 1)
    u = u_ref[...]
    row = to_row(jnp.sum(rhs_ref[...] * u, axis=1, keepdims=True), 0)
    row = row + to_row(jnp.sum(u * image, axis=1, keepdims=True), CLASSES)
    row = row + to_row(jnp.sum(v * image, axis=1, keepdims=True), 2 * CLASSES)
    row = jnp.broadcast_to(row, (4, 128))
    for s in range(N_FEAT):
        out_ref[s * 3 + 2] = row


def step_kernel(group_ref, recv_ref, chunk_ref, rhs_ref, u_ref, image_ref, v_ref, scal_ref, out_ref):
    row = sum_slot(recv_ref, 3, 2)[0:1]
    scal_ref[...] = jnp.broadcast_to(row, (8, 128))
    alpha = to_col(row, CLASSES, 0) / to_col(row, CLASSES, CLASSES)
    residual = rhs_ref[...] - alpha * image_ref[...]
    z = u_ref[...] - alpha * v_ref[...]
    rz = to_row(jnp.sum(residual * z, axis=1, keepdims=True))
    alpha_row = to_row(alpha)
    first = group_ref[0] * 4
    mine = iota((4, 128), 1) == iota((4, 128), 0) + first
    alpha_mine = jnp.sum(jnp.where(mine, alpha_row, 0.0), axis=1, keepdims=True)
    kz = chunk_ref[0] - alpha_mine * sum_slot(recv_ref, 3, 0)
    gz = chunk_ref[1] - alpha_mine * sum_slot(recv_ref, 3, 1)
    quad = jnp.sum(kz * gz, axis=1, keepdims=True)
    quad_row = jnp.sum(jnp.where(mine, quad, 0.0), axis=0, keepdims=True)
    which = iota((4, 128), 0)
    tail = jnp.where(which == 0, rz, jnp.where(which == 1, quad_row, 0.0))
    for s in range(N_FEAT):
        out_ref[s * 2] = kz
        out_ref[s * 2 + 1] = tail


def gather_kernel(recv_ref, kz_ref, tail_ref, out_ref):
    take_chunks(recv_ref, 2, kz_ref)
    tail = sum_slot(recv_ref, 2, 1)
    tail_ref[...] = tail
    for i in range(N_EX):
        out_ref[i] = tail[1:2]


def last_kernel(recv_ref, tail_ref, scal_ref, k_ref, kz_ref, out_ref):
    quad = to_col(total(recv_ref), CLASSES)
    rz_next = to_col(tail_ref[0:1, :], CLASSES)
    row = scal_ref[0:1, :]
    rz = to_col(row, CLASSES, 0)
    uu = to_col(row, CLASSES, CLASSES)
    vu = to_col(row, CLASSES, 2 * CLASSES)
    alpha = rz / uu
    beta = rz_next / rz
    cross = uu - alpha * vu
    alpha_next = rz_next / (quad + 2.0 * beta * cross + beta * beta * uu)
    k = k_ref[...]
    out_ref[...] = alpha * k + alpha_next * (kz_ref[...] + beta * k)


def per_device(features, centre_index, labels, precond):
    ex_index = lax.axis_index(EX)
    feat_index = lax.axis_index(FEAT)
    core = lax.axis_index("c")
    local = centre_index[:, 0, :] - ex_index * ROWS
    ft_local = features.T
    ft = lax.all_gather(ft_local, PLANE, axis=0, tiled=True)

    pair = local.reshape(N_PLANE, 2, OWN)
    own_col = jnp.where(core == 0, pair[:, 0], pair[:, 1]).reshape(N_PLANE * OWN, 1)
    other_col = jnp.where(core == 0, pair[:, 1], pair[:, 0]).reshape(N_PLANE * OWN, 1)
    picked = call(pick_kernel, ((N_PLANE, OWN, 2 * SLICE), BF16), ft_local, own_col, other_col, name="pick")
    picked = lax.all_to_all(picked, PLANE, 0, 0, tiled=True)
    spread = call(spread_kernel, ((N_EX, 2 * OWN, WIDTH), BF16), picked, name="spread")
    cen = lax.all_to_all(spread, EX, 0, 0, tiled=True)

    own_rows = lax.dynamic_index_in_dim(local, feat_index, 0, keepdims=False)
    slot = lax.iota(jnp.int32, N_EX)[:, None] == ex_index
    loc = jnp.where(slot, own_rows[None, :], -1).reshape(BLOCK, 1)

    sent = call(other_kernel, ((BLOCK + 8, ROWS), F32), ft, cen, name="other")
    got = lax.ppermute(sent, "c", [(0, 1), (1, 0)])
    dots, squares = call(own_kernel, [((BLOCK, ROWS), F32), ((BLOCK, 128), F32)], ft, cen, name="own")
    panel, normal, part = call(
        panel_kernel,
        [((BLOCK, ROWS), F32), ((BLOCK, ROWS), F32), ((N_EX, CLASSES, BLOCK), F32)],
        dots, squares, sent, got, labels.reshape(1, ROWS), loc, name="panel",
    )
    vec = ((CLASSES, BLOCK), F32)
    part = lax.all_to_all(part, EX, 0, 0, tiled=True)
    rhs, u, part = call(first_kernel, [vec, vec, ((N_FEAT * 2, 4, 128), F32)], part, precond, panel, normal, name="first")
    part = lax.all_to_all(part, FEAT, 0, 0, tiled=True)
    chunk, part = call(chunk_kernel, [((2, 4, 128), F32), ((N_FEAT, 4, 128), F32)], part, name="chunk")
    part = lax.all_to_all(part, FEAT, 0, 0, tiled=True)
    k, part = call(normal_kernel, [((CLASSES, ROWS), F32), ((N_EX, CLASSES, BLOCK), F32)], part, normal, name="normal")
    part = lax.all_to_all(part, EX, 0, 0, tiled=True)
    image, v, part = call(
        second_kernel, [vec, vec, ((N_FEAT * 3, 4, 128), F32)],
        part, precond, panel, normal, rhs, u, name="second",
    )
    part = lax.all_to_all(part, FEAT, 0, 0, tiled=True)
    group = (feat_index // 8).reshape(1)
    scal, part = call(
        step_kernel, [((8, 128), F32), ((N_FEAT * 2, 4, 128), F32)],
        group, part, chunk, rhs, u, image, v, name="step", smem=1,
    )
    part = lax.all_to_all(part, FEAT, 0, 0, tiled=True)
    kz, tail, part = call(
        gather_kernel, [((CLASSES, ROWS), F32), ((4, 128), F32), ((N_EX, 1, 128), F32)], part, name="gather"
    )
    part = lax.all_to_all(part, EX, 0, 0, tiled=True)
    out = call(last_kernel, ((CLASSES, ROWS), F32), part, tail, scal, k, kz, name="last")
    return out.T


def solution(mesh):
    fine = Mesh(mesh.devices.reshape(8, 2, 2, 8, 2), ("z", "xh", "xl", "y", "c"))
    in_specs = (P(EX, FEAT), P(None, EX, None), P(EX), P(FEAT, None))
    return jax.shard_map(per_device, mesh=fine, in_specs=in_specs, out_specs=P(EX, None), check_vma=False)
```

time: 983 us -> 244 us (0.25)
  waiting for transfers between devices: 559 us -> 21.2 us
  blocking collectives: 376 us -> 151 us
  Pallas kernels: 0 us -> 33.3 us
  starting transfers between devices: 0.12 us -> 18.8 us
  matrix products: 11.9 us -> 0 us
    psum x2 -> x0, waiting for transfers between devices: 405 us -> none  [per_device(): kvec = lax.psum(part_prod, 'feat')]
    psum x6 -> x0, blocking collectives: 376 us -> none  [the longest x2 127 us: per_device(): image = lax.psum(term, 'ex')]
    all_to_all x0 -> x8, blocking collectives: none -> 151 us  [the longest x3 50.7 us: per_device(): part = lax.all_to_all(part, EX, 0, 0, tiled=True)]
    all_gather x2 -> x1, waiting for transfers between devices: 154 us -> 10.2 us  [per_device(): ft = lax.all_gather(ft_local, PLANE, axis=0, tiled=True)]
    pallas_call x0 -> x12, Pallas kernels: none -> 33.3 us  [call(): pl.pallas_call(kernel, out_shape=[jax.ShapeDtypeStruct(s, d) for s, d in...]
    ppermute x0 -> x1, starting transfers between devices: none -> 12 us  [per_device(): got = lax.ppermute(sent, 'c', [(0, 1), (1, 0)])]
    dot_general x8 -> x0, matrix products: 11.9 us -> none  [the longest x1 3.9 us: per_device(): dots = jnp.dot(gathered, centres.T, preferred_element_type=jnp.float32)]
    all_to_all x0 -> x1, waiting for transfers between devices: none -> 10.2 us  [per_device(): part = lax.all_to_all(part, FEAT, 0, 0, tiled=True)]
  transfers between devices with their start and end apart: 4 -> 3, of which waited for: 4 -> 2; matrix products, arithmetic and copies ran while one was open for 0% -> 1% of each run, Pallas kernels for 0% -> 3%
where the time goes in v1:
time: 244 us; the launch traced here: 243 us
  blocking collectives  151 us (62%)
  Pallas kernels  33.3 us (14%)
  waiting for transfers between devices  21.2 us (9%)
  starting transfers between devices  18.8 us (8%)
  between operations  13.5 us (6%)
  local copies, waits for them, and re-layouts  4.73 us (2%)
    all_to_all x3, blocking collectives, per_device(): part = lax.all_to_all(part, EX, 0, 0, tiled=True)  50.7 us
    all_to_all x3, blocking collectives, per_device(): part = lax.all_to_all(part, FEAT, 0, 0, tiled=True)  44.2 us
    all_to_all x1, blocking collectives, per_device(): cen = lax.all_to_all(spread, EX, 0, 0, tiled=True)  39.8 us
    pallas_call x12, Pallas kernels, call(): pl.pallas_call(kernel, out_shape=[jax.ShapeDtypeStruct(s, d) for s, d in...  33.3 us
    all_to_all x1, blocking collectives, per_device(): picked = lax.all_to_all(picked, PLANE, 0, 0, tiled=True)  16.2 us
    ppermute x1, starting transfers between devices, per_device(): got = lax.ppermute(sent, 'c', [(0, 1), (1, 0)])  12 us
    all_gather x1, waiting for transfers between devices, per_device(): ft = lax.all_gather(ft_local, PLANE, axis=0, tiled=True)  10.2 us
    all_to_all x1, waiting for transfers between devices, per_device(): part = lax.all_to_all(part, FEAT, 0, 0, tiled=True)  10.2 us
  transfers between devices with their start and end apart: 3, of which 2 were waited for; matrix products, arithmetic and copies ran while one was open for 1% of the time, Pallas kernels for 3%

profile of v1, /device:TPU:1, one launch (start us, length us, event | category | flops | bytes accessed | tf_op | source)
XLA Modules:
  0.0 242.5 jit_solution(15191510385314751137)
XLA Ops:
  9.6 2.1 pick.1
  11.7 16.2 %all_to_all.45.in_ref = bf16[16,16,128]{2,1,0:T(8,128)(2,1)} all-to-all(bf16[16,16,128]{2,1,0:T(8,128)(2,1)} %pick.1), channel_id=1, replica_groups=mesh['z'=8,'xh'=2,'xl'=2,'y'=8,'c'=2] {'xl','y'}, dimensions={0} | all-to-all | bytes 131072 | tf_op jit(solution)/shard_map/all_to_all | solution.py:261
  28.0 2.1 spread.1
  30.1 39.8 %all_to_all.46.cen_ref = bf16[16,32,1024]{2,1,0:T(8,128)(2,1)} all-to-all(bf16[16,32,1024]{2,1,0:T(8,128)(2,1)} %spread.1), channel_id=1, replica_groups=mesh['z'=8,'xh'=2,'xl'=2,'y'=8,'c'=2] {'z','xh'}, dimensions={0} | all-to-all | bytes 2097152 | tf_op jit(solution)/shard_map/all_to_all | solution.py:263
  69.9 10.2 %all-gather.2.cloned.1.call-done.ft_ref = bf16[1024,1024]{1,0:T(8,128)(2,1)} async-done(((bf16[64,1024]{1,0:T(8,128)(2,1)}), bf16[1024,1024]{1,0:T(8,128)(2,1)}) %all-gather.2.cloned.1.call-update) | async-done | bytes 2097168 | tf_op jit(solution)/shard_map/all_gather | solution.py:255
  80.2 3.5 %other.1.sent_ref = f32[264,1024]{1,0:T(8,128)} custom-call(bf16[1024,1024]{1,0:T(8,128)(2,1)} %all-gather.2.cloned.1.call-done.ft_ref, bf16[16,32,1024]{2,1,0:T(8,128)(2,1)} %all_to_all.46.cen_ref), custom_call_target="tpu_custom_call" | custom-call | tf_op jit(solution)/shard_map/other/pallas_call | solution.py:60
  83.7 12.0 %collective-permute-start = (f32[264,1024]{1,0:T(8,128)}, f32[264,1024]{1,0:T(8,128)S(1)}, u32[]{:S(2)}, u32[]{:S(2)}) collective-permute-start(f32[264,1024]{1,0:T(8,128)} %other.1.sent_ref), channel_id=1, source_target_pairs={{0,1},{1,0},{2,3},{3,2},{4,5},{5,4},{6,7},{7,6},{8,9},{9,8},{10,11... | collective-permute-start | bytes 3244040 | tf_op jit(solution)/shard_map/ppermute | solution.py:270
  96.6 3.6 %own.1 = (f32[256,1024]{1,0:T(8,128)}, f32[256,128]{1,0:T(8,128)}) custom-call(bf16[1024,1024]{1,0:T(8,128)(2,1)} %all-gather.2.cloned.1.call-done.ft_ref, bf16[16,32,1024]{2,1,0:T(8,128)(2,1)} %all_to_all.46.cen_ref), custom_call_target="tpu_custom_call" | custom-call | tf_op jit(solution)/shard_map/own/pallas_call | solution.py:60
  101.2 4.2 %panel.1 = (f32[256,1024]{1,0:T(8,128)}, f32[256,1024]{1,0:T(8,128)}, f32[16,16,256]{2,1,0:T(8,128)}) custom-call(f32[256,1024]{1,0:T(8,128)} %get-tuple-element.25.dots_ref, f32[256,128]{1,0:T(8,128)} %get-tuple-element.26.squares_ref, f32[264,1024]{1,0:T(8,128)} %other.1.sent_ref, f32[264,1024]{1,0:T(8,128)} %copy-done, s32[1,1024]{1,0:T(1,128)} %bitcast.10, ...), custom_call_target="tpu_custom_call" | custom-call | tf_op jit(solution)/shard_map/panel/pallas_call | solution.py:60
  105.4 22.2 %all_to_all.47.recv_ref = f32[16,16,256]{2,1,0:T(8,128)} all-to-all(f32[16,16,256]{2,1,0:T(8,128)} %get-tuple-element.27), channel_id=1, replica_groups=mesh['z'=8,'xh'=2,'xl'=2,'y'=8,'c'=2] {'z','xh'}, dimensions={0} | all-to-all | bytes 524288 | tf_op jit(solution)/shard_map/all_to_all | solution.py:278
  127.6 4.0 %first.1 = (f32[16,256]{1,0:T(8,128)}, f32[16,256]{1,0:T(8,128)}, f32[64,4,128]{2,1,0:T(4,128)}) custom-call(f32[16,16,256]{2,1,0:T(8,128)} %all_to_all.47.recv_ref, f32[256,256]{1,0:T(8,128)} %pre_ref.3, f32[256,1024]{1,0:T(8,128)} %get-tuple-element.28.panel_ref, f32[256,1024]{1,0:T(8,128)} %get-tuple-element.29.normal_ref), custom_call_target="tpu_custom_call" | custom-call | tf_op jit(solution)/shard_map/first/pallas_call | solution.py:60
  131.6 15.0 %all_to_all.48.recv_ref = f32[64,4,128]{2,1,0:T(4,128)} all-to-all(f32[64,4,128]{2,1,0:T(4,128)} %get-tuple-element.30), channel_id=1, replica_groups=mesh['z'=8,'xh'=2,'xl'=2,'y'=8,'c'=2] {'xl','y','c'}, dimensions={0} | all-to-all | bytes 262144 | tf_op jit(solution)/shard_map/all_to_all | solution.py:280
  146.6 1.6 chunk.1
  148.2 14.0 %all_to_all.49.recv_ref = f32[32,4,128]{2,1,0:T(4,128)} all-to-all(f32[32,4,128]{2,1,0:T(4,128)} %get-tuple-element.31), channel_id=1, replica_groups=mesh['z'=8,'xh'=2,'xl'=2,'y'=8,'c'=2] {'xl','y','c'}, dimensions={0} | all-to-all | bytes 131072 | tf_op jit(solution)/shard_map/all_to_all | solution.py:282
  162.2 2.9 %normal.1 = (f32[16,1024]{1,0:T(8,128)}, f32[16,16,256]{2,1,0:T(8,128)}) custom-call(f32[32,4,128]{2,1,0:T(4,128)} %all_to_all.49.recv_ref, f32[256,1024]{1,0:T(8,128)} %get-tuple-element.29.normal_ref), custom_call_target="tpu_custom_call" | custom-call | tf_op jit(solution)/shard_map/normal/pallas_call | solution.py:60
  165.1 15.8 %all_to_all.50.recv_ref = f32[16,16,256]{2,1,0:T(8,128)} all-to-all(f32[16,16,256]{2,1,0:T(8,128)} %get-tuple-element.32), channel_id=1, replica_groups=mesh['z'=8,'xh'=2,'xl'=2,'y'=8,'c'=2] {'z','xh'}, dimensions={0} | all-to-all | bytes 524288 | tf_op jit(solution)/shard_map/all_to_all | solution.py:284
  181.0 4.1 %second.1 = (f32[16,256]{1,0:T(8,128)}, f32[16,256]{1,0:T(8,128)}, f32[96,4,128]{2,1,0:T(4,128)}) custom-call(f32[16,16,256]{2,1,0:T(8,128)} %all_to_all.50.recv_ref, f32[256,256]{1,0:T(8,128)} %pre_ref.3, f32[256,1024]{1,0:T(8,128)} %get-tuple-element.28.panel_ref, f32[256,1024]{1,0:T(8,128)} %get-tuple-element.29.normal_ref, ...), custom_call_target="tpu_custom_call" | custom-call | tf_op jit(solution)/shard_map/second/pallas_call | solution.py:60
  185.0 6.8 %all-to-all-start.6 = ((f32[96,4,128]{2,1,0:T(4,128)}), f32[96,4,128]{2,1,0:T(4,128)S(1)}, u32[]{:S(2)}, u32[]{:S(2)}) async-start(f32[96,4,128]{2,1,0:T(4,128)} %get-tuple-element.35), calls=%async_computation.6 | async-start | bytes 393216 | tf_op jit(solution)/shard_map/all_to_all | solution.py:289
  191.8 10.2 %all-to-all-done.6.recv_ref = f32[96,4,128]{2,1,0:T(4,128)S(1)} async-done(((f32[96,4,128]{2,1,0:T(4,128)}), f32[96,4,128]{2,1,0:T(4,128)S(1)}, u32[]{:S(2)}, u32[]{:S(2)}) %all-to-all-start.6) | async-done | bytes 196640 | tf_op jit(solution)/shard_map/all_to_all | solution.py:289
  202.7 1.9 step.1
  204.6 15.2 %all_to_all.51.recv_ref = f32[64,4,128]{2,1,0:T(4,128)} all-to-all(f32[64,4,128]{2,1,0:T(4,128)} %get-tuple-element.39), channel_id=1, replica_groups=mesh['z'=8,'xh'=2,'xl'=2,'y'=8,'c'=2] {'xl','y','c'}, dimensions={0} | all-to-all | bytes 262144 | tf_op jit(solution)/shard_map/all_to_all | solution.py:295
  219.8 1.6 gather.1
  221.4 12.7 %all_to_all.52.recv_ref = f32[16,1,128]{2,1,0:T(1,128)} all-to-all(f32[16,1,128]{2,1,0:T(1,128)} %get-tuple-element.40), channel_id=1, replica_groups=mesh['z'=8,'xh'=2,'xl'=2,'y'=8,'c'=2] {'z','xh'}, dimensions={0} | all-to-all | bytes 16384 | tf_op jit(solution)/shard_map/all_to_all | solution.py:299
  234.1 1.6 last.1
  (16 shorter events, 5.6 us)
Async XLA Ops:
  6.5 73.6 %all-gather.2.cloned.1.call-start = ((), (), s32[]{:S(2)}) async-start(), calls=%async_computation.9 | async-start | bytes 2228224 | tf_op jit(solution)/shard_map/all_gather | solution.py:255
  83.7 16.5 %collective-permute-start = (f32[264,1024]{1,0:T(8,128)}, f32[264,1024]{1,0:T(8,128)S(1)}, u32[]{:S(2)}, u32[]{:S(2)}) collective-permute-start(f32[264,1024]{1,0:T(8,128)} %other.1.sent_ref), channel_id=1, source_target_pairs={{0,1},{1,0},{2,3},{3,2},{4,5},{5,4},{6,7},{7,6},{8,9},{9,8},{10,11... | collective-permute-start | bytes 3244040 | tf_op jit(solution)/shard_map/ppermute | solution.py:270
  100.2 1.0 copy-start
  185.0 17.0 %all-to-all-start.6 = ((f32[96,4,128]{2,1,0:T(4,128)}), f32[96,4,128]{2,1,0:T(4,128)S(1)}, u32[]{:S(2)}, u32[]{:S(2)}) async-start(f32[96,4,128]{2,1,0:T(4,128)} %get-tuple-element.35), calls=%async_computation.6 | async-start | bytes 393216 | tf_op jit(solution)/shard_map/all_to_all | solution.py:289
  202.1 0.7 copy-start.1
Sparse Core Ops, SparseCore 0:
  9.4 70.7 all-gather.1

commit v2 on v1

--- a/solution.py
+++ b/solution.py
@@ -52,18 +52,19 @@
     return jnp.sum(jnp.where(place, row, 0.0), axis=1, keepdims=True)
 
 
-def call(kernel, outs, *args, name, smem=0):
+def call(kernel, outs, *args, name, smem=0, space=pltpu.VMEM):
     spec = [pl.BlockSpec(memory_space=pltpu.SMEM)] * smem
     spec += [pl.BlockSpec(memory_space=pltpu.VMEM)] * (len(args) - smem)
     many = isinstance(outs, list)
     out_spec = pl.BlockSpec(memory_space=pltpu.VMEM)
     return pl.pallas_call(
         kernel,
-        out_shape=[jax.ShapeDtypeStruct(s, d) for s, d in outs] if many else jax.ShapeDtypeStruct(*outs),
+        out_shape=[pltpu.VMEM(s, d) for s, d in outs] if many else space(*outs),
         in_specs=spec,
         out_specs=[out_spec] * len(outs) if many else out_spec,
         name=name,
-    )(*args)
+        compiler_params=pltpu.CompilerParams(vmem_limit_bytes=12 << 20),
+    )(*[x if i < smem else pltpu.with_memory_space_constraint(x, pltpu.VMEM) for i, x in enumerate(args)])
 
 
 def pick_kernel(ft_ref, own_ref, other_ref, out_ref):
@@ -81,11 +82,13 @@
     out_ref[...] = both.astype(BF16).reshape(N_PLANE, OWN, 2 * SLICE)
 
 
-def spread_kernel(in_ref, out_ref):
+def spread_kernel(side_ref, in_ref, out_ref):
     low = iota((OWN, 128), 1) < SLICE
-    for t in range(N_PLANE // 2):
-        a = in_ref[2 * t].astype(F32)
-        b = in_ref[2 * t + 1].astype(F32)
+    half = N_PLANE // 2
+    for t in range(half):
+        source = 2 * (t % (half // 2)) + half * (side_ref[0] if t < half // 2 else 1 - side_ref[0])
+        a = in_ref[source].astype(F32)
+        b = in_ref[source + 1].astype(F32)
         own = jnp.where(low, a, pltpu.roll(b, SLICE, 1)).astype(BF16)
         other = jnp.where(low, pltpu.roll(a, SLICE, 1), b).astype(BF16)
         cols = slice(128 * t, 128 * t + 128)
@@ -94,29 +97,60 @@
             out_ref[i, OWN : 2 * OWN, cols] = other
 
 
-def half_dots(ft_ref, cen_ref, first):
-    block = cen_ref[:, first : first + OWN, :].reshape(BLOCK, WIDTH)
-    dots = jnp.dot(block, ft_ref[...], preferred_element_type=F32)
-    squares = jnp.sum(jnp.square(block.astype(F32)), axis=1, keepdims=True)
-    return dots, squares
-
-
-def other_kernel(ft_ref, cen_ref, out_ref):
-    dots, squares = half_dots(ft_ref, cen_ref, OWN)
-    out_ref[0:BLOCK, :] = dots
-    out_ref[BLOCK : BLOCK + 8, :] = jnp.zeros((8, ROWS), F32)
-    out_ref[BLOCK : BLOCK + 1, :] = jnp.sum(jnp.square(ft_ref[...].astype(F32)), axis=0, keepdims=True)
+def pick_centres(cen_ref, first, half):
+    return cen_ref[:, first : first + OWN, half * WIDTH // 2 : (half + 1) * WIDTH // 2].reshape(BLOCK, WIDTH // 2)
+
+
+def row_squares(ft_ref):
+    return jnp.sum(jnp.square(ft_ref[...].astype(F32)), axis=0, keepdims=True)
+
+
+def near_kernel(ft_ref, cen_ref, other_ref, own_ref, own_sq_ref):
+    ft = ft_ref[...]
+    other_ref[0:BLOCK, :] = jnp.dot(pick_centres(cen_ref, OWN, 0), ft, preferred_element_type=F32)
+    own_ref[...] = jnp.dot(pick_centres(cen_ref, 0, 0), ft, preferred_element_type=F32)
+
+    def squares(first):
+        block = cen_ref[:, first : first + OWN, :].reshape(BLOCK, WIDTH).astype(F32)
+        return jnp.sum(jnp.square(block), axis=1, keepdims=True)
+
+    other_ref[BLOCK : BLOCK + 8, :] = jnp.zeros((8, ROWS), F32)
+    other_ref[BLOCK : BLOCK + 1, :] = row_squares(ft_ref)
     same = iota((BLOCK, BLOCK), 0) == iota((BLOCK, BLOCK), 1)
-    out_ref[BLOCK + 1 : BLOCK + 2, 0:BLOCK] = jnp.sum(jnp.where(same, squares, 0.0), axis=0, keepdims=True)
-
-
-def own_kernel(ft_ref, cen_ref, dots_ref, squares_ref):
-    dots, squares = half_dots(ft_ref, cen_ref, 0)
-    dots_ref[...] = dots
-    squares_ref[...] = jnp.broadcast_to(squares, (BLOCK, 128))
-
-
-def panel_kernel(dots_ref, squares_ref, sent_ref, recv_ref, labels_ref, loc_ref, panel_ref, normal_ref, out_ref):
+    other_ref[BLOCK + 1 : BLOCK + 2, 0:BLOCK] = jnp.sum(jnp.where(same, squares(OWN), 0.0), axis=0, keepdims=True)
+    own_sq_ref[...] = jnp.broadcast_to(squares(0), (BLOCK, 128))
+
+
+def other_kernel(ft_ref, cen_ref, near_ref, out_ref):
+    block = pick_centres(cen_ref, OWN, 1)
+    out_ref[0:BLOCK, :] = near_ref[0:BLOCK, :] + jnp.dot(block, ft_ref[...], preferred_element_type=F32)
+    out_ref[BLOCK : BLOCK + 8, :] = near_ref[BLOCK : BLOCK + 8, :]
+    out_ref[BLOCK : BLOCK + 1, :] = near_ref[BLOCK : BLOCK + 1, :] + row_squares(ft_ref)
+
+
+def own_kernel(ft_ref, cen_ref, near_ref, out_ref):
+    block = pick_centres(cen_ref, 0, 1)
+    out_ref[...] = near_ref[...] + jnp.dot(block, ft_ref[...], preferred_element_type=F32)
+
+
+def split2(x):
+    high = x.astype(BF16)
+    return high, (x - high.astype(F32)).astype(BF16)
+
+
+def split3(x):
+    high = x.astype(BF16).astype(F32)
+    rest = x - high
+    mid = rest.astype(BF16).astype(F32)
+    return jnp.concatenate([high, mid, rest - mid], axis=0).astype(BF16)
+
+
+def fold3(y):
+    n = y.shape[0] // 3
+    return y[0:n] + (y[n : 2 * n] + y[2 * n : 3 * n])
+
+
+def panel_kernel(dots_ref, squares_ref, sent_ref, recv_ref, labels_ref, loc_ref, high_ref, low_ref, place_ref, out_ref):
     row_sq = sent_ref[BLOCK : BLOCK + 1, :] + recv_ref[BLOCK : BLOCK + 1, :]
     same = iota((BLOCK, BLOCK), 0) == iota((BLOCK, BLOCK), 1)
     got = jnp.sum(jnp.where(same, recv_ref[BLOCK + 1 : BLOCK + 2, 0:BLOCK], 0.0), axis=1, keepdims=True)
@@ -124,15 +158,34 @@
     centre_scale = lax.rsqrt((squares_ref[:, 0:1] + got) / F + EPS)
     dots = dots_ref[...] + recv_ref[0:BLOCK, :]
     cosine = jnp.clip(dots * row_scale * centre_scale, -1.0, 1.0)
-    panel = jnp.exp(GAMMA * (cosine - 1.0))
-    panel_ref[...] = panel
-    placed = iota((BLOCK, ROWS), 1) == loc_ref[...]
-    normal_ref[...] = panel / EXAMPLES + jnp.where(placed, LAMBDA, 0.0)
+    high, low = split2(jnp.exp(GAMMA * (cosine - 1.0)))
+    high_ref[...] = high
+    low_ref[...] = low
+    place_ref[...] = (iota((BLOCK, ROWS), 1) == loc_ref[...]).astype(F32).astype(BF16)
     hit = iota((CLASSES, ROWS), 0) == labels_ref[...]
-    targets = jnp.where(hit, CLASSES - 1.0, -1.0)
-    rhs = dot_t(targets, panel) / EXAMPLES
+    targets = jnp.where(hit, CLASSES - 1.0, -1.0).astype(BF16)
+    rhs = (dot_t(targets, high, None) + dot_t(targets, low, None)) / EXAMPLES
     for i in range(N_EX):
         out_ref[i] = rhs
+
+
+def apply_panel(vec, high_ref, low_ref, place_ref):
+    parts = split3(vec)
+
+    def times(matrix):
+        return fold3(jnp.dot(parts, matrix, preferred_element_type=F32))
+
+    k = times(high_ref[...]) + times(low_ref[...])
+    return k, k / EXAMPLES + LAMBDA * times(place_ref[...])
+
+
+def apply_normal(k, high_ref, low_ref, place_ref):
+    parts = split3(k)
+
+    def times(matrix):
+        return fold3(dot_t(parts, matrix, None))
+
+    return (times(high_ref[...]) + times(low_ref[...])) / EXAMPLES + LAMBDA * times(place_ref[...])
 
 
 def total(ref):
@@ -161,13 +214,14 @@
     return acc
 
 
-def first_kernel(recv_ref, pre_ref, panel_ref, normal_ref, rhs_ref, u_ref, out_ref):
+def first_kernel(recv_ref, pre_ref, high_ref, low_ref, place_ref, rhs_ref, u_ref, out_ref):
     rhs = total(recv_ref)
     u = dot_t(rhs, pre_ref[...])
     rhs_ref[...] = rhs
     u_ref[...] = u
-    put_chunks(out_ref, jnp.dot(u, panel_ref[...], precision=HIGH, preferred_element_type=F32), 2, 0)
-    put_chunks(out_ref, jnp.dot(u, normal_ref[...], precision=HIGH, preferred_element_type=F32), 2, 1)
+    k, g = apply_panel(u, high_ref, low_ref, place_ref)
+    put_chunks(out_ref, k, 2, 0)
+    put_chunks(out_ref, g, 2, 1)
 
 
 def chunk_kernel(recv_ref, chunk_ref, out_ref):
@@ -178,20 +232,21 @@
         out_ref[s] = k
 
 
-def normal_kernel(recv_ref, normal_ref, k_ref, out_ref):
+def normal_kernel(recv_ref, high_ref, low_ref, place_ref, k_ref, out_ref):
     take_chunks(recv_ref, 1, k_ref)
-    image = dot_t(k_ref[...], normal_ref[...])
+    image = apply_normal(k_ref[...], high_ref, low_ref, place_ref)
     for i in range(N_EX):
         out_ref[i] = image
 
 
-def second_kernel(recv_ref, pre_ref, panel_ref, normal_ref, rhs_ref, u_ref, image_ref, v_ref, out_ref):
+def second_kernel(recv_ref, pre_ref, high_ref, low_ref, place_ref, rhs_ref, u_ref, image_ref, v_ref, out_ref):
     image = total(recv_ref)
     v = dot_t(image, pre_ref[...])
     image_ref[...] = image
     v_ref[...] = v
-    put_chunks(out_ref, jnp.dot(v, panel_ref[...], precision=HIGH, preferred_element_type=F32), 3, 0)
-    put_chunks(out_ref, jnp.dot(v, normal_ref[...], precision=HIGH, preferred_element_type=F32), 3, 1)
+    k, g = apply_panel(v, high_ref, low_ref, place_ref)
+    put_chunks(out_ref, k, 3, 0)
+    put_chunks(out_ref, g, 3, 1)
     u = u_ref[...]
     row = to_row(jnp.sum(rhs_ref[...] * u, axis=1, keepdims=True), 0)
     row = row + to_row(jnp.sum(u * image, axis=1, keepdims=True), CLASSES)
@@ -252,39 +307,45 @@
     core = lax.axis_index("c")
     local = centre_index[:, 0, :] - ex_index * ROWS
     ft_local = features.T
-    ft = lax.all_gather(ft_local, PLANE, axis=0, tiled=True)
+    near = lax.all_to_all(jnp.broadcast_to(ft_local[None], (8, SLICE, ROWS)), "y", 0, 0, tiled=True)
+    near = near.reshape(WIDTH // 2, ROWS)
+    far = lax.ppermute(near, "xl", [(0, 1), (1, 0)])
 
     pair = local.reshape(N_PLANE, 2, OWN)
     own_col = jnp.where(core == 0, pair[:, 0], pair[:, 1]).reshape(N_PLANE * OWN, 1)
     other_col = jnp.where(core == 0, pair[:, 1], pair[:, 0]).reshape(N_PLANE * OWN, 1)
     picked = call(pick_kernel, ((N_PLANE, OWN, 2 * SLICE), BF16), ft_local, own_col, other_col, name="pick")
     picked = lax.all_to_all(picked, PLANE, 0, 0, tiled=True)
-    spread = call(spread_kernel, ((N_EX, 2 * OWN, WIDTH), BF16), picked, name="spread")
+    spread = call(spread_kernel, ((N_EX, 2 * OWN, WIDTH), BF16), lax.axis_index("xl").reshape(1), picked, name="spread", smem=1)
     cen = lax.all_to_all(spread, EX, 0, 0, tiled=True)
 
     own_rows = lax.dynamic_index_in_dim(local, feat_index, 0, keepdims=False)
     slot = lax.iota(jnp.int32, N_EX)[:, None] == ex_index
     loc = jnp.where(slot, own_rows[None, :], -1).reshape(BLOCK, 1)
 
-    sent = call(other_kernel, ((BLOCK + 8, ROWS), F32), ft, cen, name="other")
+    dots_t = ((BLOCK, ROWS), F32)
+    other, own, own_sq = call(
+        near_kernel, [((BLOCK + 8, ROWS), F32), dots_t, ((BLOCK, 128), F32)], near, cen, name="near"
+    )
+    sent = call(other_kernel, ((BLOCK + 8, ROWS), F32), far, cen, other, name="other")
     got = lax.ppermute(sent, "c", [(0, 1), (1, 0)])
-    dots, squares = call(own_kernel, [((BLOCK, ROWS), F32), ((BLOCK, 128), F32)], ft, cen, name="own")
-    panel, normal, part = call(
-        panel_kernel,
-        [((BLOCK, ROWS), F32), ((BLOCK, ROWS), F32), ((N_EX, CLASSES, BLOCK), F32)],
-        dots, squares, sent, got, labels.reshape(1, ROWS), loc, name="panel",
+    own = call(own_kernel, dots_t, far, cen, own, name="own")
+    half_t = ((BLOCK, ROWS), BF16)
+    high, low, place, part = call(
+        panel_kernel, [half_t, half_t, half_t, ((N_EX, CLASSES, BLOCK), F32)],
+        own, own_sq, sent, got, labels.reshape(1, ROWS), loc, name="panel",
     )
     vec = ((CLASSES, BLOCK), F32)
     part = lax.all_to_all(part, EX, 0, 0, tiled=True)
-    rhs, u, part = call(first_kernel, [vec, vec, ((N_FEAT * 2, 4, 128), F32)], part, precond, panel, normal, name="first")
+    rhs, u, part = call(first_kernel, [vec, vec, ((N_FEAT * 2, 4, 128), F32)], part, precond, high, low, place, name="first")
     part = lax.all_to_all(part, FEAT, 0, 0, tiled=True)
     chunk, part = call(chunk_kernel, [((2, 4, 128), F32), ((N_FEAT, 4, 128), F32)], part, name="chunk")
     part = lax.all_to_all(part, FEAT, 0, 0, tiled=True)
-    k, part = call(normal_kernel, [((CLASSES, ROWS), F32), ((N_EX, CLASSES, BLOCK), F32)], part, normal, name="normal")
+    k, part = call(normal_kernel, [((CLASSES, ROWS), F32), ((N_EX, CLASSES, BLOCK), F32)], part, high, low, place, name="normal")
     part = lax.all_to_all(part, EX, 0, 0, tiled=True)
     image, v, part = call(
         second_kernel, [vec, vec, ((N_FEAT * 3, 4, 128), F32)],
-        part, precond, panel, normal, rhs, u, name="second",
+        part, precond, high, low, place, rhs, u, name="second",
     )
     part = lax.all_to_all(part, FEAT, 0, 0, tiled=True)
     group = (feat_index // 8).reshape(1)
@@ -297,7 +358,7 @@
         gather_kernel, [((CLASSES, ROWS), F32), ((4, 128), F32), ((N_EX, 1, 128), F32)], part, name="gather"
     )
     part = lax.all_to_all(part, EX, 0, 0, tiled=True)
-    out = call(last_kernel, ((CLASSES, ROWS), F32), part, tail, scal, k, kz, name="last")
+    out = call(last_kernel, ((CLASSES, ROWS), F32), part, tail, scal, k, kz, name="last", space=jax.ShapeDtypeStruct)
     return out.T
 
 

time: 244 us -> 218 us (0.89)
  waiting for transfers between devices: 21.2 us -> 71.5 us
  blocking collectives: 151 us -> 103 us
  Pallas kernels: 33.3 us -> 10.1 us
  between operations: 13.5 us -> 0.21 us
  starting transfers between devices: 18.8 us -> 28.1 us
    all_to_all x0 -> x2, waiting for transfers between devices: none -> 53 us  [the longest x1 27.8 us: per_device(): lax.all_to_all(jnp.broadcast_to(ft_local[None], (8, SLICE, ROWS)), 'y', 0...]
    all_to_all x1 -> x0, blocking collectives: 39.8 us -> none  [per_device(): cen = lax.all_to_all(spread, EX, 0, 0, tiled=True)]
    pallas_call x12 -> x13, Pallas kernels: 33.3 us -> 10.1 us  [call(): pl.pallas_call(kernel, out_shape=[pltpu.VMEM(s, d) for s, d in outs] if m...]
    all_to_all x0 -> x2, starting transfers between devices: none -> 15.9 us  [the longest x1 12.3 us: per_device(): cen = lax.all_to_all(spread, EX, 0, 0, tiled=True)]
    all_gather x1 -> x0, waiting for transfers between devices: 10.2 us -> none  [per_device(): ft = lax.all_gather(ft_local, PLANE, axis=0, tiled=True)]
    ppermute x1, starting transfers between devices: 12 us -> 3.54 us  [per_device(): got = lax.ppermute(sent, 'c', [(0, 1), (1, 0)])]
    ppermute x0 -> x1, waiting for transfers between devices: none -> 7.8 us  [per_device(): far = lax.ppermute(near, 'xl', [(0, 1), (1, 0)])]
    all_to_all x3, blocking collectives: 44.2 us -> 39.7 us  [per_device(): part = lax.all_to_all(part, FEAT, 0, 0, tiled=True)]
  transfers between devices with their start and end apart: 3 -> 5, of which waited for: 2 -> 5; matrix products, arithmetic and copies ran while one was open for 1% -> 0% of each run, Pallas kernels for 3% -> 1%
where the time goes in v2:
time: 218 us; the launch traced here: 217 us
  blocking collectives  103 us (47%)
  waiting for transfers between devices  71.5 us (33%)
  starting transfers between devices  28.1 us (13%)
  Pallas kernels  10.1 us (5%)
  local copies, waits for them, and re-layouts  4.36 us (2%)
    all_to_all x3, blocking collectives, per_device(): part = lax.all_to_all(part, EX, 0, 0, tiled=True)  47 us
    all_to_all x3, blocking collectives, per_device(): part = lax.all_to_all(part, FEAT, 0, 0, tiled=True)  39.7 us
    all_to_all x1, waiting for transfers between devices, per_device(): lax.all_to_all(jnp.broadcast_to(ft_local[None], (8, SLICE, ROWS)), 'y', 0...  27.8 us
    all_to_all x1, waiting for transfers between devices, per_device(): cen = lax.all_to_all(spread, EX, 0, 0, tiled=True)  25.2 us
    all_to_all x1, blocking collectives, per_device(): picked = lax.all_to_all(picked, PLANE, 0, 0, tiled=True)  15.8 us
    all_to_all x1, starting transfers between devices, per_device(): cen = lax.all_to_all(spread, EX, 0, 0, tiled=True)  12.3 us
    all_to_all x1, waiting for transfers between devices, per_device(): part = lax.all_to_all(part, FEAT, 0, 0, tiled=True)  10.2 us
    pallas_call x13, Pallas kernels, call(): pl.pallas_call(kernel, out_shape=[pltpu.VMEM(s, d) for s, d in outs] if m...  10.1 us
  transfers between devices with their start and end apart: 5, of which 5 were waited for; matrix products, arithmetic and copies ran while one was open for 0% of the time, Pallas kernels for 1%

profile of v2, /device:TPU:1, one launch (start us, length us, event | category | flops | bytes accessed | tf_op | source)
XLA Modules:
  0.0 217.0 jit_solution(5706517991551667451)
XLA Ops:
  0.0 0.8 copy.7
  1.1 0.9 copy-done.3
  2.5 15.8 %all_to_all.50.in_ref = bf16[16,16,128]{2,1,0:T(8,128)(2,1)S(1)} all-to-all(bf16[16,16,128]{2,1,0:T(8,128)(2,1)S(1)} %pick.1), channel_id=1, replica_groups=mesh['z'=8,'xh'=2,'xl'=2,'y'=8,'c'=2] {'xl','y'}, dimensions={0} | all-to-all | bytes 131072 | tf_op jit(solution)/shard_map/all_to_all | solution.py:318
  18.3 1.1 broadcast_in_dim.30
  19.4 3.6 %all-to-all-start = ((bf16[8,64,1024]{2,1,0:T(8,128)(2,1)}), bf16[8,64,1024]{2,1,0:T(8,128)(2,1)S(1)}, u32[]{:S(2)}, u32[]{:S(2)}) async-start(bf16[8,64,1024]{2,1,0:T(8,128)(2,1)} %broadcast_in_dim.30), calls=%async_computation | async-start | bytes 2097152 | tf_op jit(solution)/shard_map/all_to_all | solution.py:310
  23.0 1.3 spread.1
  24.3 27.8 %all-to-all-done = bf16[8,64,1024]{2,1,0:T(8,128)(2,1)S(1)} async-done(((bf16[8,64,1024]{2,1,0:T(8,128)(2,1)}), bf16[8,64,1024]{2,1,0:T(8,128)(2,1)S(1)}, u32[]{:S(2)}, u32[]{:S(2)}) %all-to-all-start) | async-done | bytes 1048608 | tf_op jit(solution)/shard_map/all_to_all | solution.py:310
  52.1 12.3 %all-to-all-start.2 = ((bf16[16,32,1024]{2,1,0:T(8,128)(2,1)}), bf16[16,32,1024]{2,1,0:T(8,128)(2,1)S(1)}, u32[]{:S(2)}, u32[]{:S(2)}) async-start(bf16[16,32,1024]{2,1,0:T(8,128)(2,1)} %spread.1), calls=%async_computation.2 | async-start | bytes 2097152 | tf_op jit(solution)/shard_map/all_to_all | solution.py:320
  64.4 1.9 collective-permute-start
  66.3 25.2 %all-to-all-done.2.cen_ref = bf16[16,32,1024]{2,1,0:T(8,128)(2,1)S(1)} async-done(((bf16[16,32,1024]{2,1,0:T(8,128)(2,1)}), bf16[16,32,1024]{2,1,0:T(8,128)(2,1)S(1)}, u32[]{:S(2)}, u32[]{:S(2)}) %all-to-all-start.2) | async-done | bytes 1048608 | tf_op jit(solution)/shard_map/all_to_all | solution.py:320
  92.3 7.8 %collective-permute-done.ft_ref = bf16[512,1024]{1,0:T(8,128)(2,1)S(1)} collective-permute-done((bf16[512,1024]{1,0:T(8,128)(2,1)S(1)}, bf16[512,1024]{1,0:T(8,128)(2,1)S(1)}, u32[]{:S(2)}, u32[]{:S(2)}) %collective-permute-start) | collective-permute-done | bytes 1048608 | tf_op jit(solution)/shard_map/ppermute | solution.py:312
  100.5 3.5 %collective-permute-start.1 = (f32[264,1024]{1,0:T(8,128)S(1)}, f32[264,1024]{1,0:T(8,128)}, u32[]{:S(2)}, u32[]{:S(2)}) collective-permute-start(f32[264,1024]{1,0:T(8,128)S(1)} %other.1.sent_ref), channel_id=1, source_target_pairs={{0,1},{1,0},{2,3},{3,2},{4,5},{5,4},{6,7},{7,6},{8,9},{9,8},{10,11... | collective-permute-start | bytes 3244040 | tf_op jit(solution)/shard_map/ppermute | solution.py:331
  104.3 1.2 copy-done.1
  106.5 2.2 %panel.1 = (bf16[256,1024]{1,0:T(8,128)(2,1)S(1)}, bf16[256,1024]{1,0:T(8,128)(2,1)S(1)}, bf16[256,1024]{1,0:T(8,128)(2,1)S(1)}, f32[16,16,256]{2,1,0:T(8,128)S(1)}) custom-call(f32[256,1024]{1,0:T(8,128)S(1)} %own.1.dots_ref, f32[256,128]{1,0:T(8,128)S(1)} %get-tuple-element.28.squares_ref, f32[264,1024]{1,0:T(8,128)S(1)} %other.1.sent_ref, ...), custom_call_target="tpu_custom_call" | custom-call | tf_op jit(solution)/shard_map/panel/pallas_call | solution.py:60
  108.8 21.3 %all_to_all.51.recv_ref = f32[16,16,256]{2,1,0:T(8,128)S(1)} all-to-all(f32[16,16,256]{2,1,0:T(8,128)S(1)} %get-tuple-element.30), channel_id=1, replica_groups=mesh['z'=8,'xh'=2,'xl'=2,'y'=8,'c'=2] {'z','xh'}, dimensions={0} | all-to-all | bytes 524288 | tf_op jit(solution)/shard_map/all_to_all | solution.py:339
  130.1 1.0 first.1
  131.1 13.7 %all_to_all.52.recv_ref = f32[64,4,128]{2,1,0:T(4,128)S(1)} all-to-all(f32[64,4,128]{2,1,0:T(4,128)S(1)} %get-tuple-element.34), channel_id=1, replica_groups=mesh['z'=8,'xh'=2,'xl'=2,'y'=8,'c'=2] {'xl','y','c'}, dimensions={0} | all-to-all | bytes 262144 | tf_op jit(solution)/shard_map/all_to_all | solution.py:341
  144.8 12.5 %all_to_all.53.recv_ref = f32[32,4,128]{2,1,0:T(4,128)S(1)} all-to-all(f32[32,4,128]{2,1,0:T(4,128)S(1)} %get-tuple-element.35), channel_id=1, replica_groups=mesh['z'=8,'xh'=2,'xl'=2,'y'=8,'c'=2] {'xl','y','c'}, dimensions={0} | all-to-all | bytes 131072 | tf_op jit(solution)/shard_map/all_to_all | solution.py:343
  157.9 14.2 %all_to_all.54.recv_ref = f32[16,16,256]{2,1,0:T(8,128)S(1)} all-to-all(f32[16,16,256]{2,1,0:T(8,128)S(1)} %get-tuple-element.36), channel_id=1, replica_groups=mesh['z'=8,'xh'=2,'xl'=2,'y'=8,'c'=2] {'z','xh'}, dimensions={0} | all-to-all | bytes 524288 | tf_op jit(solution)/shard_map/all_to_all | solution.py:345
  172.1 1.7 second.1
  173.9 6.8 %all-to-all-start.7 = ((f32[96,4,128]{2,1,0:T(4,128)}), f32[96,4,128]{2,1,0:T(4,128)S(1)}, u32[]{:S(2)}, u32[]{:S(2)}) async-start(f32[96,4,128]{2,1,0:T(4,128)} %get-tuple-element.39), calls=%async_computation.7 | async-start | bytes 393216 | tf_op jit(solution)/shard_map/all_to_all | solution.py:350
  180.7 10.2 %all-to-all-done.7.recv_ref = f32[96,4,128]{2,1,0:T(4,128)S(1)} async-done(((f32[96,4,128]{2,1,0:T(4,128)}), f32[96,4,128]{2,1,0:T(4,128)S(1)}, u32[]{:S(2)}, u32[]{:S(2)}) %all-to-all-start.7) | async-done | bytes 196640 | tf_op jit(solution)/shard_map/all_to_all | solution.py:350
  191.2 13.6 %all_to_all.55.recv_ref = f32[64,4,128]{2,1,0:T(4,128)S(1)} all-to-all(f32[64,4,128]{2,1,0:T(4,128)S(1)} %get-tuple-element.43), channel_id=1, replica_groups=mesh['z'=8,'xh'=2,'xl'=2,'y'=8,'c'=2] {'xl','y','c'}, dimensions={0} | all-to-all | bytes 262144 | tf_op jit(solution)/shard_map/all_to_all | solution.py:356
  204.9 11.4 %all_to_all.56.recv_ref = f32[16,1,128]{2,1,0:T(1,128)S(1)} all-to-all(f32[16,1,128]{2,1,0:T(1,128)S(1)} %get-tuple-element.44), channel_id=1, replica_groups=mesh['z'=8,'xh'=2,'xl'=2,'y'=8,'c'=2] {'z','xh'}, dimensions={0} | all-to-all | bytes 16384 | tf_op jit(solution)/shard_map/all_to_all | solution.py:360
  (28 shorter events, 4.8 us)
Async XLA Ops:
  0.0 18.3 %copy-start.4 = (bf16[1024,64]{0,1:T(8,128)(2,1)S(1)}, bf16[1024,64]{0,1:T(8,128)(2,1)}, u32[]{:S(2)}) copy-start(bf16[1024,64]{0,1:T(8,128)(2,1)} %param.4) | copy-start | bytes 393220
  1.1 0.9 copy-start.3
  19.4 32.7 %all-to-all-start = ((bf16[8,64,1024]{2,1,0:T(8,128)(2,1)}), bf16[8,64,1024]{2,1,0:T(8,128)(2,1)S(1)}, u32[]{:S(2)}, u32[]{:S(2)}) async-start(bf16[8,64,1024]{2,1,0:T(8,128)(2,1)} %broadcast_in_dim.30), calls=%async_computation | async-start | bytes 2097152 | tf_op jit(solution)/shard_map/all_to_all | solution.py:310
  52.1 39.4 %all-to-all-start.2 = ((bf16[16,32,1024]{2,1,0:T(8,128)(2,1)}), bf16[16,32,1024]{2,1,0:T(8,128)(2,1)S(1)}, u32[]{:S(2)}, u32[]{:S(2)}) async-start(bf16[16,32,1024]{2,1,0:T(8,128)(2,1)} %spread.1), calls=%async_computation.2 | async-start | bytes 2097152 | tf_op jit(solution)/shard_map/all_to_all | solution.py:320
  64.4 35.7 %collective-permute-start = (bf16[512,1024]{1,0:T(8,128)(2,1)S(1)}, bf16[512,1024]{1,0:T(8,128)(2,1)S(1)}, u32[]{:S(2)}, u32[]{:S(2)}) collective-permute-start(bf16[512,1024]{1,0:T(8,128)(2,1)S(1)} %bitcast.9), channel_id=1, source_target_pairs={{0,16},{16,0},{1,17},{17,1},{2,18},{18,2},{3,19},{19,3},{4,20},{20... | collective-permute-start | bytes 3145736 | tf_op jit(solution)/shard_map/ppermute | solution.py:312
  92.3 8.3 %copy-start = (f32[256,1024]{1,0:T(8,128)}, f32[256,1024]{1,0:T(8,128)S(1)}, u32[]{:S(2)}) copy-start(f32[256,1024]{1,0:T(8,128)S(1)} %get-tuple-element.27.near_ref) | copy-start | bytes 3145732
  100.5 6.0 %collective-permute-start.1 = (f32[264,1024]{1,0:T(8,128)S(1)}, f32[264,1024]{1,0:T(8,128)}, u32[]{:S(2)}, u32[]{:S(2)}) collective-permute-start(f32[264,1024]{1,0:T(8,128)S(1)} %other.1.sent_ref), channel_id=1, source_target_pairs={{0,1},{1,0},{2,3},{3,2},{4,5},{5,4},{6,7},{7,6},{8,9},{9,8},{10,11... | collective-permute-start | bytes 3244040 | tf_op jit(solution)/shard_map/ppermute | solution.py:331
  104.3 1.2 copy-start.1
  105.5 1.0 copy-start.5
  106.5 23.6 %copy-start.2 = (f32[256,256]{1,0:T(8,128)S(1)}, f32[256,256]{1,0:T(8,128)}, u32[]{:S(2)}) copy-start(f32[256,256]{1,0:T(8,128)} %pre_ref.3) | copy-start | bytes 786436
  173.9 17.0 %all-to-all-start.7 = ((f32[96,4,128]{2,1,0:T(4,128)}), f32[96,4,128]{2,1,0:T(4,128)S(1)}, u32[]{:S(2)}, u32[]{:S(2)}) async-start(f32[96,4,128]{2,1,0:T(4,128)} %get-tuple-element.39), calls=%async_computation.7 | async-start | bytes 393216 | tf_op jit(solution)/shard_map/all_to_all | solution.py:350

commit v3 on v2

--- a/solution.py
+++ b/solution.py
@@ -1,11 +1,10 @@
-import functools
-
 import jax
 import jax.numpy as jnp
 from jax import lax
 from jax.experimental import pallas as pl
 from jax.experimental.pallas import tpu as pltpu
 from jax.sharding import Mesh, PartitionSpec as P
+
 
 CLASSES = 16
 GAMMA = 4.0
@@ -24,6 +23,8 @@
 SLICE = 64
 WIDTH = N_PLANE * SLICE
 F = 2048
+N_Y = 8
+OFFSETS = (0, -1, 1, -2, 2, -3, 3, 4)
 EXAMPLES = ROWS * N_EX
 
 EX = ("z", "xh")
@@ -52,19 +53,24 @@
     return jnp.sum(jnp.where(place, row, 0.0), axis=1, keepdims=True)
 
 
-def call(kernel, outs, *args, name, smem=0, space=pltpu.VMEM):
-    spec = [pl.BlockSpec(memory_space=pltpu.SMEM)] * smem
-    spec += [pl.BlockSpec(memory_space=pltpu.VMEM)] * (len(args) - smem)
+def call(kernel, outs, *args, smem=0, hbm=0, space=pltpu.VMEM, scratch=()):
+    vmem = len(args) - smem - hbm
+    spaces = [pltpu.SMEM] * smem + [pltpu.VMEM] * vmem + [pl.ANY] * hbm
+    args = list(args)
+    for i in range(smem, smem + vmem):
+        args[i] = pltpu.with_memory_space_constraint(args[i], pltpu.VMEM)
+    for i in range(smem + vmem, len(args)):
+        args[i] = pltpu.with_memory_space_constraint(args[i], pltpu.HBM)
     many = isinstance(outs, list)
     out_spec = pl.BlockSpec(memory_space=pltpu.VMEM)
     return pl.pallas_call(
         kernel,
-        out_shape=[pltpu.VMEM(s, d) for s, d in outs] if many else space(*outs),
-        in_specs=spec,
+        out_shape=[space(s, d) for s, d in outs] if many else space(*outs),
+        in_specs=[pl.BlockSpec(memory_space=m) for m in spaces],
         out_specs=[out_spec] * len(outs) if many else out_spec,
-        name=name,
+        scratch_shapes=scratch,
         compiler_params=pltpu.CompilerParams(vmem_limit_bytes=12 << 20),
-    )(*[x if i < smem else pltpu.with_memory_space_constraint(x, pltpu.VMEM) for i, x in enumerate(args)])
+    )(*args)
 
 
 def pick_kernel(ft_ref, own_ref, other_ref, out_ref):
@@ -82,13 +88,13 @@
     out_ref[...] = both.astype(BF16).reshape(N_PLANE, OWN, 2 * SLICE)
 
 
-def spread_kernel(side_ref, in_ref, out_ref):
+def spread_kernel(place_ref, in_ref, out_ref):
     low = iota((OWN, 128), 1) < SLICE
-    half = N_PLANE // 2
-    for t in range(half):
-        source = 2 * (t % (half // 2)) + half * (side_ref[0] if t < half // 2 else 1 - side_ref[0])
-        a = in_ref[source].astype(F32)
-        b = in_ref[source + 1].astype(F32)
+    side, y = place_ref[0], place_ref[1]
+    for t, offset in enumerate(OFFSETS):
+        row = lax.rem(y + (offset + N_Y), N_Y)
+        a = in_ref[side * N_Y + row].astype(F32)
+        b = in_ref[(1 - side) * N_Y + row].astype(F32)
         own = jnp.where(low, a, pltpu.roll(b, SLICE, 1)).astype(BF16)
         other = jnp.where(low, pltpu.roll(a, SLICE, 1), b).astype(BF16)
         cols = slice(128 * t, 128 * t + 128)
@@ -97,40 +103,43 @@
             out_ref[i, OWN : 2 * OWN, cols] = other
 
 
-def pick_centres(cen_ref, first, half):
-    return cen_ref[:, first : first + OWN, half * WIDTH // 2 : (half + 1) * WIDTH // 2].reshape(BLOCK, WIDTH // 2)
-
-
-def row_squares(ft_ref):
-    return jnp.sum(jnp.square(ft_ref[...].astype(F32)), axis=0, keepdims=True)
-
-
-def near_kernel(ft_ref, cen_ref, other_ref, own_ref, own_sq_ref):
+def diagonal():
+    return iota((BLOCK, BLOCK), 0) == iota((BLOCK, BLOCK), 1)
+
+
+def half_dots(ft, cen_ref, first):
+    block = cen_ref[:, first : first + OWN, :].reshape(BLOCK, WIDTH)
+    squares = jnp.sum(jnp.square(block.astype(F32)), axis=1, keepdims=True)
+    squares = jnp.sum(jnp.where(diagonal(), squares, 0.0), axis=0, keepdims=True)
+    return jnp.dot(block, ft, preferred_element_type=F32), squares
+
+
+def dots_kernel(near_ref, far_ref, cen_ref, *refs):
+    *chunk_hbm, out_ref, dots_ref, squares_ref, ft_ref, sems = refs
+    copies = []
+    for i, chunk in enumerate(chunk_hbm):
+        copies.append(pltpu.make_async_copy(chunk, ft_ref.at[128 * i : 128 * i + 128], sems.at[i]))
+        copies[-1].start()
+    first = 128 * len(chunk_hbm)
+    ft_ref[first : first + SLICE] = near_ref[...]
+    ft_ref[first + SLICE : first + 2 * SLICE] = far_ref[...]
+
+    def squares(start):
+        return jnp.sum(jnp.square(ft_ref[start : start + 128].astype(F32)), axis=0, keepdims=True)
+
+    row_sq = squares(first)
+    for i, copy in enumerate(copies):
+        copy.wait()
+        row_sq += squares(128 * i)
+    out_ref[BLOCK : BLOCK + 8, :] = jnp.zeros((8, ROWS), F32)
+    out_ref[BLOCK : BLOCK + 1, :] = row_sq
     ft = ft_ref[...]
-    other_ref[0:BLOCK, :] = jnp.dot(pick_centres(cen_ref, OWN, 0), ft, preferred_element_type=F32)
-    own_ref[...] = jnp.dot(pick_centres(cen_ref, 0, 0), ft, preferred_element_type=F32)
-
-    def squares(first):
-        block = cen_ref[:, first : first + OWN, :].reshape(BLOCK, WIDTH).astype(F32)
-        return jnp.sum(jnp.square(block), axis=1, keepdims=True)
-
-    other_ref[BLOCK : BLOCK + 8, :] = jnp.zeros((8, ROWS), F32)
-    other_ref[BLOCK : BLOCK + 1, :] = row_squares(ft_ref)
-    same = iota((BLOCK, BLOCK), 0) == iota((BLOCK, BLOCK), 1)
-    other_ref[BLOCK + 1 : BLOCK + 2, 0:BLOCK] = jnp.sum(jnp.where(same, squares(OWN), 0.0), axis=0, keepdims=True)
-    own_sq_ref[...] = jnp.broadcast_to(squares(0), (BLOCK, 128))
-
-
-def other_kernel(ft_ref, cen_ref, near_ref, out_ref):
-    block = pick_centres(cen_ref, OWN, 1)
-    out_ref[0:BLOCK, :] = near_ref[0:BLOCK, :] + jnp.dot(block, ft_ref[...], preferred_element_type=F32)
-    out_ref[BLOCK : BLOCK + 8, :] = near_ref[BLOCK : BLOCK + 8, :]
-    out_ref[BLOCK : BLOCK + 1, :] = near_ref[BLOCK : BLOCK + 1, :] + row_squares(ft_ref)
-
-
-def own_kernel(ft_ref, cen_ref, near_ref, out_ref):
-    block = pick_centres(cen_ref, 0, 1)
-    out_ref[...] = near_ref[...] + jnp.dot(block, ft_ref[...], preferred_element_type=F32)
+    dots, squares = half_dots(ft, cen_ref, OWN)
+    out_ref[0:BLOCK, :] = dots
+    out_ref[BLOCK + 1 : BLOCK + 2, 0:BLOCK] = squares
+    dots, squares = half_dots(ft, cen_ref, 0)
+    dots_ref[...] = dots
+    squares_ref[...] = jnp.broadcast_to(squares, (8, BLOCK))
 
 
 def split2(x):
@@ -150,20 +159,25 @@
     return y[0:n] + (y[n : 2 * n] + y[2 * n : 3 * n])
 
 
-def panel_kernel(dots_ref, squares_ref, sent_ref, recv_ref, labels_ref, loc_ref, high_ref, low_ref, place_ref, out_ref):
+def panel_kernel(
+    dots_ref, squares_ref, sent_ref, labels_ref, loc_ref, recv_hbm, high_ref, low_ref, place_ref, out_ref, recv_ref, sem
+):
+    copy = pltpu.make_async_copy(recv_hbm, recv_ref, sem)
+    copy.start()
+    place_ref[...] = (iota((BLOCK, ROWS), 1) == loc_ref[...]).astype(F32).astype(BF16)
+    hit = iota((CLASSES, ROWS), 0) == labels_ref[...]
+    targets = jnp.where(hit, CLASSES - 1.0, -1.0).astype(BF16)
+    copy.wait()
     row_sq = sent_ref[BLOCK : BLOCK + 1, :] + recv_ref[BLOCK : BLOCK + 1, :]
-    same = iota((BLOCK, BLOCK), 0) == iota((BLOCK, BLOCK), 1)
-    got = jnp.sum(jnp.where(same, recv_ref[BLOCK + 1 : BLOCK + 2, 0:BLOCK], 0.0), axis=1, keepdims=True)
+    centre_sq = squares_ref[0:1, :] + recv_ref[BLOCK + 1 : BLOCK + 2, 0:BLOCK]
+    centre_sq = jnp.sum(jnp.where(diagonal(), centre_sq, 0.0), axis=1, keepdims=True)
     row_scale = lax.rsqrt(row_sq / F + EPS)
-    centre_scale = lax.rsqrt((squares_ref[:, 0:1] + got) / F + EPS)
+    centre_scale = lax.rsqrt(centre_sq / F + EPS)
     dots = dots_ref[...] + recv_ref[0:BLOCK, :]
     cosine = jnp.clip(dots * row_scale * centre_scale, -1.0, 1.0)
     high, low = split2(jnp.exp(GAMMA * (cosine - 1.0)))
     high_ref[...] = high
     low_ref[...] = low
-    place_ref[...] = (iota((BLOCK, ROWS), 1) == loc_ref[...]).astype(F32).astype(BF16)
-    hit = iota((CLASSES, ROWS), 0) == labels_ref[...]
-    targets = jnp.where(hit, CLASSES - 1.0, -1.0).astype(BF16)
     rhs = (dot_t(targets, high, None) + dot_t(targets, low, None)) / EXAMPLES
     for i in range(N_EX):
         out_ref[i] = rhs
@@ -301,22 +315,30 @@
     out_ref[...] = alpha * k + alpha_next * (kz_ref[...] + beta * k)
 
 
-def per_device(features, centre_index, labels, precond):
+def predict(features, centre_index, labels, precond):
     ex_index = lax.axis_index(EX)
     feat_index = lax.axis_index(FEAT)
     core = lax.axis_index("c")
     local = centre_index[:, 0, :] - ex_index * ROWS
     ft_local = features.T
-    near = lax.all_to_all(jnp.broadcast_to(ft_local[None], (8, SLICE, ROWS)), "y", 0, 0, tiled=True)
-    near = near.reshape(WIDTH // 2, ROWS)
-    far = lax.ppermute(near, "xl", [(0, 1), (1, 0)])
+    swapped = lax.ppermute(ft_local, "xl", [(0, 1), (1, 0)])
+    here = jnp.concatenate([ft_local, swapped], axis=0)
+    up = [(i, (i + 1) % N_Y) for i in range(N_Y)]
+    down = [(i, (i - 1) % N_Y) for i in range(N_Y)]
+    chunks = [here]
+    below = above = here
+    for _ in range(3):
+        below = lax.ppermute(below, "y", up)
+        above = lax.ppermute(above, "y", down)
+        chunks += [below, above]
+    chunks += [lax.ppermute(below[:SLICE], "y", up), lax.ppermute(above[SLICE:], "y", down)]
 
     pair = local.reshape(N_PLANE, 2, OWN)
     own_col = jnp.where(core == 0, pair[:, 0], pair[:, 1]).reshape(N_PLANE * OWN, 1)
     other_col = jnp.where(core == 0, pair[:, 1], pair[:, 0]).reshape(N_PLANE * OWN, 1)
-    picked = call(pick_kernel, ((N_PLANE, OWN, 2 * SLICE), BF16), ft_local, own_col, other_col, name="pick")
+    picked = call(pick_kernel, ((N_PLANE, OWN, 2 * SLICE), BF16), ft_local, own_col, other_col)
     picked = lax.all_to_all(picked, PLANE, 0, 0, tiled=True)
-    spread = call(spread_kernel, ((N_EX, 2 * OWN, WIDTH), BF16), lax.axis_index("xl").reshape(1), picked, name="spread", smem=1)
+    spread = call(spread_kernel, ((N_EX, 2 * OWN, WIDTH), BF16), jnp.stack([lax.axis_index("xl"), lax.axis_index("y")]), picked, smem=1)
     cen = lax.all_to_all(spread, EX, 0, 0, tiled=True)
 
     own_rows = lax.dynamic_index_in_dim(local, feat_index, 0, keepdims=False)
@@ -324,45 +346,44 @@
     loc = jnp.where(slot, own_rows[None, :], -1).reshape(BLOCK, 1)
 
     dots_t = ((BLOCK, ROWS), F32)
-    other, own, own_sq = call(
-        near_kernel, [((BLOCK + 8, ROWS), F32), dots_t, ((BLOCK, 128), F32)], near, cen, name="near"
+    sent, own, own_sq = call(
+        dots_kernel, [((BLOCK + 8, ROWS), F32), dots_t, ((8, BLOCK), F32)], *chunks[-2:], cen, *chunks[:-2],
+        hbm=len(chunks) - 2,
+        scratch=[pltpu.VMEM((WIDTH, ROWS), BF16), pltpu.SemaphoreType.DMA((len(chunks) - 2,))],
     )
-    sent = call(other_kernel, ((BLOCK + 8, ROWS), F32), far, cen, other, name="other")
     got = lax.ppermute(sent, "c", [(0, 1), (1, 0)])
-    own = call(own_kernel, dots_t, far, cen, own, name="own")
     half_t = ((BLOCK, ROWS), BF16)
     high, low, place, part = call(
         panel_kernel, [half_t, half_t, half_t, ((N_EX, CLASSES, BLOCK), F32)],
-        own, own_sq, sent, got, labels.reshape(1, ROWS), loc, name="panel",
+        own, own_sq, sent, labels.reshape(1, ROWS), loc, got, hbm=1,
+        scratch=[pltpu.VMEM(sent.shape, F32), pltpu.SemaphoreType.DMA],
     )
     vec = ((CLASSES, BLOCK), F32)
     part = lax.all_to_all(part, EX, 0, 0, tiled=True)
-    rhs, u, part = call(first_kernel, [vec, vec, ((N_FEAT * 2, 4, 128), F32)], part, precond, high, low, place, name="first")
+    rhs, u, part = call(first_kernel, [vec, vec, ((N_FEAT * 2, 4, 128), F32)], part, precond, high, low, place)
     part = lax.all_to_all(part, FEAT, 0, 0, tiled=True)
-    chunk, part = call(chunk_kernel, [((2, 4, 128), F32), ((N_FEAT, 4, 128), F32)], part, name="chunk")
+    chunk, part = call(chunk_kernel, [((2, 4, 128), F32), ((N_FEAT, 4, 128), F32)], part)
     part = lax.all_to_all(part, FEAT, 0, 0, tiled=True)
-    k, part = call(normal_kernel, [((CLASSES, ROWS), F32), ((N_EX, CLASSES, BLOCK), F32)], part, high, low, place, name="normal")
+    k, part = call(normal_kernel, [((CLASSES, ROWS), F32), ((N_EX, CLASSES, BLOCK), F32)], part, high, low, place)
     part = lax.all_to_all(part, EX, 0, 0, tiled=True)
     image, v, part = call(
         second_kernel, [vec, vec, ((N_FEAT * 3, 4, 128), F32)],
-        part, precond, high, low, place, rhs, u, name="second",
+        part, precond, high, low, place, rhs, u,
     )
     part = lax.all_to_all(part, FEAT, 0, 0, tiled=True)
     group = (feat_index // 8).reshape(1)
     scal, part = call(
         step_kernel, [((8, 128), F32), ((N_FEAT * 2, 4, 128), F32)],
-        group, part, chunk, rhs, u, image, v, name="step", smem=1,
+        group, part, chunk, rhs, u, image, v, smem=1,
     )
     part = lax.all_to_all(part, FEAT, 0, 0, tiled=True)
-    kz, tail, part = call(
-        gather_kernel, [((CLASSES, ROWS), F32), ((4, 128), F32), ((N_EX, 1, 128), F32)], part, name="gather"
-    )
+    kz, tail, part = call(gather_kernel, [((CLASSES, ROWS), F32), ((4, 128), F32), ((N_EX, 1, 128), F32)], part)
     part = lax.all_to_all(part, EX, 0, 0, tiled=True)
-    out = call(last_kernel, ((CLASSES, ROWS), F32), part, tail, scal, k, kz, name="last", space=jax.ShapeDtypeStruct)
+    out = call(last_kernel, ((CLASSES, ROWS), F32), part, tail, scal, k, kz, space=jax.ShapeDtypeStruct)
     return out.T
 
 
 def solution(mesh):
     fine = Mesh(mesh.devices.reshape(8, 2, 2, 8, 2), ("z", "xh", "xl", "y", "c"))
     in_specs = (P(EX, FEAT), P(None, EX, None), P(EX), P(FEAT, None))
-    return jax.shard_map(per_device, mesh=fine, in_specs=in_specs, out_specs=P(EX, None), check_vma=False)
+    return jax.shard_map(predict, mesh=fine, in_specs=in_specs, out_specs=P(EX, None), check_vma=False)

time: 218 us -> 202 us (0.927)
  waiting for transfers between devices: 71.5 us -> 32 us
  starting transfers between devices: 28.1 us -> 65.7 us
  blocking collectives: 103 us -> 88.4 us
  local copies, waits for them, and re-layouts: 4.36 us -> 2.04 us
    all_to_all x3, waiting for transfers between devices: 63.2 us -> 17.5 us  [the longest x1 10.2 us: predict(): part = lax.all_to_all(part, FEAT, 0, 0, tiled=True)]
    ppermute x2 -> x10, starting transfers between devices: 5.46 us -> 37.8 us  [the longest x3 13 us: predict(): above = lax.ppermute(above, 'y', down)]
    all_to_all x7 -> x6, blocking collectives: 103 us -> 88.4 us  [the longest x3 46.6 us: predict(): part = lax.all_to_all(part, EX, 0, 0, tiled=True)]
    ppermute x2 -> x10, waiting for transfers between devices: 8.35 us -> 14.5 us  [the longest x3 5.98 us: predict(): below = lax.ppermute(below, 'y', up)]
    all_to_all x3, starting transfers between devices: 22.7 us -> 27.9 us  [the longest x1 12.4 us: predict(): cen = lax.all_to_all(spread, EX, 0, 0, tiled=True)]
    pallas_call x13 -> x11, Pallas kernels: 10.1 us -> 12.1 us  [call(): pl.pallas_call(kernel, out_shape=[space(s, d) for s, d in outs] if many e...]
  transfers between devices with their start and end apart: 5 -> 13, of which waited for: 5 -> 9; matrix products, arithmetic and copies ran while one was open for 0% -> 0% of each run, Pallas kernels for 1% -> 0%
where the time goes in v3:
time: 202 us; the launch traced here: 201 us
  blocking collectives  88.4 us (44%)
  starting transfers between devices  65.7 us (33%)
  waiting for transfers between devices  32 us (16%)
  Pallas kernels  12.1 us (6%)
  local copies, waits for them, and re-layouts  2.04 us (1%)
    all_to_all x3, blocking collectives, predict(): part = lax.all_to_all(part, EX, 0, 0, tiled=True)  46.6 us
    all_to_all x3, blocking collectives, predict(): part = lax.all_to_all(part, FEAT, 0, 0, tiled=True)  41.9 us
    ppermute x3, starting transfers between devices, predict(): above = lax.ppermute(above, 'y', down)  13 us
    all_to_all x1, starting transfers between devices, predict(): cen = lax.all_to_all(spread, EX, 0, 0, tiled=True)  12.4 us
    pallas_call x11, Pallas kernels, call(): pl.pallas_call(kernel, out_shape=[space(s, d) for s, d in outs] if many e...  12.1 us
    all_to_all x1, waiting for transfers between devices, predict(): part = lax.all_to_all(part, FEAT, 0, 0, tiled=True)  10.2 us
    ppermute x1, starting transfers between devices, predict(): got = lax.ppermute(sent, 'c', [(0, 1), (1, 0)])  9.79 us
    all_to_all x1, starting transfers between devices, predict(): picked = lax.all_to_all(picked, PLANE, 0, 0, tiled=True)  8.67 us
  transfers between devices with their start and end apart: 13, of which 9 were waited for; matrix products, arithmetic and copies ran while one was open for 0% of the time, Pallas kernels for 0%

profile of v3, /device:TPU:1, one launch (start us, length us, event | category | flops | bytes accessed | tf_op | source)
XLA Modules:
  0.0 200.9 jit_solution(5241085948037431790)
XLA Ops:
  3.1 8.7 %all-to-all-start = ((bf16[16,16,128]{2,1,0:T(8,128)(2,1)}), bf16[16,16,128]{2,1,0:T(8,128)(2,1)S(1)}, u32[]{:S(2)}, u32[]{:S(2)}) async-start(bf16[16,16,128]{2,1,0:T(8,128)(2,1)} %shard_map.46), calls=%async_computation | async-start | bytes 131072 | tf_op jit(solution)/shard_map/all_to_all | solution.py:340
  11.8 7.3 %all-to-all-done.in_ref = bf16[16,16,128]{2,1,0:T(8,128)(2,1)S(1)} async-done(((bf16[16,16,128]{2,1,0:T(8,128)(2,1)}), bf16[16,16,128]{2,1,0:T(8,128)(2,1)S(1)}, u32[]{:S(2)}, u32[]{:S(2)}) %all-to-all-start) | async-done | bytes 65568 | tf_op jit(solution)/shard_map/all_to_all | solution.py:340
  21.0 12.4 %all-to-all-start.1 = ((bf16[16,32,1024]{2,1,0:T(8,128)(2,1)}), bf16[16,32,1024]{2,1,0:T(8,128)(2,1)S(1)}, u32[]{:S(2)}, u32[]{:S(2)}) async-start(bf16[16,32,1024]{2,1,0:T(8,128)(2,1)} %shard_map.47), calls=%async_computation.1 | async-start | bytes 2097152 | tf_op jit(solution)/shard_map/all_to_all | solution.py:342
  33.4 1.9 collective-permute-start
  35.4 3.8 %collective-permute-done = bf16[64,1024]{1,0:T(8,128)(2,1)S(1)} collective-permute-done((bf16[64,1024]{1,0:T(8,128)(2,1)S(1)}, bf16[64,1024]{1,0:T(8,128)(2,1)S(1)}, u32[]{:S(2)}, u32[]{:S(2)}) %collective-permute-start) | collective-permute-done | bytes 131104 | tf_op jit(solution)/shard_map/ppermute | solution.py:324
  39.2 2.6 %collective-permute-start.1 = (bf16[128,1024]{1,0:T(8,128)(2,1)S(1)}, bf16[128,1024]{1,0:T(8,128)(2,1)S(1)}, u32[]{:S(2)}, u32[]{:S(2)}) collective-permute-start(bf16[128,1024]{1,0:T(8,128)(2,1)S(1)} %pad_maximum_fusion.refs_0_), channel_id=1, source_target_pairs={{0,2},{2,4},{4,6},{6,8},{8,10},{10,12},{12,14},{14,0},{1,3},{3,5},... | collective-permute-start | bytes 786440 | tf_op jit(solution)/shard_map/ppermute | solution.py:331
  41.8 3.9 %collective-permute-start.5 = (bf16[128,1024]{1,0:T(8,128)(2,1)S(1)}, bf16[128,1024]{1,0:T(8,128)(2,1)S(1)}, u32[]{:S(2)}, u32[]{:S(2)}) collective-permute-start(bf16[128,1024]{1,0:T(8,128)(2,1)S(1)} %pad_maximum_fusion.refs_0_), channel_id=1, source_target_pairs={{0,14},{2,0},{4,2},{6,4},{8,6},{10,8},{12,10},{14,12},{1,15},{3,1}... | collective-permute-start | bytes 786440 | tf_op jit(solution)/shard_map/ppermute | solution.py:332
  45.7 2.1 %collective-permute-done.1.refs_1_ = bf16[128,1024]{1,0:T(8,128)(2,1)S(1)} collective-permute-done((bf16[128,1024]{1,0:T(8,128)(2,1)S(1)}, bf16[128,1024]{1,0:T(8,128)(2,1)S(1)}, u32[]{:S(2)}, u32[]{:S(2)}) %collective-permute-start.1) | collective-permute-done | bytes 262176 | tf_op jit(solution)/shard_map/ppermute | solution.py:331
  49.8 4.6 %collective-permute-start.6 = (bf16[128,1024]{1,0:T(8,128)(2,1)S(1)}, bf16[128,1024]{1,0:T(8,128)(2,1)S(1)}, u32[]{:S(2)}, u32[]{:S(2)}) collective-permute-start(bf16[128,1024]{1,0:T(8,128)(2,1)S(1)} %collective-permute-done.5.refs_2_), channel_id=1, source_target_pairs={{0,14},{2,0},{4,2},{6,4},{8,6},{10,8},{12,10},{14,12},{1,15},{3,1}... | collective-permute-start | bytes 786440 | tf_op jit(solution)/shard_map/ppermute | solution.py:332
  54.3 2.1 %collective-permute-done.2.refs_3_ = bf16[128,1024]{1,0:T(8,128)(2,1)S(1)} collective-permute-done((bf16[128,1024]{1,0:T(8,128)(2,1)S(1)}, bf16[128,1024]{1,0:T(8,128)(2,1)S(1)}, u32[]{:S(2)}, u32[]{:S(2)}) %collective-permute-start.2) | collective-permute-done | bytes 262176 | tf_op jit(solution)/shard_map/ppermute | solution.py:331
  58.4 4.6 %collective-permute-start.7 = (bf16[128,1024]{1,0:T(8,128)(2,1)S(1)}, bf16[128,1024]{1,0:T(8,128)(2,1)S(1)}, u32[]{:S(2)}, u32[]{:S(2)}) collective-permute-start(bf16[128,1024]{1,0:T(8,128)(2,1)S(1)} %collective-permute-done.6.refs_4_), channel_id=1, source_target_pairs={{0,14},{2,0},{4,2},{6,4},{8,6},{10,8},{12,10},{14,12},{1,15},{3,1}... | collective-permute-start | bytes 786440 | tf_op jit(solution)/shard_map/ppermute | solution.py:332
  66.7 4.7 %collective-permute-start.8 = (bf16[64,1024]{1,0:T(8,128)(2,1)S(1)}, bf16[64,1024]{1,0:T(8,128)(2,1)S(1)}, u32[]{:S(2)}, u32[]{:S(2)}) collective-permute-start(bf16[64,1024]{1,0:T(8,128)(2,1)S(1)} %slice.19), channel_id=1, source_target_pairs={{0,14},{2,0},{4,2},{6,4},{8,6},{10,8},{12,10},{14,12},{1,15},{3,1}... | collective-permute-start | bytes 393224 | tf_op jit(solution)/shard_map/ppermute | solution.py:334
  74.0 2.8 %shard_map.48 = (f32[264,1024]{1,0:T(8,128)S(1)}, f32[256,1024]{1,0:T(8,128)S(1)}, f32[8,256]{1,0:T(8,128)S(1)}) custom-call(bf16[64,1024]{1,0:T(8,128)(2,1)S(1)} %collective-permute-done.4.near_ref, bf16[64,1024]{1,0:T(8,128)(2,1)S(1)} %collective-permute-done.8.far_ref, bf16[16,32,1024]{2,1,0:T(8,128)(2,1)S(1)} %all-to-all-done.1.cen_ref, ...), custom_call_target="tpu_custom_call" | custom-call | tf_op jit(solution)/shard_map/pallas_call | solution.py:66
  76.7 9.8 %collective-permute-start.9 = (f32[264,1024]{1,0:T(8,128)S(1)}, f32[264,1024]{1,0:T(8,128)}, u32[]{:S(2)}, u32[]{:S(2)}) collective-permute-start(f32[264,1024]{1,0:T(8,128)S(1)} %get-tuple-element.29.sent_ref), channel_id=1, source_target_pairs={{0,1},{1,0},{2,3},{3,2},{4,5},{5,4},{6,7},{7,6},{8,9},{9,8},{10,11... | collective-permute-start | bytes 3244040 | tf_op jit(solution)/shard_map/ppermute | solution.py:354
  86.8 2.2 %collective-permute-done.9.recv_hbm = f32[264,1024]{1,0:T(8,128)} collective-permute-done((f32[264,1024]{1,0:T(8,128)S(1)}, f32[264,1024]{1,0:T(8,128)}, u32[]{:S(2)}, u32[]{:S(2)}) %collective-permute-start.9) | collective-permute-done | bytes 1081376 | tf_op jit(solution)/shard_map/ppermute | solution.py:354
  89.0 1.9 shard_map.49
  90.9 20.9 %all_to_all.45.recv_ref = f32[16,16,256]{2,1,0:T(8,128)S(1)} all-to-all(f32[16,16,256]{2,1,0:T(8,128)S(1)} %get-tuple-element.30), channel_id=1, replica_groups=mesh['z'=8,'xh'=2,'xl'=2,'y'=8,'c'=2] {'z','xh'}, dimensions={0} | all-to-all | bytes 524288 | tf_op jit(solution)/shard_map/all_to_all | solution.py:362
  112.8 15.8 %all_to_all.46.recv_ref = f32[64,4,128]{2,1,0:T(4,128)S(1)} all-to-all(f32[64,4,128]{2,1,0:T(4,128)S(1)} %get-tuple-element.34), channel_id=1, replica_groups=mesh['z'=8,'xh'=2,'xl'=2,'y'=8,'c'=2] {'xl','y','c'}, dimensions={0} | all-to-all | bytes 262144 | tf_op jit(solution)/shard_map/all_to_all | solution.py:364
  128.7 12.5 %all_to_all.47.recv_ref = f32[32,4,128]{2,1,0:T(4,128)S(1)} all-to-all(f32[32,4,128]{2,1,0:T(4,128)S(1)} %get-tuple-element.35), channel_id=1, replica_groups=mesh['z'=8,'xh'=2,'xl'=2,'y'=8,'c'=2] {'xl','y','c'}, dimensions={0} | all-to-all | bytes 131072 | tf_op jit(solution)/shard_map/all_to_all | solution.py:366
  141.8 14.2 %all_to_all.48.recv_ref = f32[16,16,256]{2,1,0:T(8,128)S(1)} all-to-all(f32[16,16,256]{2,1,0:T(8,128)S(1)} %get-tuple-element.36), channel_id=1, replica_groups=mesh['z'=8,'xh'=2,'xl'=2,'y'=8,'c'=2] {'z','xh'}, dimensions={0} | all-to-all | bytes 524288 | tf_op jit(solution)/shard_map/all_to_all | solution.py:368
  157.7 6.8 %all-to-all-start.6 = ((f32[96,4,128]{2,1,0:T(4,128)}), f32[96,4,128]{2,1,0:T(4,128)S(1)}, u32[]{:S(2)}, u32[]{:S(2)}) async-start(f32[96,4,128]{2,1,0:T(4,128)} %get-tuple-element.39), calls=%async_computation.6 | async-start | bytes 393216 | tf_op jit(solution)/shard_map/all_to_all | solution.py:373
  164.6 10.2 %all-to-all-done.6.recv_ref = f32[96,4,128]{2,1,0:T(4,128)S(1)} async-done(((f32[96,4,128]{2,1,0:T(4,128)}), f32[96,4,128]{2,1,0:T(4,128)S(1)}, u32[]{:S(2)}, u32[]{:S(2)}) %all-to-all-start.6) | async-done | bytes 196640 | tf_op jit(solution)/shard_map/all_to_all | solution.py:373
  175.1 13.6 %all_to_all.49.recv_ref = f32[64,4,128]{2,1,0:T(4,128)S(1)} all-to-all(f32[64,4,128]{2,1,0:T(4,128)S(1)} %get-tuple-element.43), channel_id=1, replica_groups=mesh['z'=8,'xh'=2,'xl'=2,'y'=8,'c'=2] {'xl','y','c'}, dimensions={0} | all-to-all | bytes 262144 | tf_op jit(solution)/shard_map/all_to_all | solution.py:379
  188.8 11.4 %all_to_all.50.recv_ref = f32[16,1,128]{2,1,0:T(1,128)S(1)} all-to-all(f32[16,1,128]{2,1,0:T(1,128)S(1)} %get-tuple-element.44), channel_id=1, replica_groups=mesh['z'=8,'xh'=2,'xl'=2,'y'=8,'c'=2] {'z','xh'}, dimensions={0} | all-to-all | bytes 16384 | tf_op jit(solution)/shard_map/all_to_all | solution.py:381
  (54 shorter events, 19.7 us)
Async XLA Ops:
  1.0 0.9 copy-start.1
  3.1 16.1 %all-to-all-start = ((bf16[16,16,128]{2,1,0:T(8,128)(2,1)}), bf16[16,16,128]{2,1,0:T(8,128)(2,1)S(1)}, u32[]{:S(2)}, u32[]{:S(2)}) async-start(bf16[16,16,128]{2,1,0:T(8,128)(2,1)} %shard_map.46), calls=%async_computation | async-start | bytes 131072 | tf_op jit(solution)/shard_map/all_to_all | solution.py:340
  21.0 12.4 %copy-start.2 = (bf16[1024,64]{0,1:T(8,128)(2,1)S(1)}, bf16[1024,64]{0,1:T(8,128)(2,1)}, u32[]{:S(2)}) copy-start(bf16[1024,64]{0,1:T(8,128)(2,1)} %param.4) | copy-start | bytes 393220
  21.0 53.0 %all-to-all-start.1 = ((bf16[16,32,1024]{2,1,0:T(8,128)(2,1)}), bf16[16,32,1024]{2,1,0:T(8,128)(2,1)S(1)}, u32[]{:S(2)}, u32[]{:S(2)}) async-start(bf16[16,32,1024]{2,1,0:T(8,128)(2,1)} %shard_map.47), calls=%async_computation.1 | async-start | bytes 2097152 | tf_op jit(solution)/shard_map/all_to_all | solution.py:342
  33.4 5.7 %collective-permute-start = (bf16[64,1024]{1,0:T(8,128)(2,1)S(1)}, bf16[64,1024]{1,0:T(8,128)(2,1)S(1)}, u32[]{:S(2)}, u32[]{:S(2)}) collective-permute-start(bf16[64,1024]{1,0:T(8,128)(2,1)S(1)} %bitcast.10), channel_id=1, source_target_pairs={{0,16},{16,0},{1,17},{17,1},{2,18},{18,2},{3,19},{19,3},{4,20},{20... | collective-permute-start | bytes 393224 | tf_op jit(solution)/shard_map/ppermute | solution.py:324
  39.2 33.0 %copy-start.4 = (bf16[128,1024]{1,0:T(8,128)(2,1)}, bf16[128,1024]{1,0:T(8,128)(2,1)S(1)}, u32[]{:S(2)}) copy-start(bf16[128,1024]{1,0:T(8,128)(2,1)S(1)} %pad_maximum_fusion.refs_0_) | copy-start | bytes 786436
  39.2 8.6 %collective-permute-start.1 = (bf16[128,1024]{1,0:T(8,128)(2,1)S(1)}, bf16[128,1024]{1,0:T(8,128)(2,1)S(1)}, u32[]{:S(2)}, u32[]{:S(2)}) collective-permute-start(bf16[128,1024]{1,0:T(8,128)(2,1)S(1)} %pad_maximum_fusion.refs_0_), channel_id=1, source_target_pairs={{0,2},{2,4},{4,6},{6,8},{8,10},{10,12},{12,14},{14,0},{1,3},{3,5},... | collective-permute-start | bytes 786440 | tf_op jit(solution)/shard_map/ppermute | solution.py:331
  41.8 7.9 %collective-permute-start.5 = (bf16[128,1024]{1,0:T(8,128)(2,1)S(1)}, bf16[128,1024]{1,0:T(8,128)(2,1)S(1)}, u32[]{:S(2)}, u32[]{:S(2)}) collective-permute-start(bf16[128,1024]{1,0:T(8,128)(2,1)S(1)} %pad_maximum_fusion.refs_0_), channel_id=1, source_target_pairs={{0,14},{2,0},{4,2},{6,4},{8,6},{10,8},{12,10},{14,12},{1,15},{3,1}... | collective-permute-start | bytes 786440 | tf_op jit(solution)/shard_map/ppermute | solution.py:332
  47.8 10.6 %copy-start.7 = (bf16[128,1024]{1,0:T(8,128)(2,1)}, bf16[128,1024]{1,0:T(8,128)(2,1)S(1)}, u32[]{:S(2)}) copy-start(bf16[128,1024]{1,0:T(8,128)(2,1)S(1)} %collective-permute-done.1.refs_1_) | copy-start | bytes 786436
  47.8 8.6 %collective-permute-start.2 = (bf16[128,1024]{1,0:T(8,128)(2,1)S(1)}, bf16[128,1024]{1,0:T(8,128)(2,1)S(1)}, u32[]{:S(2)}, u32[]{:S(2)}) collective-permute-start(bf16[128,1024]{1,0:T(8,128)(2,1)S(1)} %collective-permute-done.1.refs_1_), channel_id=1, source_target_pairs={{0,2},{2,4},{4,6},{6,8},{8,10},{10,12},{12,14},{14,0},{1,3},{3,5},... | collective-permute-start | bytes 786440 | tf_op jit(solution)/shard_map/ppermute | solution.py:331
  49.7 8.6 %copy-start.8 = (bf16[128,1024]{1,0:T(8,128)(2,1)}, bf16[128,1024]{1,0:T(8,128)(2,1)S(1)}, u32[]{:S(2)}) copy-start(bf16[128,1024]{1,0:T(8,128)(2,1)S(1)} %collective-permute-done.5.refs_2_) | copy-start | bytes 786436
  49.8 8.6 %collective-permute-start.6 = (bf16[128,1024]{1,0:T(8,128)(2,1)S(1)}, bf16[128,1024]{1,0:T(8,128)(2,1)S(1)}, u32[]{:S(2)}, u32[]{:S(2)}) collective-permute-start(bf16[128,1024]{1,0:T(8,128)(2,1)S(1)} %collective-permute-done.5.refs_2_), channel_id=1, source_target_pairs={{0,14},{2,0},{4,2},{6,4},{8,6},{10,8},{12,10},{14,12},{1,15},{3,1}... | collective-permute-start | bytes 786440 | tf_op jit(solution)/shard_map/ppermute | solution.py:332
  56.4 15.8 %copy-start.9 = (bf16[128,1024]{1,0:T(8,128)(2,1)}, bf16[128,1024]{1,0:T(8,128)(2,1)S(1)}, u32[]{:S(2)}) copy-start(bf16[128,1024]{1,0:T(8,128)(2,1)S(1)} %collective-permute-done.2.refs_3_) | copy-start | bytes 786436
  56.4 8.3 %collective-permute-start.3 = (bf16[128,1024]{1,0:T(8,128)(2,1)S(1)}, bf16[128,1024]{1,0:T(8,128)(2,1)S(1)}, u32[]{:S(2)}, u32[]{:S(2)}) collective-permute-start(bf16[128,1024]{1,0:T(8,128)(2,1)S(1)} %collective-permute-done.2.refs_3_), channel_id=1, source_target_pairs={{0,2},{2,4},{4,6},{6,8},{8,10},{10,12},{12,14},{14,0},{1,3},{3,5},... | collective-permute-start | bytes 786440 | tf_op jit(solution)/shard_map/ppermute | solution.py:331
  58.4 13.8 %copy-start.10 = (bf16[128,1024]{1,0:T(8,128)(2,1)}, bf16[128,1024]{1,0:T(8,128)(2,1)S(1)}, u32[]{:S(2)}) copy-start(bf16[128,1024]{1,0:T(8,128)(2,1)S(1)} %collective-permute-done.6.refs_4_) | copy-start | bytes 786436
  58.4 8.3 %collective-permute-start.7 = (bf16[128,1024]{1,0:T(8,128)(2,1)S(1)}, bf16[128,1024]{1,0:T(8,128)(2,1)S(1)}, u32[]{:S(2)}, u32[]{:S(2)}) collective-permute-start(bf16[128,1024]{1,0:T(8,128)(2,1)S(1)} %collective-permute-done.6.refs_4_), channel_id=1, source_target_pairs={{0,14},{2,0},{4,2},{6,4},{8,6},{10,8},{12,10},{14,12},{1,15},{3,1}... | collective-permute-start | bytes 786440 | tf_op jit(solution)/shard_map/ppermute | solution.py:332
  64.7 7.4 %copy-start.5 = (bf16[128,1024]{1,0:T(8,128)(2,1)}, bf16[128,1024]{1,0:T(8,128)(2,1)S(1)}, u32[]{:S(2)}) copy-start(bf16[128,1024]{1,0:T(8,128)(2,1)S(1)} %collective-permute-done.3.refs_5_) | copy-start | bytes 786436
  64.8 7.4 %collective-permute-start.4 = (bf16[64,1024]{1,0:T(8,128)(2,1)S(1)}, bf16[64,1024]{1,0:T(8,128)(2,1)S(1)}, u32[]{:S(2)}, u32[]{:S(2)}) collective-permute-start(bf16[64,1024]{1,0:T(8,128)(2,1)S(1)} %slice.18), channel_id=1, source_target_pairs={{0,2},{2,4},{4,6},{6,8},{8,10},{10,12},{12,14},{14,0},{1,3},{3,5},... | collective-permute-start | bytes 393224 | tf_op jit(solution)/shard_map/ppermute | solution.py:334
  66.7 5.5 %copy-start.6 = (bf16[128,1024]{1,0:T(8,128)(2,1)}, bf16[128,1024]{1,0:T(8,128)(2,1)S(1)}, u32[]{:S(2)}) copy-start(bf16[128,1024]{1,0:T(8,128)(2,1)S(1)} %collective-permute-done.7.refs_6_) | copy-start | bytes 786436
  66.7 22.3 %copy-start.3 = (s32[1024]{0:T(1024)S(1)}, s32[1024]{0:T(1024)}, u32[]{:S(2)}) copy-start(s32[1024]{0:T(1024)} %param.6) | copy-start | bytes 12292
  66.7 7.2 %collective-permute-start.8 = (bf16[64,1024]{1,0:T(8,128)(2,1)S(1)}, bf16[64,1024]{1,0:T(8,128)(2,1)S(1)}, u32[]{:S(2)}, u32[]{:S(2)}) collective-permute-start(bf16[64,1024]{1,0:T(8,128)(2,1)S(1)} %slice.19), channel_id=1, source_target_pairs={{0,14},{2,0},{4,2},{6,4},{8,6},{10,8},{12,10},{14,12},{1,15},{3,1}... | collective-permute-start | bytes 393224 | tf_op jit(solution)/shard_map/ppermute | solution.py:334
  76.7 12.2 %collective-permute-start.9 = (f32[264,1024]{1,0:T(8,128)S(1)}, f32[264,1024]{1,0:T(8,128)}, u32[]{:S(2)}, u32[]{:S(2)}) collective-permute-start(f32[264,1024]{1,0:T(8,128)S(1)} %get-tuple-element.29.sent_ref), channel_id=1, source_target_pairs={{0,1},{1,0},{2,3},{3,2},{4,5},{5,4},{6,7},{7,6},{8,9},{9,8},{10,11... | collective-permute-start | bytes 3244040 | tf_op jit(solution)/shard_map/ppermute | solution.py:354
  89.0 22.8 %copy-start = (f32[256,256]{1,0:T(8,128)S(1)}, f32[256,256]{1,0:T(8,128)}, u32[]{:S(2)}) copy-start(f32[256,256]{1,0:T(8,128)} %pre_ref.3) | copy-start | bytes 786436
  157.7 17.0 %all-to-all-start.6 = ((f32[96,4,128]{2,1,0:T(4,128)}), f32[96,4,128]{2,1,0:T(4,128)S(1)}, u32[]{:S(2)}, u32[]{:S(2)}) async-start(f32[96,4,128]{2,1,0:T(4,128)} %get-tuple-element.39), calls=%async_computation.6 | async-start | bytes 393216 | tf_op jit(solution)/shard_map/all_to_all | solution.py:373

commit v4 on v3

--- a/solution.py
+++ b/solution.py
@@ -24,7 +24,7 @@
 WIDTH = N_PLANE * SLICE
 F = 2048
 N_Y = 8
-OFFSETS = (0, -1, 1, -2, 2, -3, 3, 4)
+OFFSETS = (0, 4, -1, 1, -2, 2, -3, 3)
 EXAMPLES = ROWS * N_EX
 
 EX = ("z", "xh")
@@ -114,20 +114,17 @@
     return jnp.dot(block, ft, preferred_element_type=F32), squares
 
 
-def dots_kernel(near_ref, far_ref, cen_ref, *refs):
+def dots_kernel(cen_ref, *refs):
     *chunk_hbm, out_ref, dots_ref, squares_ref, ft_ref, sems = refs
     copies = []
     for i, chunk in enumerate(chunk_hbm):
         copies.append(pltpu.make_async_copy(chunk, ft_ref.at[128 * i : 128 * i + 128], sems.at[i]))
         copies[-1].start()
-    first = 128 * len(chunk_hbm)
-    ft_ref[first : first + SLICE] = near_ref[...]
-    ft_ref[first + SLICE : first + 2 * SLICE] = far_ref[...]
 
     def squares(start):
         return jnp.sum(jnp.square(ft_ref[start : start + 128].astype(F32)), axis=0, keepdims=True)
 
-    row_sq = squares(first)
+    row_sq = jnp.zeros((1, ROWS), F32)
     for i, copy in enumerate(copies):
         copy.wait()
         row_sq += squares(128 * i)
@@ -331,7 +328,7 @@
         below = lax.ppermute(below, "y", up)
         above = lax.ppermute(above, "y", down)
         chunks += [below, above]
-    chunks += [lax.ppermute(below[:SLICE], "y", up), lax.ppermute(above[SLICE:], "y", down)]
+    chunks.insert(1, lax.ppermute(here, "y", [(i, (i + N_Y // 2) % N_Y) for i in range(N_Y)]))
 
     pair = local.reshape(N_PLANE, 2, OWN)
     own_col = jnp.where(core == 0, pair[:, 0], pair[:, 1]).reshape(N_PLANE * OWN, 1)
@@ -347,9 +344,8 @@
 
     dots_t = ((BLOCK, ROWS), F32)
     sent, own, own_sq = call(
-        dots_kernel, [((BLOCK + 8, ROWS), F32), dots_t, ((8, BLOCK), F32)], *chunks[-2:], cen, *chunks[:-2],
-        hbm=len(chunks) - 2,
-        scratch=[pltpu.VMEM((WIDTH, ROWS), BF16), pltpu.SemaphoreType.DMA((len(chunks) - 2,))],
+        dots_kernel, [((BLOCK + 8, ROWS), F32), dots_t, ((8, BLOCK), F32)], cen, *chunks, hbm=len(chunks),
+        scratch=[pltpu.VMEM((WIDTH, ROWS), BF16), pltpu.SemaphoreType.DMA((len(chunks),))],
     )
     got = lax.ppermute(sent, "c", [(0, 1), (1, 0)])
     half_t = ((BLOCK, ROWS), BF16)

time: 202 us -> 206 us (1.020)
  waiting for transfers between devices: 32 us -> 36.1 us
    ppermute x3, waiting for transfers between devices: 5.98 us -> 9.69 us  [predict(): below = lax.ppermute(below, 'y', up)]
    ppermute x2 -> x1, starting transfers between devices: 6.63 us -> 3.06 us  [predict(): lax.ppermute(here, 'y', [(i, (i + N_Y // 2) % N_Y) for i in range(N_Y)])]
    ppermute x3, waiting for transfers between devices: 0.01 us -> 2.42 us  [predict(): above = lax.ppermute(above, 'y', down)]
  transfers between devices with their start and end apart: 13 -> 12, of which waited for: 9 -> 8; matrix products, arithmetic and copies ran while one was open for 0% -> 0% of each run, Pallas kernels for 0% -> 0%
where the time goes in v4:
time: 206 us; the launch traced here: 204 us
  blocking collectives  88.2 us (43%)
  starting transfers between devices  63.7 us (31%)
  waiting for transfers between devices  36.1 us (18%)
  Pallas kernels  12.2 us (6%)
  local copies, waits for them, and re-layouts  3.38 us (2%)
    all_to_all x3, blocking collectives, predict(): part = lax.all_to_all(part, EX, 0, 0, tiled=True)  45.1 us
    all_to_all x3, blocking collectives, predict(): part = lax.all_to_all(part, FEAT, 0, 0, tiled=True)  43.2 us
    ppermute x3, starting transfers between devices, predict(): above = lax.ppermute(above, 'y', down)  14 us
    all_to_all x1, starting transfers between devices, predict(): cen = lax.all_to_all(spread, EX, 0, 0, tiled=True)  12.4 us
    pallas_call x11, Pallas kernels, call(): pl.pallas_call(kernel, out_shape=[space(s, d) for s, d in outs] if many e...  12.2 us
    all_to_all x1, waiting for transfers between devices, predict(): part = lax.all_to_all(part, FEAT, 0, 0, tiled=True)  10.2 us
    ppermute x1, starting transfers between devices, predict(): got = lax.ppermute(sent, 'c', [(0, 1), (1, 0)])  10.2 us
    ppermute x3, waiting for transfers between devices, predict(): below = lax.ppermute(below, 'y', up)  9.69 us
  transfers between devices with their start and end apart: 12, of which 8 were waited for; matrix products, arithmetic and copies ran while one was open for 0% of the time, Pallas kernels for 0%

profile of v4, /device:TPU:1, one launch (start us, length us, event | category | flops | bytes accessed | tf_op | source)
XLA Modules:
  0.0 204.1 jit_solution(17354637888669743427)
XLA Ops:
  3.1 8.7 %all-to-all-start = ((bf16[16,16,128]{2,1,0:T(8,128)(2,1)}), bf16[16,16,128]{2,1,0:T(8,128)(2,1)S(1)}, u32[]{:S(2)}, u32[]{:S(2)}) async-start(bf16[16,16,128]{2,1,0:T(8,128)(2,1)} %shard_map.46), calls=%async_computation | async-start | bytes 131072 | tf_op jit(solution)/shard_map/all_to_all | solution.py:337
  11.8 7.3 %all-to-all-done.in_ref = bf16[16,16,128]{2,1,0:T(8,128)(2,1)S(1)} async-done(((bf16[16,16,128]{2,1,0:T(8,128)(2,1)}), bf16[16,16,128]{2,1,0:T(8,128)(2,1)S(1)}, u32[]{:S(2)}, u32[]{:S(2)}) %all-to-all-start) | async-done | bytes 65568 | tf_op jit(solution)/shard_map/all_to_all | solution.py:337
  21.0 12.4 %all-to-all-start.1 = ((bf16[16,32,1024]{2,1,0:T(8,128)(2,1)}), bf16[16,32,1024]{2,1,0:T(8,128)(2,1)S(1)}, u32[]{:S(2)}, u32[]{:S(2)}) async-start(bf16[16,32,1024]{2,1,0:T(8,128)(2,1)} %shard_map.47), calls=%async_computation.1 | async-start | bytes 2097152 | tf_op jit(solution)/shard_map/all_to_all | solution.py:339
  35.4 3.8 %collective-permute-done = bf16[64,1024]{1,0:T(8,128)(2,1)S(1)} collective-permute-done((bf16[64,1024]{1,0:T(8,128)(2,1)S(1)}, bf16[64,1024]{1,0:T(8,128)(2,1)S(1)}, u32[]{:S(2)}, u32[]{:S(2)}) %collective-permute-start) | collective-permute-done | bytes 131104 | tf_op jit(solution)/shard_map/ppermute | solution.py:321
  39.2 2.8 %collective-permute-start.2 = (bf16[128,1024]{1,0:T(8,128)(2,1)S(1)}, bf16[128,1024]{1,0:T(8,128)(2,1)S(1)}, u32[]{:S(2)}, u32[]{:S(2)}) collective-permute-start(bf16[128,1024]{1,0:T(8,128)(2,1)S(1)} %pad_maximum_fusion.refs_0_), channel_id=1, source_target_pairs={{0,2},{2,4},{4,6},{6,8},{8,10},{10,12},{12,14},{14,0},{1,3},{3,5},... | collective-permute-start | bytes 786440 | tf_op jit(solution)/shard_map/ppermute | solution.py:328
  42.0 3.9 %collective-permute-start.3 = (bf16[128,1024]{1,0:T(8,128)(2,1)S(1)}, bf16[128,1024]{1,0:T(8,128)(2,1)S(1)}, u32[]{:S(2)}, u32[]{:S(2)}) collective-permute-start(bf16[128,1024]{1,0:T(8,128)(2,1)S(1)} %pad_maximum_fusion.refs_0_), channel_id=1, source_target_pairs={{0,14},{2,0},{4,2},{6,4},{8,6},{10,8},{12,10},{14,12},{1,15},{3,1}... | collective-permute-start | bytes 786440 | tf_op jit(solution)/shard_map/ppermute | solution.py:329
  45.8 2.1 %collective-permute-done.2.refs_2_ = bf16[128,1024]{1,0:T(8,128)(2,1)S(1)} collective-permute-done((bf16[128,1024]{1,0:T(8,128)(2,1)S(1)}, bf16[128,1024]{1,0:T(8,128)(2,1)S(1)}, u32[]{:S(2)}, u32[]{:S(2)}) %collective-permute-start.2) | collective-permute-done | bytes 262176 | tf_op jit(solution)/shard_map/ppermute | solution.py:328
  49.9 4.6 %collective-permute-start.5 = (bf16[128,1024]{1,0:T(8,128)(2,1)S(1)}, bf16[128,1024]{1,0:T(8,128)(2,1)S(1)}, u32[]{:S(2)}, u32[]{:S(2)}) collective-permute-start(bf16[128,1024]{1,0:T(8,128)(2,1)S(1)} %collective-permute-done.3.refs_3_), channel_id=1, source_target_pairs={{0,14},{2,0},{4,2},{6,4},{8,6},{10,8},{12,10},{14,12},{1,15},{3,1}... | collective-permute-start | bytes 786440 | tf_op jit(solution)/shard_map/ppermute | solution.py:329
  54.5 3.1 %collective-permute-start.1 = (bf16[128,1024]{1,0:T(8,128)(2,1)S(1)}, bf16[128,1024]{1,0:T(8,128)(2,1)S(1)}, u32[]{:S(2)}, u32[]{:S(2)}) collective-permute-start(bf16[128,1024]{1,0:T(8,128)(2,1)S(1)} %pad_maximum_fusion.refs_0_), channel_id=1, source_target_pairs={{0,8},{2,10},{4,12},{6,14},{8,0},{10,2},{12,4},{14,6},{1,9},{3,11}... | collective-permute-start | bytes 786440 | tf_op jit(solution)/shard_map/ppermute | solution.py:331
  59.5 2.4 %collective-permute-done.5.refs_5_ = bf16[128,1024]{1,0:T(8,128)(2,1)S(1)} collective-permute-done((bf16[128,1024]{1,0:T(8,128)(2,1)S(1)}, bf16[128,1024]{1,0:T(8,128)(2,1)S(1)}, u32[]{:S(2)}, u32[]{:S(2)}) %collective-permute-start.5) | collective-permute-done | bytes 262176 | tf_op jit(solution)/shard_map/ppermute | solution.py:329
  61.9 5.5 %collective-permute-start.7 = (bf16[128,1024]{1,0:T(8,128)(2,1)S(1)}, bf16[128,1024]{1,0:T(8,128)(2,1)S(1)}, u32[]{:S(2)}, u32[]{:S(2)}) collective-permute-start(bf16[128,1024]{1,0:T(8,128)(2,1)S(1)} %collective-permute-done.5.refs_5_), channel_id=1, source_target_pairs={{0,14},{2,0},{4,2},{6,4},{8,6},{10,8},{12,10},{14,12},{1,15},{3,1}... | collective-permute-start | bytes 786440 | tf_op jit(solution)/shard_map/ppermute | solution.py:329
  67.9 7.6 %collective-permute-done.6.refs_6_ = bf16[128,1024]{1,0:T(8,128)(2,1)S(1)} collective-permute-done((bf16[128,1024]{1,0:T(8,128)(2,1)S(1)}, bf16[128,1024]{1,0:T(8,128)(2,1)S(1)}, u32[]{:S(2)}, u32[]{:S(2)}) %collective-permute-start.6) | collective-permute-done | bytes 262176 | tf_op jit(solution)/shard_map/ppermute | solution.py:328
  76.9 2.8 %shard_map.48 = (f32[264,1024]{1,0:T(8,128)S(1)}, f32[256,1024]{1,0:T(8,128)S(1)}, f32[8,256]{1,0:T(8,128)S(1)}) custom-call(bf16[16,32,1024]{2,1,0:T(8,128)(2,1)S(1)} %all-to-all-done.1.cen_ref, bf16[128,1024]{1,0:T(8,128)(2,1)} %copy-done.4, bf16[128,1024]{1,0:T(8,128)(2,1)} %copy-done.9, bf16[128,1024]{1,0:T(8,128)(2,1)} %copy-done.5, ...), custom_call_target="tpu_custom_call" | custom-call | tf_op jit(solution)/shard_map/pallas_call | solution.py:66
  79.7 10.2 %collective-permute-start.8 = (f32[264,1024]{1,0:T(8,128)S(1)}, f32[264,1024]{1,0:T(8,128)}, u32[]{:S(2)}, u32[]{:S(2)}) collective-permute-start(f32[264,1024]{1,0:T(8,128)S(1)} %get-tuple-element.29.sent_ref), channel_id=1, source_target_pairs={{0,1},{1,0},{2,3},{3,2},{4,5},{5,4},{6,7},{7,6},{8,9},{9,8},{10,11... | collective-permute-start | bytes 3244040 | tf_op jit(solution)/shard_map/ppermute | solution.py:350
  90.2 2.2 %collective-permute-done.8.recv_hbm = f32[264,1024]{1,0:T(8,128)} collective-permute-done((f32[264,1024]{1,0:T(8,128)S(1)}, f32[264,1024]{1,0:T(8,128)}, u32[]{:S(2)}, u32[]{:S(2)}) %collective-permute-start.8) | collective-permute-done | bytes 1081376 | tf_op jit(solution)/shard_map/ppermute | solution.py:350
  92.4 1.9 shard_map.49
  94.3 19.4 %all_to_all.45.recv_ref = f32[16,16,256]{2,1,0:T(8,128)S(1)} all-to-all(f32[16,16,256]{2,1,0:T(8,128)S(1)} %get-tuple-element.30), channel_id=1, replica_groups=mesh['z'=8,'xh'=2,'xl'=2,'y'=8,'c'=2] {'z','xh'}, dimensions={0} | all-to-all | bytes 524288 | tf_op jit(solution)/shard_map/all_to_all | solution.py:358
  114.8 17.1 %all_to_all.46.recv_ref = f32[64,4,128]{2,1,0:T(4,128)S(1)} all-to-all(f32[64,4,128]{2,1,0:T(4,128)S(1)} %get-tuple-element.34), channel_id=1, replica_groups=mesh['z'=8,'xh'=2,'xl'=2,'y'=8,'c'=2] {'xl','y','c'}, dimensions={0} | all-to-all | bytes 262144 | tf_op jit(solution)/shard_map/all_to_all | solution.py:360
  131.9 12.5 %all_to_all.47.recv_ref = f32[32,4,128]{2,1,0:T(4,128)S(1)} all-to-all(f32[32,4,128]{2,1,0:T(4,128)S(1)} %get-tuple-element.35), channel_id=1, replica_groups=mesh['z'=8,'xh'=2,'xl'=2,'y'=8,'c'=2] {'xl','y','c'}, dimensions={0} | all-to-all | bytes 131072 | tf_op jit(solution)/shard_map/all_to_all | solution.py:362
  145.0 14.2 %all_to_all.48.recv_ref = f32[16,16,256]{2,1,0:T(8,128)S(1)} all-to-all(f32[16,16,256]{2,1,0:T(8,128)S(1)} %get-tuple-element.36), channel_id=1, replica_groups=mesh['z'=8,'xh'=2,'xl'=2,'y'=8,'c'=2] {'z','xh'}, dimensions={0} | all-to-all | bytes 524288 | tf_op jit(solution)/shard_map/all_to_all | solution.py:364
  161.0 6.8 %all-to-all-start.6 = ((f32[96,4,128]{2,1,0:T(4,128)}), f32[96,4,128]{2,1,0:T(4,128)S(1)}, u32[]{:S(2)}, u32[]{:S(2)}) async-start(f32[96,4,128]{2,1,0:T(4,128)} %get-tuple-element.39), calls=%async_computation.6 | async-start | bytes 393216 | tf_op jit(solution)/shard_map/all_to_all | solution.py:369
  167.8 10.2 %all-to-all-done.6.recv_ref = f32[96,4,128]{2,1,0:T(4,128)S(1)} async-done(((f32[96,4,128]{2,1,0:T(4,128)}), f32[96,4,128]{2,1,0:T(4,128)S(1)}, u32[]{:S(2)}, u32[]{:S(2)}) %all-to-all-start.6) | async-done | bytes 196640 | tf_op jit(solution)/shard_map/all_to_all | solution.py:369
  178.3 13.6 %all_to_all.49.recv_ref = f32[64,4,128]{2,1,0:T(4,128)S(1)} all-to-all(f32[64,4,128]{2,1,0:T(4,128)S(1)} %get-tuple-element.43), channel_id=1, replica_groups=mesh['z'=8,'xh'=2,'xl'=2,'y'=8,'c'=2] {'xl','y','c'}, dimensions={0} | all-to-all | bytes 262144 | tf_op jit(solution)/shard_map/all_to_all | solution.py:375
  192.0 11.4 %all_to_all.50.recv_ref = f32[16,1,128]{2,1,0:T(1,128)S(1)} all-to-all(f32[16,1,128]{2,1,0:T(1,128)S(1)} %get-tuple-element.44), channel_id=1, replica_groups=mesh['z'=8,'xh'=2,'xl'=2,'y'=8,'c'=2] {'z','xh'}, dimensions={0} | all-to-all | bytes 16384 | tf_op jit(solution)/shard_map/all_to_all | solution.py:377
  (52 shorter events, 17.3 us)
Async XLA Ops:
  1.0 0.9 copy-start.1
  3.1 16.1 %all-to-all-start = ((bf16[16,16,128]{2,1,0:T(8,128)(2,1)}), bf16[16,16,128]{2,1,0:T(8,128)(2,1)S(1)}, u32[]{:S(2)}, u32[]{:S(2)}) async-start(bf16[16,16,128]{2,1,0:T(8,128)(2,1)} %shard_map.46), calls=%async_computation | async-start | bytes 131072 | tf_op jit(solution)/shard_map/all_to_all | solution.py:337
  21.0 12.4 %copy-start.2 = (bf16[1024,64]{0,1:T(8,128)(2,1)S(1)}, bf16[1024,64]{0,1:T(8,128)(2,1)}, u32[]{:S(2)}) copy-start(bf16[1024,64]{0,1:T(8,128)(2,1)} %param.4) | copy-start | bytes 393220
  21.0 55.9 %all-to-all-start.1 = ((bf16[16,32,1024]{2,1,0:T(8,128)(2,1)}), bf16[16,32,1024]{2,1,0:T(8,128)(2,1)S(1)}, u32[]{:S(2)}, u32[]{:S(2)}) async-start(bf16[16,32,1024]{2,1,0:T(8,128)(2,1)} %shard_map.47), calls=%async_computation.1 | async-start | bytes 2097152 | tf_op jit(solution)/shard_map/all_to_all | solution.py:339
  33.4 5.7 %collective-permute-start = (bf16[64,1024]{1,0:T(8,128)(2,1)S(1)}, bf16[64,1024]{1,0:T(8,128)(2,1)S(1)}, u32[]{:S(2)}, u32[]{:S(2)}) collective-permute-start(bf16[64,1024]{1,0:T(8,128)(2,1)S(1)} %bitcast.10), channel_id=1, source_target_pairs={{0,16},{16,0},{1,17},{17,1},{2,18},{18,2},{3,19},{19,3},{4,20},{20... | collective-permute-start | bytes 393224 | tf_op jit(solution)/shard_map/ppermute | solution.py:321
  39.2 37.7 %copy-start.4 = (bf16[128,1024]{1,0:T(8,128)(2,1)}, bf16[128,1024]{1,0:T(8,128)(2,1)S(1)}, u32[]{:S(2)}) copy-start(bf16[128,1024]{1,0:T(8,128)(2,1)S(1)} %pad_maximum_fusion.refs_0_) | copy-start | bytes 786436
  39.2 53.2 %copy-start.3 = (s32[1024]{0:T(1024)S(1)}, s32[1024]{0:T(1024)}, u32[]{:S(2)}) copy-start(s32[1024]{0:T(1024)} %param.6) | copy-start | bytes 12292
  39.2 8.8 %collective-permute-start.2 = (bf16[128,1024]{1,0:T(8,128)(2,1)S(1)}, bf16[128,1024]{1,0:T(8,128)(2,1)S(1)}, u32[]{:S(2)}, u32[]{:S(2)}) collective-permute-start(bf16[128,1024]{1,0:T(8,128)(2,1)S(1)} %pad_maximum_fusion.refs_0_), channel_id=1, source_target_pairs={{0,2},{2,4},{4,6},{6,8},{8,10},{10,12},{12,14},{14,0},{1,3},{3,5},... | collective-permute-start | bytes 786440 | tf_op jit(solution)/shard_map/ppermute | solution.py:328
  42.0 7.9 %collective-permute-start.3 = (bf16[128,1024]{1,0:T(8,128)(2,1)S(1)}, bf16[128,1024]{1,0:T(8,128)(2,1)S(1)}, u32[]{:S(2)}, u32[]{:S(2)}) collective-permute-start(bf16[128,1024]{1,0:T(8,128)(2,1)S(1)} %pad_maximum_fusion.refs_0_), channel_id=1, source_target_pairs={{0,14},{2,0},{4,2},{6,4},{8,6},{10,8},{12,10},{14,12},{1,15},{3,1}... | collective-permute-start | bytes 786440 | tf_op jit(solution)/shard_map/ppermute | solution.py:329
  48.0 27.5 %copy-start.5 = (bf16[128,1024]{1,0:T(8,128)(2,1)}, bf16[128,1024]{1,0:T(8,128)(2,1)S(1)}, u32[]{:S(2)}) copy-start(bf16[128,1024]{1,0:T(8,128)(2,1)S(1)} %collective-permute-done.2.refs_2_) | copy-start | bytes 786436
  48.0 9.6 %collective-permute-start.4 = (bf16[128,1024]{1,0:T(8,128)(2,1)S(1)}, bf16[128,1024]{1,0:T(8,128)(2,1)S(1)}, u32[]{:S(2)}, u32[]{:S(2)}) collective-permute-start(bf16[128,1024]{1,0:T(8,128)(2,1)S(1)} %collective-permute-done.2.refs_2_), channel_id=1, source_target_pairs={{0,2},{2,4},{4,6},{6,8},{8,10},{10,12},{12,14},{14,0},{1,3},{3,5},... | collective-permute-start | bytes 786440 | tf_op jit(solution)/shard_map/ppermute | solution.py:328
  49.9 25.6 %copy-start.6 = (bf16[128,1024]{1,0:T(8,128)(2,1)}, bf16[128,1024]{1,0:T(8,128)(2,1)S(1)}, u32[]{:S(2)}) copy-start(bf16[128,1024]{1,0:T(8,128)(2,1)S(1)} %collective-permute-done.3.refs_3_) | copy-start | bytes 786436
  49.9 12.0 %collective-permute-start.5 = (bf16[128,1024]{1,0:T(8,128)(2,1)S(1)}, bf16[128,1024]{1,0:T(8,128)(2,1)S(1)}, u32[]{:S(2)}, u32[]{:S(2)}) collective-permute-start(bf16[128,1024]{1,0:T(8,128)(2,1)S(1)} %collective-permute-done.3.refs_3_), channel_id=1, source_target_pairs={{0,14},{2,0},{4,2},{6,4},{8,6},{10,8},{12,10},{14,12},{1,15},{3,1}... | collective-permute-start | bytes 786440 | tf_op jit(solution)/shard_map/ppermute | solution.py:329
  54.5 13.4 %collective-permute-start.1 = (bf16[128,1024]{1,0:T(8,128)(2,1)S(1)}, bf16[128,1024]{1,0:T(8,128)(2,1)S(1)}, u32[]{:S(2)}, u32[]{:S(2)}) collective-permute-start(bf16[128,1024]{1,0:T(8,128)(2,1)S(1)} %pad_maximum_fusion.refs_0_), channel_id=1, source_target_pairs={{0,8},{2,10},{4,12},{6,14},{8,0},{10,2},{12,4},{14,6},{1,9},{3,11}... | collective-permute-start | bytes 786440 | tf_op jit(solution)/shard_map/ppermute | solution.py:331
  57.6 17.9 %copy-start.7 = (bf16[128,1024]{1,0:T(8,128)(2,1)}, bf16[128,1024]{1,0:T(8,128)(2,1)S(1)}, u32[]{:S(2)}) copy-start(bf16[128,1024]{1,0:T(8,128)(2,1)S(1)} %collective-permute-done.4.refs_4_) | copy-start | bytes 786436
  57.6 17.9 %collective-permute-start.6 = (bf16[128,1024]{1,0:T(8,128)(2,1)S(1)}, bf16[128,1024]{1,0:T(8,128)(2,1)S(1)}, u32[]{:S(2)}, u32[]{:S(2)}) collective-permute-start(bf16[128,1024]{1,0:T(8,128)(2,1)S(1)} %collective-permute-done.4.refs_4_), channel_id=1, source_target_pairs={{0,2},{2,4},{4,6},{6,8},{8,10},{10,12},{12,14},{14,0},{1,3},{3,5},... | collective-permute-start | bytes 786440 | tf_op jit(solution)/shard_map/ppermute | solution.py:328
  61.9 13.6 %copy-start.8 = (bf16[128,1024]{1,0:T(8,128)(2,1)}, bf16[128,1024]{1,0:T(8,128)(2,1)S(1)}, u32[]{:S(2)}) copy-start(bf16[128,1024]{1,0:T(8,128)(2,1)S(1)} %collective-permute-done.5.refs_5_) | copy-start | bytes 786436
  61.9 13.6 %collective-permute-start.7 = (bf16[128,1024]{1,0:T(8,128)(2,1)S(1)}, bf16[128,1024]{1,0:T(8,128)(2,1)S(1)}, u32[]{:S(2)}, u32[]{:S(2)}) collective-permute-start(bf16[128,1024]{1,0:T(8,128)(2,1)S(1)} %collective-permute-done.5.refs_5_), channel_id=1, source_target_pairs={{0,14},{2,0},{4,2},{6,4},{8,6},{10,8},{12,10},{14,12},{1,15},{3,1}... | collective-permute-start | bytes 786440 | tf_op jit(solution)/shard_map/ppermute | solution.py:329
  67.9 7.6 %copy-start.9 = (bf16[128,1024]{1,0:T(8,128)(2,1)}, bf16[128,1024]{1,0:T(8,128)(2,1)S(1)}, u32[]{:S(2)}) copy-start(bf16[128,1024]{1,0:T(8,128)(2,1)S(1)} %collective-permute-done.1.refs_1_) | copy-start | bytes 786436
  75.5 0.7 copy-start.10
  76.2 0.7 copy-start.11
  79.7 12.7 %collective-permute-start.8 = (f32[264,1024]{1,0:T(8,128)S(1)}, f32[264,1024]{1,0:T(8,128)}, u32[]{:S(2)}, u32[]{:S(2)}) collective-permute-start(f32[264,1024]{1,0:T(8,128)S(1)} %get-tuple-element.29.sent_ref), channel_id=1, source_target_pairs={{0,1},{1,0},{2,3},{3,2},{4,5},{5,4},{6,7},{7,6},{8,9},{9,8},{10,11... | collective-permute-start | bytes 3244040 | tf_op jit(solution)/shard_map/ppermute | solution.py:350
  92.4 21.4 %copy-start = (f32[256,256]{1,0:T(8,128)S(1)}, f32[256,256]{1,0:T(8,128)}, u32[]{:S(2)}) copy-start(f32[256,256]{1,0:T(8,128)} %pre_ref.3) | copy-start | bytes 786436
  161.0 17.0 %all-to-all-start.6 = ((f32[96,4,128]{2,1,0:T(4,128)}), f32[96,4,128]{2,1,0:T(4,128)S(1)}, u32[]{:S(2)}, u32[]{:S(2)}) async-start(f32[96,4,128]{2,1,0:T(4,128)} %get-tuple-element.39), calls=%async_computation.6 | async-start | bytes 393216 | tf_op jit(solution)/shard_map/all_to_all | solution.py:369

commit v5 on v3

--- a/solution.py
+++ b/solution.py
@@ -73,24 +73,34 @@
     )(*args)
 
 
-def pick_kernel(ft_ref, own_ref, other_ref, out_ref):
-    ft = ft_ref[...]
-    zero = jnp.zeros_like(ft)
-    n = N_PLANE * OWN
-    lane = iota((n, ROWS), 1)
-
-    def chosen(index_ref, table):
-        mask = (lane == index_ref[...]).astype(F32).astype(BF16)
-        return lax.dot_general(mask, table, LANES, preferred_element_type=F32)
-
-    both = chosen(own_ref, jnp.concatenate([ft, zero], axis=0))
-    both = both + chosen(other_ref, jnp.concatenate([zero, ft], axis=0))
+def pick_kernel(spot_ref, index_ref, ft_hbm, out_ref, both_ref, sem):
+    both_ref[...] = jnp.zeros_like(both_ref)
+    low = pltpu.make_async_copy(ft_hbm, both_ref.at[0:SLICE, 0:ROWS], sem.at[0])
+    high = pltpu.make_async_copy(ft_hbm, both_ref.at[SLICE : 2 * SLICE, ROWS : 2 * ROWS], sem.at[1])
+    low.start()
+    high.start()
+    core, base = spot_ref[3], spot_ref[4]
+    lane = iota((OWN, ROWS), 1)
+    index = index_ref[...]
+    blocks = iota((OWN, N_FEAT), 1)
+
+    def mask(block):
+        col = jnp.sum(jnp.where(blocks == block, index, 0), axis=1, keepdims=True) - base
+        return (lane == col).astype(F32).astype(BF16)
+
+    def masks(side):
+        return jnp.concatenate([mask(2 * p + side) for p in range(N_PLANE)], axis=0)
+
+    chosen = jnp.concatenate([masks(core), masks(1 - core)], axis=1)
+    low.wait()
+    high.wait()
+    both = lax.dot_general(chosen, both_ref[...], LANES, preferred_element_type=F32)
     out_ref[...] = both.astype(BF16).reshape(N_PLANE, OWN, 2 * SLICE)
 
 
-def spread_kernel(place_ref, in_ref, out_ref):
+def spread_kernel(spot_ref, in_ref, out_ref):
     low = iota((OWN, 128), 1) < SLICE
-    side, y = place_ref[0], place_ref[1]
+    side, y = spot_ref[0], spot_ref[1]
     for t, offset in enumerate(OFFSETS):
         row = lax.rem(y + (offset + N_Y), N_Y)
         a = in_ref[side * N_Y + row].astype(F32)
@@ -114,8 +124,7 @@
     return jnp.dot(block, ft, preferred_element_type=F32), squares
 
 
-def dots_kernel(near_ref, far_ref, cen_ref, *refs):
-    *chunk_hbm, out_ref, dots_ref, squares_ref, ft_ref, sems = refs
+def load_features(chunk_hbm, near_ref, far_ref, ft_ref, sems):
     copies = []
     for i, chunk in enumerate(chunk_hbm):
         copies.append(pltpu.make_async_copy(chunk, ft_ref.at[128 * i : 128 * i + 128], sems.at[i]))
@@ -123,21 +132,32 @@
     first = 128 * len(chunk_hbm)
     ft_ref[first : first + SLICE] = near_ref[...]
     ft_ref[first + SLICE : first + 2 * SLICE] = far_ref[...]
+    return copies
+
+
+def other_kernel(near_ref, far_ref, cen_ref, *refs):
+    *chunk_hbm, out_ref, ft_ref, sems = refs
+    copies = load_features(chunk_hbm, near_ref, far_ref, ft_ref, sems)
 
     def squares(start):
         return jnp.sum(jnp.square(ft_ref[start : start + 128].astype(F32)), axis=0, keepdims=True)
 
-    row_sq = squares(first)
+    row_sq = squares(128 * len(chunk_hbm))
     for i, copy in enumerate(copies):
         copy.wait()
         row_sq += squares(128 * i)
     out_ref[BLOCK : BLOCK + 8, :] = jnp.zeros((8, ROWS), F32)
     out_ref[BLOCK : BLOCK + 1, :] = row_sq
-    ft = ft_ref[...]
-    dots, squares = half_dots(ft, cen_ref, OWN)
+    dots, squares = half_dots(ft_ref[...], cen_ref, OWN)
     out_ref[0:BLOCK, :] = dots
     out_ref[BLOCK + 1 : BLOCK + 2, 0:BLOCK] = squares
-    dots, squares = half_dots(ft, cen_ref, 0)
+
+
+def own_kernel(near_ref, far_ref, cen_ref, *refs):
+    *chunk_hbm, dots_ref, squares_ref, ft_ref, sems = refs
+    for copy in load_features(chunk_hbm, near_ref, far_ref, ft_ref, sems):
+        copy.wait()
+    dots, squares = half_dots(ft_ref[...], cen_ref, 0)
     dots_ref[...] = dots
     squares_ref[...] = jnp.broadcast_to(squares, (8, BLOCK))
 
@@ -270,7 +290,7 @@
         out_ref[s * 3 + 2] = row
 
 
-def step_kernel(group_ref, recv_ref, chunk_ref, rhs_ref, u_ref, image_ref, v_ref, scal_ref, out_ref):
+def step_kernel(spot_ref, recv_ref, chunk_ref, rhs_ref, u_ref, image_ref, v_ref, scal_ref, out_ref):
     row = sum_slot(recv_ref, 3, 2)[0:1]
     scal_ref[...] = jnp.broadcast_to(row, (8, 128))
     alpha = to_col(row, CLASSES, 0) / to_col(row, CLASSES, CLASSES)
@@ -278,7 +298,7 @@
     z = u_ref[...] - alpha * v_ref[...]
     rz = to_row(jnp.sum(residual * z, axis=1, keepdims=True))
     alpha_row = to_row(alpha)
-    first = group_ref[0] * 4
+    first = spot_ref[2] * 4
     mine = iota((4, 128), 1) == iota((4, 128), 0) + first
     alpha_mine = jnp.sum(jnp.where(mine, alpha_row, 0.0), axis=1, keepdims=True)
     kz = chunk_ref[0] - alpha_mine * sum_slot(recv_ref, 3, 0)
@@ -333,12 +353,13 @@
         chunks += [below, above]
     chunks += [lax.ppermute(below[:SLICE], "y", up), lax.ppermute(above[SLICE:], "y", down)]
 
-    pair = local.reshape(N_PLANE, 2, OWN)
-    own_col = jnp.where(core == 0, pair[:, 0], pair[:, 1]).reshape(N_PLANE * OWN, 1)
-    other_col = jnp.where(core == 0, pair[:, 1], pair[:, 0]).reshape(N_PLANE * OWN, 1)
-    picked = call(pick_kernel, ((N_PLANE, OWN, 2 * SLICE), BF16), ft_local, own_col, other_col)
+    spot = jnp.stack([lax.axis_index("xl"), lax.axis_index("y"), feat_index // 8, core, ex_index * ROWS])
+    picked = call(
+        pick_kernel, ((N_PLANE, OWN, 2 * SLICE), BF16), spot, centre_index[:, 0, :].T, ft_local, smem=1, hbm=1,
+        scratch=[pltpu.VMEM((2 * SLICE, 2 * ROWS), BF16), pltpu.SemaphoreType.DMA((2,))],
+    )
     picked = lax.all_to_all(picked, PLANE, 0, 0, tiled=True)
-    spread = call(spread_kernel, ((N_EX, 2 * OWN, WIDTH), BF16), jnp.stack([lax.axis_index("xl"), lax.axis_index("y")]), picked, smem=1)
+    spread = call(spread_kernel, ((N_EX, 2 * OWN, WIDTH), BF16), spot, picked, smem=1)
     cen = lax.all_to_all(spread, EX, 0, 0, tiled=True)
 
     own_rows = lax.dynamic_index_in_dim(local, feat_index, 0, keepdims=False)
@@ -346,12 +367,12 @@
     loc = jnp.where(slot, own_rows[None, :], -1).reshape(BLOCK, 1)
 
     dots_t = ((BLOCK, ROWS), F32)
-    sent, own, own_sq = call(
-        dots_kernel, [((BLOCK + 8, ROWS), F32), dots_t, ((8, BLOCK), F32)], *chunks[-2:], cen, *chunks[:-2],
-        hbm=len(chunks) - 2,
-        scratch=[pltpu.VMEM((WIDTH, ROWS), BF16), pltpu.SemaphoreType.DMA((len(chunks) - 2,))],
-    )
+    operands = (*chunks[-2:], cen, *chunks[:-2])
+    still = len(chunks) - 2
+    scratch = [pltpu.VMEM((WIDTH, ROWS), BF16), pltpu.SemaphoreType.DMA((still,))]
+    sent = call(other_kernel, ((BLOCK + 8, ROWS), F32), *operands, hbm=still, scratch=scratch)
     got = lax.ppermute(sent, "c", [(0, 1), (1, 0)])
+    own, own_sq = call(own_kernel, [dots_t, ((8, BLOCK), F32)], *operands, hbm=still, scratch=scratch)
     half_t = ((BLOCK, ROWS), BF16)
     high, low, place, part = call(
         panel_kernel, [half_t, half_t, half_t, ((N_EX, CLASSES, BLOCK), F32)],
@@ -371,10 +392,9 @@
         part, precond, high, low, place, rhs, u,
     )
     part = lax.all_to_all(part, FEAT, 0, 0, tiled=True)
-    group = (feat_index // 8).reshape(1)
     scal, part = call(
         step_kernel, [((8, 128), F32), ((N_FEAT * 2, 4, 128), F32)],
-        group, part, chunk, rhs, u, image, v, smem=1,
+        spot, part, chunk, rhs, u, image, v, smem=1,
     )
     part = lax.all_to_all(part, FEAT, 0, 0, tiled=True)
     kz, tail, part = call(gather_kernel, [((CLASSES, ROWS), F32), ((4, 128), F32), ((N_EX, 1, 128), F32)], part)

time: 202 us -> 201 us (level)
  blocking collectives: 88.4 us -> 121 us
  waiting for transfers between devices: 32 us -> 12.3 us
  starting transfers between devices: 65.7 us -> 50.2 us
  Pallas kernels: 12.1 us -> 14.8 us
    all_to_all x2 -> x0, waiting for transfers between devices: 17.5 us -> none  [the longest x1 10.2 us: predict(): part = lax.all_to_all(part, FEAT, 0, 0, tiled=True)]
    all_to_all x3 -> x4, blocking collectives: 41.9 us -> 57.8 us  [predict(): part = lax.all_to_all(part, FEAT, 0, 0, tiled=True)]
    all_to_all x0 -> x1, blocking collectives: none -> 15.8 us  [predict(): picked = lax.all_to_all(picked, PLANE, 0, 0, tiled=True)]
    all_to_all x2 -> x0, starting transfers between devices: 15.5 us -> none  [the longest x1 8.67 us: predict(): picked = lax.all_to_all(picked, PLANE, 0, 0, tiled=True)]
    pallas_call x11 -> x12, Pallas kernels: 12.1 us -> 14.8 us  [call(): pl.pallas_call(kernel, out_shape=[space(s, d) for s, d in outs] if many e...]
    ppermute x1, waiting for transfers between devices: 2.22 us -> 0.01 us  [predict(): got = lax.ppermute(sent, 'c', [(0, 1), (1, 0)])]
  transfers between devices with their start and end apart: 13 -> 11, of which waited for: 9 -> 6; matrix products, arithmetic and copies ran while one was open for 0% -> 0% of each run, Pallas kernels for 0% -> 1%
where the time goes in v5:
time: 201 us; the launch traced here: 199 us
  blocking collectives  121 us (60%)
  starting transfers between devices  50.2 us (25%)
  Pallas kernels  14.8 us (7%)
  waiting for transfers between devices  12.3 us (6%)
    all_to_all x4, blocking collectives, predict(): part = lax.all_to_all(part, FEAT, 0, 0, tiled=True)  57.8 us
    all_to_all x3, blocking collectives, predict(): part = lax.all_to_all(part, EX, 0, 0, tiled=True)  46.9 us
    all_to_all x1, blocking collectives, predict(): picked = lax.all_to_all(picked, PLANE, 0, 0, tiled=True)  15.8 us
    pallas_call x12, Pallas kernels, call(): pl.pallas_call(kernel, out_shape=[space(s, d) for s, d in outs] if many e...  14.8 us
    ppermute x3, starting transfers between devices, predict(): above = lax.ppermute(above, 'y', down)  13 us
    all_to_all x1, starting transfers between devices, predict(): cen = lax.all_to_all(spread, EX, 0, 0, tiled=True)  12.4 us
    ppermute x1, starting transfers between devices, predict(): got = lax.ppermute(sent, 'c', [(0, 1), (1, 0)])  9.76 us
    ppermute x3, starting transfers between devices, predict(): below = lax.ppermute(below, 'y', up)  6.45 us
  transfers between devices with their start and end apart: 11, of which 6 were waited for; matrix products, arithmetic and copies ran while one was open for 0% of the time, Pallas kernels for 1%

profile of v5, /device:TPU:1, one launch (start us, length us, event | category | flops | bytes accessed | tf_op | source)
XLA Modules:
  0.0 199.3 jit_solution(11429271342728495088)
XLA Ops:
  0.8 2.2 %shard_map.46 = bf16[16,16,128]{2,1,0:T(8,128)(2,1)S(1)} custom-call(s32[5]{0:T(128)S(1)} %stack.23.spot_ref, s32[16,32]{1,0:T(8,128)S(1)} %bitcast.11, bf16[64,1024]{1,0:T(8,128)(2,1)} %bitcast.14), custom_call_target="tpu_custom_call" | custom-call | tf_op jit(solution)/shard_map/pallas_call | solution.py:66
  3.0 15.8 %all_to_all.45.in_ref = bf16[16,16,128]{2,1,0:T(8,128)(2,1)S(1)} all-to-all(bf16[16,16,128]{2,1,0:T(8,128)(2,1)S(1)} %shard_map.46), channel_id=1, replica_groups=mesh['z'=8,'xh'=2,'xl'=2,'y'=8,'c'=2] {'xl','y'}, dimensions={0} | all-to-all | bytes 131072 | tf_op jit(solution)/shard_map/all_to_all | solution.py:361
  20.8 12.4 %all-to-all-start.1 = ((bf16[16,32,1024]{2,1,0:T(8,128)(2,1)}), bf16[16,32,1024]{2,1,0:T(8,128)(2,1)S(1)}, u32[]{:S(2)}, u32[]{:S(2)}) async-start(bf16[16,32,1024]{2,1,0:T(8,128)(2,1)} %shard_map.47), calls=%async_computation.1 | async-start | bytes 2097152 | tf_op jit(solution)/shard_map/all_to_all | solution.py:363
  33.2 1.9 collective-permute-start
  35.1 3.8 %collective-permute-done = bf16[64,1024]{1,0:T(8,128)(2,1)S(1)} collective-permute-done((bf16[64,1024]{1,0:T(8,128)(2,1)S(1)}, bf16[64,1024]{1,0:T(8,128)(2,1)S(1)}, u32[]{:S(2)}, u32[]{:S(2)}) %collective-permute-start) | collective-permute-done | bytes 131104 | tf_op jit(solution)/shard_map/ppermute | solution.py:344
  39.0 2.6 %collective-permute-start.1 = (bf16[128,1024]{1,0:T(8,128)(2,1)S(1)}, bf16[128,1024]{1,0:T(8,128)(2,1)S(1)}, u32[]{:S(2)}, u32[]{:S(2)}) collective-permute-start(bf16[128,1024]{1,0:T(8,128)(2,1)S(1)} %pad_maximum_fusion.refs_0_), channel_id=1, source_target_pairs={{0,2},{2,4},{4,6},{6,8},{8,10},{10,12},{12,14},{14,0},{1,3},{3,5},... | collective-permute-start | bytes 786440 | tf_op jit(solution)/shard_map/ppermute | solution.py:351
  41.6 3.9 %collective-permute-start.5 = (bf16[128,1024]{1,0:T(8,128)(2,1)S(1)}, bf16[128,1024]{1,0:T(8,128)(2,1)S(1)}, u32[]{:S(2)}, u32[]{:S(2)}) collective-permute-start(bf16[128,1024]{1,0:T(8,128)(2,1)S(1)} %pad_maximum_fusion.refs_0_), channel_id=1, source_target_pairs={{0,14},{2,0},{4,2},{6,4},{8,6},{10,8},{12,10},{14,12},{1,15},{3,1}... | collective-permute-start | bytes 786440 | tf_op jit(solution)/shard_map/ppermute | solution.py:352
  45.5 2.1 %collective-permute-done.1.refs_1_ = bf16[128,1024]{1,0:T(8,128)(2,1)S(1)} collective-permute-done((bf16[128,1024]{1,0:T(8,128)(2,1)S(1)}, bf16[128,1024]{1,0:T(8,128)(2,1)S(1)}, u32[]{:S(2)}, u32[]{:S(2)}) %collective-permute-start.1) | collective-permute-done | bytes 262176 | tf_op jit(solution)/shard_map/ppermute | solution.py:351
  49.5 4.6 %collective-permute-start.6 = (bf16[128,1024]{1,0:T(8,128)(2,1)S(1)}, bf16[128,1024]{1,0:T(8,128)(2,1)S(1)}, u32[]{:S(2)}, u32[]{:S(2)}) collective-permute-start(bf16[128,1024]{1,0:T(8,128)(2,1)S(1)} %collective-permute-done.5.refs_2_), channel_id=1, source_target_pairs={{0,14},{2,0},{4,2},{6,4},{8,6},{10,8},{12,10},{14,12},{1,15},{3,1}... | collective-permute-start | bytes 786440 | tf_op jit(solution)/shard_map/ppermute | solution.py:352
  54.1 2.1 %collective-permute-done.2.refs_3_ = bf16[128,1024]{1,0:T(8,128)(2,1)S(1)} collective-permute-done((bf16[128,1024]{1,0:T(8,128)(2,1)S(1)}, bf16[128,1024]{1,0:T(8,128)(2,1)S(1)}, u32[]{:S(2)}, u32[]{:S(2)}) %collective-permute-start.2) | collective-permute-done | bytes 262176 | tf_op jit(solution)/shard_map/ppermute | solution.py:351
  58.1 4.6 %collective-permute-start.7 = (bf16[128,1024]{1,0:T(8,128)(2,1)S(1)}, bf16[128,1024]{1,0:T(8,128)(2,1)S(1)}, u32[]{:S(2)}, u32[]{:S(2)}) collective-permute-start(bf16[128,1024]{1,0:T(8,128)(2,1)S(1)} %collective-permute-done.6.refs_4_), channel_id=1, source_target_pairs={{0,14},{2,0},{4,2},{6,4},{8,6},{10,8},{12,10},{14,12},{1,15},{3,1}... | collective-permute-start | bytes 786440 | tf_op jit(solution)/shard_map/ppermute | solution.py:352
  64.5 1.9 collective-permute-start.4
  66.5 4.7 %collective-permute-start.8 = (bf16[64,1024]{1,0:T(8,128)(2,1)S(1)}, bf16[64,1024]{1,0:T(8,128)(2,1)S(1)}, u32[]{:S(2)}, u32[]{:S(2)}) collective-permute-start(bf16[64,1024]{1,0:T(8,128)(2,1)S(1)} %slice.9), channel_id=1, source_target_pairs={{0,14},{2,0},{4,2},{6,4},{8,6},{10,8},{12,10},{14,12},{1,15},{3,1}... | collective-permute-start | bytes 393224 | tf_op jit(solution)/shard_map/ppermute | solution.py:354
  73.8 2.2 %shard_map.49.sent_ref = f32[264,1024]{1,0:T(8,128)S(1)} custom-call(bf16[64,1024]{1,0:T(8,128)(2,1)S(1)} %collective-permute-done.4.near_ref, bf16[64,1024]{1,0:T(8,128)(2,1)S(1)} %collective-permute-done.8.far_ref, bf16[16,32,1024]{2,1,0:T(8,128)(2,1)S(1)} %all-to-all-done.1.cen_ref, bf16[128,1024]{1,0:T(8,128)(2,1)} %copy-done.4, ...), custom_call_target="tpu_custom_call" | custom-call | tf_op jit(solution)/shard_map/pallas_call | solution.py:66
  76.0 9.8 %collective-permute-start.9 = (f32[264,1024]{1,0:T(8,128)S(1)}, f32[264,1024]{1,0:T(8,128)}, u32[]{:S(2)}, u32[]{:S(2)}) collective-permute-start(f32[264,1024]{1,0:T(8,128)S(1)} %shard_map.49.sent_ref), channel_id=1, source_target_pairs={{0,1},{1,0},{2,3},{3,2},{4,5},{5,4},{6,7},{7,6},{8,9},{9,8},{10,11... | collective-permute-start | bytes 3244040 | tf_op jit(solution)/shard_map/ppermute | solution.py:374
  86.1 2.2 %shard_map.48 = (f32[256,1024]{1,0:T(8,128)S(1)}, f32[8,256]{1,0:T(8,128)S(1)}) custom-call(bf16[64,1024]{1,0:T(8,128)(2,1)S(1)} %collective-permute-done.4.near_ref, bf16[64,1024]{1,0:T(8,128)(2,1)S(1)} %collective-permute-done.8.far_ref, bf16[16,32,1024]{2,1,0:T(8,128)(2,1)S(1)} %all-to-all-done.1.cen_ref, bf16[128,1024]{1,0:T(8,128)(2,1)} %copy-done.4, ...), custom_call_target="tpu_custom_call" | custom-call | tf_op jit(solution)/shard_map/pallas_call | solution.py:66
  88.4 1.9 shard_map.50
  90.3 21.2 %all_to_all.46.recv_ref = f32[16,16,256]{2,1,0:T(8,128)S(1)} all-to-all(f32[16,16,256]{2,1,0:T(8,128)S(1)} %get-tuple-element.28), channel_id=1, replica_groups=mesh['z'=8,'xh'=2,'xl'=2,'y'=8,'c'=2] {'z','xh'}, dimensions={0} | all-to-all | bytes 524288 | tf_op jit(solution)/shard_map/all_to_all | solution.py:383
  112.6 15.5 %all_to_all.47.recv_ref = f32[64,4,128]{2,1,0:T(4,128)S(1)} all-to-all(f32[64,4,128]{2,1,0:T(4,128)S(1)} %get-tuple-element.32), channel_id=1, replica_groups=mesh['z'=8,'xh'=2,'xl'=2,'y'=8,'c'=2] {'xl','y','c'}, dimensions={0} | all-to-all | bytes 262144 | tf_op jit(solution)/shard_map/all_to_all | solution.py:385
  128.2 12.5 %all_to_all.48.recv_ref = f32[32,4,128]{2,1,0:T(4,128)S(1)} all-to-all(f32[32,4,128]{2,1,0:T(4,128)S(1)} %get-tuple-element.33), channel_id=1, replica_groups=mesh['z'=8,'xh'=2,'xl'=2,'y'=8,'c'=2] {'xl','y','c'}, dimensions={0} | all-to-all | bytes 131072 | tf_op jit(solution)/shard_map/all_to_all | solution.py:387
  141.2 14.2 %all_to_all.49.recv_ref = f32[16,16,256]{2,1,0:T(8,128)S(1)} all-to-all(f32[16,16,256]{2,1,0:T(8,128)S(1)} %get-tuple-element.34), channel_id=1, replica_groups=mesh['z'=8,'xh'=2,'xl'=2,'y'=8,'c'=2] {'z','xh'}, dimensions={0} | all-to-all | bytes 524288 | tf_op jit(solution)/shard_map/all_to_all | solution.py:389
  156.5 16.2 %all_to_all.50.recv_ref = f32[96,4,128]{2,1,0:T(4,128)S(1)} all-to-all(f32[96,4,128]{2,1,0:T(4,128)S(1)} %get-tuple-element.37), channel_id=1, replica_groups=mesh['z'=8,'xh'=2,'xl'=2,'y'=8,'c'=2] {'xl','y','c'}, dimensions={0} | all-to-all | bytes 393216 | tf_op jit(solution)/shard_map/all_to_all | solution.py:394
  173.5 13.6 %all_to_all.51.recv_ref = f32[64,4,128]{2,1,0:T(4,128)S(1)} all-to-all(f32[64,4,128]{2,1,0:T(4,128)S(1)} %get-tuple-element.41), channel_id=1, replica_groups=mesh['z'=8,'xh'=2,'xl'=2,'y'=8,'c'=2] {'xl','y','c'}, dimensions={0} | all-to-all | bytes 262144 | tf_op jit(solution)/shard_map/all_to_all | solution.py:399
  187.2 11.4 %all_to_all.52.recv_ref = f32[16,1,128]{2,1,0:T(1,128)S(1)} all-to-all(f32[16,1,128]{2,1,0:T(1,128)S(1)} %get-tuple-element.42), channel_id=1, replica_groups=mesh['z'=8,'xh'=2,'xl'=2,'y'=8,'c'=2] {'z','xh'}, dimensions={0} | all-to-all | bytes 16384 | tf_op jit(solution)/shard_map/all_to_all | solution.py:401
  (50 shorter events, 15.5 us)
Async XLA Ops:
  0.1 0.7 copy-start.1
  20.7 12.4 %copy-start.11 = (bf16[1024,64]{0,1:T(8,128)(2,1)S(1)}, bf16[1024,64]{0,1:T(8,128)(2,1)}, u32[]{:S(2)}) copy-start(bf16[1024,64]{0,1:T(8,128)(2,1)} %param.4) | copy-start | bytes 393220
  20.8 53.0 %all-to-all-start.1 = ((bf16[16,32,1024]{2,1,0:T(8,128)(2,1)}), bf16[16,32,1024]{2,1,0:T(8,128)(2,1)S(1)}, u32[]{:S(2)}, u32[]{:S(2)}) async-start(bf16[16,32,1024]{2,1,0:T(8,128)(2,1)} %shard_map.47), calls=%async_computation.1 | async-start | bytes 2097152 | tf_op jit(solution)/shard_map/all_to_all | solution.py:363
  33.2 5.7 %collective-permute-start = (bf16[64,1024]{1,0:T(8,128)(2,1)S(1)}, bf16[64,1024]{1,0:T(8,128)(2,1)S(1)}, u32[]{:S(2)}, u32[]{:S(2)}) collective-permute-start(bf16[64,1024]{1,0:T(8,128)(2,1)S(1)} %bitcast.15), channel_id=1, source_target_pairs={{0,16},{16,0},{1,17},{17,1},{2,18},{18,2},{3,19},{19,3},{4,20},{20... | collective-permute-start | bytes 393224 | tf_op jit(solution)/shard_map/ppermute | solution.py:344
  39.0 34.8 %copy-start.4 = (bf16[128,1024]{1,0:T(8,128)(2,1)}, bf16[128,1024]{1,0:T(8,128)(2,1)S(1)}, u32[]{:S(2)}) copy-start(bf16[128,1024]{1,0:T(8,128)(2,1)S(1)} %pad_maximum_fusion.refs_0_) | copy-start | bytes 786436
  39.0 8.6 %collective-permute-start.1 = (bf16[128,1024]{1,0:T(8,128)(2,1)S(1)}, bf16[128,1024]{1,0:T(8,128)(2,1)S(1)}, u32[]{:S(2)}, u32[]{:S(2)}) collective-permute-start(bf16[128,1024]{1,0:T(8,128)(2,1)S(1)} %pad_maximum_fusion.refs_0_), channel_id=1, source_target_pairs={{0,2},{2,4},{4,6},{6,8},{8,10},{10,12},{12,14},{14,0},{1,3},{3,5},... | collective-permute-start | bytes 786440 | tf_op jit(solution)/shard_map/ppermute | solution.py:351
  41.6 7.9 %collective-permute-start.5 = (bf16[128,1024]{1,0:T(8,128)(2,1)S(1)}, bf16[128,1024]{1,0:T(8,128)(2,1)S(1)}, u32[]{:S(2)}, u32[]{:S(2)}) collective-permute-start(bf16[128,1024]{1,0:T(8,128)(2,1)S(1)} %pad_maximum_fusion.refs_0_), channel_id=1, source_target_pairs={{0,14},{2,0},{4,2},{6,4},{8,6},{10,8},{12,10},{14,12},{1,15},{3,1}... | collective-permute-start | bytes 786440 | tf_op jit(solution)/shard_map/ppermute | solution.py:352
  47.6 26.1 %copy-start.7 = (bf16[128,1024]{1,0:T(8,128)(2,1)}, bf16[128,1024]{1,0:T(8,128)(2,1)S(1)}, u32[]{:S(2)}) copy-start(bf16[128,1024]{1,0:T(8,128)(2,1)S(1)} %collective-permute-done.1.refs_1_) | copy-start | bytes 786436
  47.6 8.6 %collective-permute-start.2 = (bf16[128,1024]{1,0:T(8,128)(2,1)S(1)}, bf16[128,1024]{1,0:T(8,128)(2,1)S(1)}, u32[]{:S(2)}, u32[]{:S(2)}) collective-permute-start(bf16[128,1024]{1,0:T(8,128)(2,1)S(1)} %collective-permute-done.1.refs_1_), channel_id=1, source_target_pairs={{0,2},{2,4},{4,6},{6,8},{8,10},{10,12},{12,14},{14,0},{1,3},{3,5},... | collective-permute-start | bytes 786440 | tf_op jit(solution)/shard_map/ppermute | solution.py:351
  49.5 24.2 %copy-start.8 = (bf16[128,1024]{1,0:T(8,128)(2,1)}, bf16[128,1024]{1,0:T(8,128)(2,1)S(1)}, u32[]{:S(2)}) copy-start(bf16[128,1024]{1,0:T(8,128)(2,1)S(1)} %collective-permute-done.5.refs_2_) | copy-start | bytes 786436
  49.5 8.6 %collective-permute-start.6 = (bf16[128,1024]{1,0:T(8,128)(2,1)S(1)}, bf16[128,1024]{1,0:T(8,128)(2,1)S(1)}, u32[]{:S(2)}, u32[]{:S(2)}) collective-permute-start(bf16[128,1024]{1,0:T(8,128)(2,1)S(1)} %collective-permute-done.5.refs_2_), channel_id=1, source_target_pairs={{0,14},{2,0},{4,2},{6,4},{8,6},{10,8},{12,10},{14,12},{1,15},{3,1}... | collective-permute-start | bytes 786440 | tf_op jit(solution)/shard_map/ppermute | solution.py:352
  56.2 17.5 %copy-start.9 = (bf16[128,1024]{1,0:T(8,128)(2,1)}, bf16[128,1024]{1,0:T(8,128)(2,1)S(1)}, u32[]{:S(2)}) copy-start(bf16[128,1024]{1,0:T(8,128)(2,1)S(1)} %collective-permute-done.2.refs_3_) | copy-start | bytes 786436
  56.2 8.3 %collective-permute-start.3 = (bf16[128,1024]{1,0:T(8,128)(2,1)S(1)}, bf16[128,1024]{1,0:T(8,128)(2,1)S(1)}, u32[]{:S(2)}, u32[]{:S(2)}) collective-permute-start(bf16[128,1024]{1,0:T(8,128)(2,1)S(1)} %collective-permute-done.2.refs_3_), channel_id=1, source_target_pairs={{0,2},{2,4},{4,6},{6,8},{8,10},{10,12},{12,14},{14,0},{1,3},{3,5},... | collective-permute-start | bytes 786440 | tf_op jit(solution)/shard_map/ppermute | solution.py:351
  58.1 8.3 %copy-start.10 = (bf16[128,1024]{1,0:T(8,128)(2,1)}, bf16[128,1024]{1,0:T(8,128)(2,1)S(1)}, u32[]{:S(2)}) copy-start(bf16[128,1024]{1,0:T(8,128)(2,1)S(1)} %collective-permute-done.6.refs_4_) | copy-start | bytes 786436
  58.1 8.3 %collective-permute-start.7 = (bf16[128,1024]{1,0:T(8,128)(2,1)S(1)}, bf16[128,1024]{1,0:T(8,128)(2,1)S(1)}, u32[]{:S(2)}, u32[]{:S(2)}) collective-permute-start(bf16[128,1024]{1,0:T(8,128)(2,1)S(1)} %collective-permute-done.6.refs_4_), channel_id=1, source_target_pairs={{0,14},{2,0},{4,2},{6,4},{8,6},{10,8},{12,10},{14,12},{1,15},{3,1}... | collective-permute-start | bytes 786440 | tf_op jit(solution)/shard_map/ppermute | solution.py:352
  64.5 9.2 %copy-start.5 = (bf16[128,1024]{1,0:T(8,128)(2,1)}, bf16[128,1024]{1,0:T(8,128)(2,1)S(1)}, u32[]{:S(2)}) copy-start(bf16[128,1024]{1,0:T(8,128)(2,1)S(1)} %collective-permute-done.3.refs_5_) | copy-start | bytes 786436
  64.5 7.4 %collective-permute-start.4 = (bf16[64,1024]{1,0:T(8,128)(2,1)S(1)}, bf16[64,1024]{1,0:T(8,128)(2,1)S(1)}, u32[]{:S(2)}, u32[]{:S(2)}) collective-permute-start(bf16[64,1024]{1,0:T(8,128)(2,1)S(1)} %slice.8), channel_id=1, source_target_pairs={{0,2},{2,4},{4,6},{6,8},{8,10},{10,12},{12,14},{14,0},{1,3},{3,5},... | collective-permute-start | bytes 393224 | tf_op jit(solution)/shard_map/ppermute | solution.py:354
  66.5 7.3 %copy-start.6 = (bf16[128,1024]{1,0:T(8,128)(2,1)}, bf16[128,1024]{1,0:T(8,128)(2,1)S(1)}, u32[]{:S(2)}) copy-start(bf16[128,1024]{1,0:T(8,128)(2,1)S(1)} %collective-permute-done.7.refs_6_) | copy-start | bytes 786436
  66.5 19.2 %copy-start.2 = (s32[32,1,16]{0,2,1:T(8,128)S(1)}, s32[32,1,16]{0,2,1:T(8,128)}, u32[]{:S(2)}) copy-start(s32[32,1,16]{0,2,1:T(8,128)} %param.5) | copy-start | bytes 6148
  66.5 7.2 %collective-permute-start.8 = (bf16[64,1024]{1,0:T(8,128)(2,1)S(1)}, bf16[64,1024]{1,0:T(8,128)(2,1)S(1)}, u32[]{:S(2)}, u32[]{:S(2)}) collective-permute-start(bf16[64,1024]{1,0:T(8,128)(2,1)S(1)} %slice.9), channel_id=1, source_target_pairs={{0,14},{2,0},{4,2},{6,4},{8,6},{10,8},{12,10},{14,12},{1,15},{3,1}... | collective-permute-start | bytes 393224 | tf_op jit(solution)/shard_map/ppermute | solution.py:354
  76.0 12.4 %collective-permute-start.9 = (f32[264,1024]{1,0:T(8,128)S(1)}, f32[264,1024]{1,0:T(8,128)}, u32[]{:S(2)}, u32[]{:S(2)}) collective-permute-start(f32[264,1024]{1,0:T(8,128)S(1)} %shard_map.49.sent_ref), channel_id=1, source_target_pairs={{0,1},{1,0},{2,3},{3,2},{4,5},{5,4},{6,7},{7,6},{8,9},{9,8},{10,11... | collective-permute-start | bytes 3244040 | tf_op jit(solution)/shard_map/ppermute | solution.py:374
  86.1 2.2 %copy-start.3 = (s32[1024]{0:T(1024)S(1)}, s32[1024]{0:T(1024)}, u32[]{:S(2)}) copy-start(s32[1024]{0:T(1024)} %param.6) | copy-start | bytes 12292
  88.4 23.2 %copy-start = (f32[256,256]{1,0:T(8,128)S(1)}, f32[256,256]{1,0:T(8,128)}, u32[]{:S(2)}) copy-start(f32[256,256]{1,0:T(8,128)} %pre_ref.3) | copy-start | bytes 786436

commit v6 on v5

--- a/solution.py
+++ b/solution.py
@@ -73,13 +73,11 @@
     )(*args)
 
 
-def pick_kernel(spot_ref, index_ref, ft_hbm, out_ref, both_ref, sem):
-    both_ref[...] = jnp.zeros_like(both_ref)
-    low = pltpu.make_async_copy(ft_hbm, both_ref.at[0:SLICE, 0:ROWS], sem.at[0])
-    high = pltpu.make_async_copy(ft_hbm, both_ref.at[SLICE : 2 * SLICE, ROWS : 2 * ROWS], sem.at[1])
-    low.start()
-    high.start()
+def pick_kernel(spot_ref, index_ref, ft_hbm, out_ref, mine_ref, ft_ref, sem):
+    copy = pltpu.make_async_copy(ft_hbm, ft_ref, sem)
+    copy.start()
     core, base = spot_ref[3], spot_ref[4]
+    mine_ref[...] = (iota((4, 128), 1) == iota((4, 128), 0) + spot_ref[2] * 4).astype(F32)
     lane = iota((OWN, ROWS), 1)
     index = index_ref[...]
     blocks = iota((OWN, N_FEAT), 1)
@@ -88,21 +86,23 @@
         col = jnp.sum(jnp.where(blocks == block, index, 0), axis=1, keepdims=True) - base
         return (lane == col).astype(F32).astype(BF16)
 
-    def masks(side):
-        return jnp.concatenate([mask(2 * p + side) for p in range(N_PLANE)], axis=0)
-
-    chosen = jnp.concatenate([masks(core), masks(1 - core)], axis=1)
-    low.wait()
-    high.wait()
-    both = lax.dot_general(chosen, both_ref[...], LANES, preferred_element_type=F32)
+    def chosen(side, table):
+        masks = jnp.concatenate([mask(2 * p + side) for p in range(N_PLANE)], axis=0)
+        return lax.dot_general(masks, table, LANES, preferred_element_type=F32)
+
+    copy.wait()
+    ft = ft_ref[...]
+    zero = jnp.zeros_like(ft)
+    both = chosen(core, jnp.concatenate([ft, zero], axis=0)) + chosen(1 - core, jnp.concatenate([zero, ft], axis=0))
     out_ref[...] = both.astype(BF16).reshape(N_PLANE, OWN, 2 * SLICE)
 
 
 def spread_kernel(spot_ref, in_ref, out_ref):
     low = iota((OWN, 128), 1) < SLICE
     side, y = spot_ref[0], spot_ref[1]
+    sign = 1 - 2 * spot_ref[3]
     for t, offset in enumerate(OFFSETS):
-        row = lax.rem(y + (offset + N_Y), N_Y)
+        row = lax.rem(y + N_Y + sign * offset, N_Y)
         a = in_ref[side * N_Y + row].astype(F32)
         b = in_ref[(1 - side) * N_Y + row].astype(F32)
         own = jnp.where(low, a, pltpu.roll(b, SLICE, 1)).astype(BF16)
@@ -290,7 +290,7 @@
         out_ref[s * 3 + 2] = row
 
 
-def step_kernel(spot_ref, recv_ref, chunk_ref, rhs_ref, u_ref, image_ref, v_ref, scal_ref, out_ref):
+def step_kernel(mine_ref, recv_ref, chunk_ref, rhs_ref, u_ref, image_ref, v_ref, scal_ref, out_ref):
     row = sum_slot(recv_ref, 3, 2)[0:1]
     scal_ref[...] = jnp.broadcast_to(row, (8, 128))
     alpha = to_col(row, CLASSES, 0) / to_col(row, CLASSES, CLASSES)
@@ -298,13 +298,12 @@
     z = u_ref[...] - alpha * v_ref[...]
     rz = to_row(jnp.sum(residual * z, axis=1, keepdims=True))
     alpha_row = to_row(alpha)
-    first = spot_ref[2] * 4
-    mine = iota((4, 128), 1) == iota((4, 128), 0) + first
-    alpha_mine = jnp.sum(jnp.where(mine, alpha_row, 0.0), axis=1, keepdims=True)
+    mine = mine_ref[...]
+    alpha_mine = jnp.sum(mine * alpha_row, axis=1, keepdims=True)
     kz = chunk_ref[0] - alpha_mine * sum_slot(recv_ref, 3, 0)
     gz = chunk_ref[1] - alpha_mine * sum_slot(recv_ref, 3, 1)
     quad = jnp.sum(kz * gz, axis=1, keepdims=True)
-    quad_row = jnp.sum(jnp.where(mine, quad, 0.0), axis=0, keepdims=True)
+    quad_row = jnp.sum(mine * quad, axis=0, keepdims=True)
     which = iota((4, 128), 0)
     tail = jnp.where(which == 0, rz, jnp.where(which == 1, quad_row, 0.0))
     for s in range(N_FEAT):
@@ -343,20 +342,20 @@
     ft_local = features.T
     swapped = lax.ppermute(ft_local, "xl", [(0, 1), (1, 0)])
     here = jnp.concatenate([ft_local, swapped], axis=0)
-    up = [(i, (i + 1) % N_Y) for i in range(N_Y)]
-    down = [(i, (i - 1) % N_Y) for i in range(N_Y)]
+    up = [(2 * i + c, 2 * ((i + 1 - 2 * c) % N_Y) + c) for i in range(N_Y) for c in range(2)]
+    down = [(2 * i + c, 2 * ((i - 1 + 2 * c) % N_Y) + c) for i in range(N_Y) for c in range(2)]
     chunks = [here]
     below = above = here
     for _ in range(3):
-        below = lax.ppermute(below, "y", up)
-        above = lax.ppermute(above, "y", down)
+        below = lax.ppermute(below, ("y", "c"), up)
+        above = lax.ppermute(above, ("y", "c"), down)
         chunks += [below, above]
-    chunks += [lax.ppermute(below[:SLICE], "y", up), lax.ppermute(above[SLICE:], "y", down)]
+    chunks += [lax.ppermute(below[:SLICE], ("y", "c"), up), lax.ppermute(above[SLICE:], ("y", "c"), down)]
 
     spot = jnp.stack([lax.axis_index("xl"), lax.axis_index("y"), feat_index // 8, core, ex_index * ROWS])
-    picked = call(
-        pick_kernel, ((N_PLANE, OWN, 2 * SLICE), BF16), spot, centre_index[:, 0, :].T, ft_local, smem=1, hbm=1,
-        scratch=[pltpu.VMEM((2 * SLICE, 2 * ROWS), BF16), pltpu.SemaphoreType.DMA((2,))],
+    picked, mine = call(
+        pick_kernel, [((N_PLANE, OWN, 2 * SLICE), BF16), ((4, 128), F32)], spot, centre_index[:, 0, :].T, ft_local, smem=1, hbm=1,
+        scratch=[pltpu.VMEM((SLICE, ROWS), BF16), pltpu.SemaphoreType.DMA],
     )
     picked = lax.all_to_all(picked, PLANE, 0, 0, tiled=True)
     spread = call(spread_kernel, ((N_EX, 2 * OWN, WIDTH), BF16), spot, picked, smem=1)
@@ -394,7 +393,7 @@
     part = lax.all_to_all(part, FEAT, 0, 0, tiled=True)
     scal, part = call(
         step_kernel, [((8, 128), F32), ((N_FEAT * 2, 4, 128), F32)],
-        spot, part, chunk, rhs, u, image, v, smem=1,
+        mine, part, chunk, rhs, u, image, v,
     )
     part = lax.all_to_all(part, FEAT, 0, 0, tiled=True)
     kz, tail, part = call(gather_kernel, [((CLASSES, ROWS), F32), ((4, 128), F32), ((N_EX, 1, 128), F32)], part)

time: 201 us -> 205 us (1.020)
  waiting for transfers between devices: 12.3 us -> 19 us
  starting transfers between devices: 50.2 us -> 47.9 us
    ppermute x8, waiting for transfers between devices: 8.5 us -> 15.2 us  [the longest x3 8.39 us: predict(): below = lax.ppermute(below, ('y', 'c'), up)]
where the time goes in v6:
time: 205 us; the launch traced here: 204 us
  blocking collectives  121 us (59%)
  starting transfers between devices  47.9 us (23%)
  waiting for transfers between devices  19 us (9%)
  Pallas kernels  14.1 us (7%)
    all_to_all x4, blocking collectives, predict(): part = lax.all_to_all(part, FEAT, 0, 0, tiled=True)  58.1 us
    all_to_all x3, blocking collectives, predict(): part = lax.all_to_all(part, EX, 0, 0, tiled=True)  47 us
    all_to_all x1, blocking collectives, predict(): picked = lax.all_to_all(picked, PLANE, 0, 0, tiled=True)  15.8 us
    pallas_call x12, Pallas kernels, call(): pl.pallas_call(kernel, out_shape=[space(s, d) for s, d in outs] if many e...  14.1 us
    all_to_all x1, starting transfers between devices, predict(): cen = lax.all_to_all(spread, EX, 0, 0, tiled=True)  12.4 us
    ppermute x3, starting transfers between devices, predict(): below = lax.ppermute(below, ('y', 'c'), up)  12.1 us
    ppermute x3, waiting for transfers between devices, predict(): below = lax.ppermute(below, ('y', 'c'), up)  8.39 us
    ppermute x1, starting transfers between devices, predict(): got = lax.ppermute(sent, 'c', [(0, 1), (1, 0)])  7.81 us
  transfers between devices with their start and end apart: 11, of which 6 were waited for; matrix products, arithmetic and copies ran while one was open for 0% of the time, Pallas kernels for 1%

profile of v6, /device:TPU:1, one launch (start us, length us, event | category | flops | bytes accessed | tf_op | source)
XLA Modules:
  0.0 203.5 jit_solution(7625943073430536500)
XLA Ops:
  0.8 2.1 %shard_map.46 = (bf16[16,16,128]{2,1,0:T(8,128)(2,1)S(1)}, f32[4,128]{1,0:T(4,128)S(1)}) custom-call(s32[5]{0:T(128)S(1)} %stack.23.spot_ref, s32[16,32]{1,0:T(8,128)S(1)} %bitcast.11, bf16[64,1024]{1,0:T(8,128)(2,1)} %bitcast.14), custom_call_target="tpu_custom_call" | custom-call | tf_op jit(solution)/shard_map/pallas_call | solution.py:66
  2.9 15.8 %all_to_all.45.in_ref = bf16[16,16,128]{2,1,0:T(8,128)(2,1)S(1)} all-to-all(bf16[16,16,128]{2,1,0:T(8,128)(2,1)S(1)} %get-tuple-element.29), channel_id=1, replica_groups=mesh['z'=8,'xh'=2,'xl'=2,'y'=8,'c'=2] {'xl','y'}, dimensions={0} | all-to-all | bytes 131072 | tf_op jit(solution)/shard_map/all_to_all | solution.py:360
  20.6 12.4 %all-to-all-start.1 = ((bf16[16,32,1024]{2,1,0:T(8,128)(2,1)}), bf16[16,32,1024]{2,1,0:T(8,128)(2,1)S(1)}, u32[]{:S(2)}, u32[]{:S(2)}) async-start(bf16[16,32,1024]{2,1,0:T(8,128)(2,1)} %shard_map.47), calls=%async_computation.1 | async-start | bytes 2097152 | tf_op jit(solution)/shard_map/all_to_all | solution.py:362
  35.0 3.8 %collective-permute-done = bf16[64,1024]{1,0:T(8,128)(2,1)S(1)} collective-permute-done((bf16[64,1024]{1,0:T(8,128)(2,1)S(1)}, bf16[64,1024]{1,0:T(8,128)(2,1)S(1)}, u32[]{:S(2)}, u32[]{:S(2)}) %collective-permute-start) | collective-permute-done | bytes 131104 | tf_op jit(solution)/shard_map/ppermute | solution.py:343
  38.8 2.9 %collective-permute-start.1 = (bf16[128,1024]{1,0:T(8,128)(2,1)S(1)}, bf16[128,1024]{1,0:T(8,128)(2,1)S(1)}, u32[]{:S(2)}, u32[]{:S(2)}) collective-permute-start(bf16[128,1024]{1,0:T(8,128)(2,1)S(1)} %pad_maximum_fusion.refs_0_), channel_id=1, source_target_pairs={{0,2},{1,15},{2,4},{3,1},{4,6},{5,3},{6,8},{7,5},{8,10},{9,7},{10,... | collective-permute-start | bytes 786440 | tf_op jit(solution)/shard_map/ppermute | solution.py:350
  41.8 2.4 %collective-permute-start.5 = (bf16[128,1024]{1,0:T(8,128)(2,1)S(1)}, bf16[128,1024]{1,0:T(8,128)(2,1)S(1)}, u32[]{:S(2)}, u32[]{:S(2)}) collective-permute-start(bf16[128,1024]{1,0:T(8,128)(2,1)S(1)} %pad_maximum_fusion.refs_0_), channel_id=1, source_target_pairs={{0,14},{1,3},{2,0},{3,5},{4,2},{5,7},{6,4},{7,9},{8,6},{9,11},{10,... | collective-permute-start | bytes 786440 | tf_op jit(solution)/shard_map/ppermute | solution.py:351
  44.1 2.1 %collective-permute-done.1.refs_1_ = bf16[128,1024]{1,0:T(8,128)(2,1)S(1)} collective-permute-done((bf16[128,1024]{1,0:T(8,128)(2,1)S(1)}, bf16[128,1024]{1,0:T(8,128)(2,1)S(1)}, u32[]{:S(2)}, u32[]{:S(2)}) %collective-permute-start.1) | collective-permute-done | bytes 262176 | tf_op jit(solution)/shard_map/ppermute | solution.py:350
  46.3 4.1 %collective-permute-start.2 = (bf16[128,1024]{1,0:T(8,128)(2,1)S(1)}, bf16[128,1024]{1,0:T(8,128)(2,1)S(1)}, u32[]{:S(2)}, u32[]{:S(2)}) collective-permute-start(bf16[128,1024]{1,0:T(8,128)(2,1)S(1)} %collective-permute-done.1.refs_1_), channel_id=1, source_target_pairs={{0,2},{1,15},{2,4},{3,1},{4,6},{5,3},{6,8},{7,5},{8,10},{9,7},{10,... | collective-permute-start | bytes 786440 | tf_op jit(solution)/shard_map/ppermute | solution.py:350
  53.7 2.5 %collective-permute-done.2.refs_3_ = bf16[128,1024]{1,0:T(8,128)(2,1)S(1)} collective-permute-done((bf16[128,1024]{1,0:T(8,128)(2,1)S(1)}, bf16[128,1024]{1,0:T(8,128)(2,1)S(1)}, u32[]{:S(2)}, u32[]{:S(2)}) %collective-permute-start.2) | collective-permute-done | bytes 262176 | tf_op jit(solution)/shard_map/ppermute | solution.py:350
  56.3 5.1 %collective-permute-start.3 = (bf16[128,1024]{1,0:T(8,128)(2,1)S(1)}, bf16[128,1024]{1,0:T(8,128)(2,1)S(1)}, u32[]{:S(2)}, u32[]{:S(2)}) collective-permute-start(bf16[128,1024]{1,0:T(8,128)(2,1)S(1)} %collective-permute-done.2.refs_3_), channel_id=1, source_target_pairs={{0,2},{1,15},{2,4},{3,1},{4,6},{5,3},{6,8},{7,5},{8,10},{9,7},{10,... | collective-permute-start | bytes 786440 | tf_op jit(solution)/shard_map/ppermute | solution.py:350
  63.3 3.8 %collective-permute-done.3.refs_5_ = bf16[128,1024]{1,0:T(8,128)(2,1)S(1)} collective-permute-done((bf16[128,1024]{1,0:T(8,128)(2,1)S(1)}, bf16[128,1024]{1,0:T(8,128)(2,1)S(1)}, u32[]{:S(2)}, u32[]{:S(2)}) %collective-permute-start.3) | collective-permute-done | bytes 262176 | tf_op jit(solution)/shard_map/ppermute | solution.py:350
  67.1 5.3 %collective-permute-start.4 = (bf16[64,1024]{1,0:T(8,128)(2,1)S(1)}, bf16[64,1024]{1,0:T(8,128)(2,1)S(1)}, u32[]{:S(2)}, u32[]{:S(2)}) collective-permute-start(bf16[64,1024]{1,0:T(8,128)(2,1)S(1)} %slice.8), channel_id=1, source_target_pairs={{0,2},{1,15},{2,4},{3,1},{4,6},{5,3},{6,8},{7,5},{8,10},{9,7},{10,... | collective-permute-start | bytes 393224 | tf_op jit(solution)/shard_map/ppermute | solution.py:353
  72.5 2.1 %collective-permute-start.8 = (bf16[64,1024]{1,0:T(8,128)(2,1)S(1)}, bf16[64,1024]{1,0:T(8,128)(2,1)S(1)}, u32[]{:S(2)}, u32[]{:S(2)}) collective-permute-start(bf16[64,1024]{1,0:T(8,128)(2,1)S(1)} %slice.9), channel_id=1, source_target_pairs={{0,14},{1,3},{2,0},{3,5},{4,2},{5,7},{6,4},{7,9},{8,6},{9,11},{10,... | collective-permute-start | bytes 393224 | tf_op jit(solution)/shard_map/ppermute | solution.py:353
  74.5 5.3 %collective-permute-done.8.far_ref = bf16[64,1024]{1,0:T(8,128)(2,1)S(1)} collective-permute-done((bf16[64,1024]{1,0:T(8,128)(2,1)S(1)}, bf16[64,1024]{1,0:T(8,128)(2,1)S(1)}, u32[]{:S(2)}, u32[]{:S(2)}) %collective-permute-start.8) | collective-permute-done | bytes 131104 | tf_op jit(solution)/shard_map/ppermute | solution.py:353
  79.9 2.2 %shard_map.49.sent_ref = f32[264,1024]{1,0:T(8,128)S(1)} custom-call(bf16[64,1024]{1,0:T(8,128)(2,1)S(1)} %collective-permute-done.4.near_ref, bf16[64,1024]{1,0:T(8,128)(2,1)S(1)} %collective-permute-done.8.far_ref, bf16[16,32,1024]{2,1,0:T(8,128)(2,1)S(1)} %all-to-all-done.1.cen_ref, bf16[128,1024]{1,0:T(8,128)(2,1)} %copy-done.4, ...), custom_call_target="tpu_custom_call" | custom-call | tf_op jit(solution)/shard_map/pallas_call | solution.py:66
  82.1 7.8 %collective-permute-start.9 = (f32[264,1024]{1,0:T(8,128)S(1)}, f32[264,1024]{1,0:T(8,128)}, u32[]{:S(2)}, u32[]{:S(2)}) collective-permute-start(f32[264,1024]{1,0:T(8,128)S(1)} %shard_map.49.sent_ref), channel_id=1, source_target_pairs={{0,1},{1,0},{2,3},{3,2},{4,5},{5,4},{6,7},{7,6},{8,9},{9,8},{10,11... | collective-permute-start | bytes 3244040 | tf_op jit(solution)/shard_map/ppermute | solution.py:373
  90.3 2.2 %shard_map.48 = (f32[256,1024]{1,0:T(8,128)S(1)}, f32[8,256]{1,0:T(8,128)S(1)}) custom-call(bf16[64,1024]{1,0:T(8,128)(2,1)S(1)} %collective-permute-done.4.near_ref, bf16[64,1024]{1,0:T(8,128)(2,1)S(1)} %collective-permute-done.8.far_ref, bf16[16,32,1024]{2,1,0:T(8,128)(2,1)S(1)} %all-to-all-done.1.cen_ref, bf16[128,1024]{1,0:T(8,128)(2,1)} %copy-done.4, ...), custom_call_target="tpu_custom_call" | custom-call | tf_op jit(solution)/shard_map/pallas_call | solution.py:66
  94.5 21.4 %all_to_all.46.recv_ref = f32[16,16,256]{2,1,0:T(8,128)S(1)} all-to-all(f32[16,16,256]{2,1,0:T(8,128)S(1)} %get-tuple-element.32), channel_id=1, replica_groups=mesh['z'=8,'xh'=2,'xl'=2,'y'=8,'c'=2] {'z','xh'}, dimensions={0} | all-to-all | bytes 524288 | tf_op jit(solution)/shard_map/all_to_all | solution.py:382
  116.9 15.9 %all_to_all.47.recv_ref = f32[64,4,128]{2,1,0:T(4,128)S(1)} all-to-all(f32[64,4,128]{2,1,0:T(4,128)S(1)} %get-tuple-element.36), channel_id=1, replica_groups=mesh['z'=8,'xh'=2,'xl'=2,'y'=8,'c'=2] {'xl','y','c'}, dimensions={0} | all-to-all | bytes 262144 | tf_op jit(solution)/shard_map/all_to_all | solution.py:384
  132.9 12.5 %all_to_all.48.recv_ref = f32[32,4,128]{2,1,0:T(4,128)S(1)} all-to-all(f32[32,4,128]{2,1,0:T(4,128)S(1)} %get-tuple-element.37), channel_id=1, replica_groups=mesh['z'=8,'xh'=2,'xl'=2,'y'=8,'c'=2] {'xl','y','c'}, dimensions={0} | all-to-all | bytes 131072 | tf_op jit(solution)/shard_map/all_to_all | solution.py:386
  145.9 14.2 %all_to_all.49.recv_ref = f32[16,16,256]{2,1,0:T(8,128)S(1)} all-to-all(f32[16,16,256]{2,1,0:T(8,128)S(1)} %get-tuple-element.38), channel_id=1, replica_groups=mesh['z'=8,'xh'=2,'xl'=2,'y'=8,'c'=2] {'z','xh'}, dimensions={0} | all-to-all | bytes 524288 | tf_op jit(solution)/shard_map/all_to_all | solution.py:388
  161.2 16.2 %all_to_all.50.recv_ref = f32[96,4,128]{2,1,0:T(4,128)S(1)} all-to-all(f32[96,4,128]{2,1,0:T(4,128)S(1)} %get-tuple-element.41), channel_id=1, replica_groups=mesh['z'=8,'xh'=2,'xl'=2,'y'=8,'c'=2] {'xl','y','c'}, dimensions={0} | all-to-all | bytes 393216 | tf_op jit(solution)/shard_map/all_to_all | solution.py:393
  177.7 13.6 %all_to_all.51.recv_ref = f32[64,4,128]{2,1,0:T(4,128)S(1)} all-to-all(f32[64,4,128]{2,1,0:T(4,128)S(1)} %get-tuple-element.45), channel_id=1, replica_groups=mesh['z'=8,'xh'=2,'xl'=2,'y'=8,'c'=2] {'xl','y','c'}, dimensions={0} | all-to-all | bytes 262144 | tf_op jit(solution)/shard_map/all_to_all | solution.py:398
  191.3 11.4 %all_to_all.52.recv_ref = f32[16,1,128]{2,1,0:T(1,128)S(1)} all-to-all(f32[16,1,128]{2,1,0:T(1,128)S(1)} %get-tuple-element.46), channel_id=1, replica_groups=mesh['z'=8,'xh'=2,'xl'=2,'y'=8,'c'=2] {'z','xh'}, dimensions={0} | all-to-all | bytes 16384 | tf_op jit(solution)/shard_map/all_to_all | solution.py:400
  (50 shorter events, 16.0 us)
Async XLA Ops:
  0.1 0.7 copy-start.1
  20.6 12.5 %copy-start.11 = (bf16[1024,64]{0,1:T(8,128)(2,1)S(1)}, bf16[1024,64]{0,1:T(8,128)(2,1)}, u32[]{:S(2)}) copy-start(bf16[1024,64]{0,1:T(8,128)(2,1)} %param.4) | copy-start | bytes 393220
  20.6 59.2 %all-to-all-start.1 = ((bf16[16,32,1024]{2,1,0:T(8,128)(2,1)}), bf16[16,32,1024]{2,1,0:T(8,128)(2,1)S(1)}, u32[]{:S(2)}, u32[]{:S(2)}) async-start(bf16[16,32,1024]{2,1,0:T(8,128)(2,1)} %shard_map.47), calls=%async_computation.1 | async-start | bytes 2097152 | tf_op jit(solution)/shard_map/all_to_all | solution.py:362
  33.1 5.7 %collective-permute-start = (bf16[64,1024]{1,0:T(8,128)(2,1)S(1)}, bf16[64,1024]{1,0:T(8,128)(2,1)S(1)}, u32[]{:S(2)}, u32[]{:S(2)}) collective-permute-start(bf16[64,1024]{1,0:T(8,128)(2,1)S(1)} %bitcast.15), channel_id=1, source_target_pairs={{0,16},{16,0},{1,17},{17,1},{2,18},{18,2},{3,19},{19,3},{4,20},{20... | collective-permute-start | bytes 393224 | tf_op jit(solution)/shard_map/ppermute | solution.py:343
  38.8 41.0 %copy-start.4 = (bf16[128,1024]{1,0:T(8,128)(2,1)}, bf16[128,1024]{1,0:T(8,128)(2,1)S(1)}, u32[]{:S(2)}) copy-start(bf16[128,1024]{1,0:T(8,128)(2,1)S(1)} %pad_maximum_fusion.refs_0_) | copy-start | bytes 786436
  38.8 7.4 %collective-permute-start.1 = (bf16[128,1024]{1,0:T(8,128)(2,1)S(1)}, bf16[128,1024]{1,0:T(8,128)(2,1)S(1)}, u32[]{:S(2)}, u32[]{:S(2)}) collective-permute-start(bf16[128,1024]{1,0:T(8,128)(2,1)S(1)} %pad_maximum_fusion.refs_0_), channel_id=1, source_target_pairs={{0,2},{1,15},{2,4},{3,1},{4,6},{5,3},{6,8},{7,5},{8,10},{9,7},{10,... | collective-permute-start | bytes 786440 | tf_op jit(solution)/shard_map/ppermute | solution.py:350
  41.8 10.1 %collective-permute-start.5 = (bf16[128,1024]{1,0:T(8,128)(2,1)S(1)}, bf16[128,1024]{1,0:T(8,128)(2,1)S(1)}, u32[]{:S(2)}, u32[]{:S(2)}) collective-permute-start(bf16[128,1024]{1,0:T(8,128)(2,1)S(1)} %pad_maximum_fusion.refs_0_), channel_id=1, source_target_pairs={{0,14},{1,3},{2,0},{3,5},{4,2},{5,7},{6,4},{7,9},{8,6},{9,11},{10,... | collective-permute-start | bytes 786440 | tf_op jit(solution)/shard_map/ppermute | solution.py:351
  46.3 33.6 %copy-start.7 = (bf16[128,1024]{1,0:T(8,128)(2,1)}, bf16[128,1024]{1,0:T(8,128)(2,1)S(1)}, u32[]{:S(2)}) copy-start(bf16[128,1024]{1,0:T(8,128)(2,1)S(1)} %collective-permute-done.1.refs_1_) | copy-start | bytes 786436
  46.3 10.0 %collective-permute-start.2 = (bf16[128,1024]{1,0:T(8,128)(2,1)S(1)}, bf16[128,1024]{1,0:T(8,128)(2,1)S(1)}, u32[]{:S(2)}, u32[]{:S(2)}) collective-permute-start(bf16[128,1024]{1,0:T(8,128)(2,1)S(1)} %collective-permute-done.1.refs_1_), channel_id=1, source_target_pairs={{0,2},{1,15},{2,4},{3,1},{4,6},{5,3},{6,8},{7,5},{8,10},{9,7},{10,... | collective-permute-start | bytes 786440 | tf_op jit(solution)/shard_map/ppermute | solution.py:350
  51.8 28.0 %copy-start.8 = (bf16[128,1024]{1,0:T(8,128)(2,1)}, bf16[128,1024]{1,0:T(8,128)(2,1)S(1)}, u32[]{:S(2)}) copy-start(bf16[128,1024]{1,0:T(8,128)(2,1)S(1)} %collective-permute-done.5.refs_2_) | copy-start | bytes 786436
  51.8 9.5 %collective-permute-start.6 = (bf16[128,1024]{1,0:T(8,128)(2,1)S(1)}, bf16[128,1024]{1,0:T(8,128)(2,1)S(1)}, u32[]{:S(2)}, u32[]{:S(2)}) collective-permute-start(bf16[128,1024]{1,0:T(8,128)(2,1)S(1)} %collective-permute-done.5.refs_2_), channel_id=1, source_target_pairs={{0,14},{1,3},{2,0},{3,5},{4,2},{5,7},{6,4},{7,9},{8,6},{9,11},{10,... | collective-permute-start | bytes 786440 | tf_op jit(solution)/shard_map/ppermute | solution.py:351
  56.3 23.6 %copy-start.9 = (bf16[128,1024]{1,0:T(8,128)(2,1)}, bf16[128,1024]{1,0:T(8,128)(2,1)S(1)}, u32[]{:S(2)}) copy-start(bf16[128,1024]{1,0:T(8,128)(2,1)S(1)} %collective-permute-done.2.refs_3_) | copy-start | bytes 786436
  56.3 10.8 %collective-permute-start.3 = (bf16[128,1024]{1,0:T(8,128)(2,1)S(1)}, bf16[128,1024]{1,0:T(8,128)(2,1)S(1)}, u32[]{:S(2)}, u32[]{:S(2)}) collective-permute-start(bf16[128,1024]{1,0:T(8,128)(2,1)S(1)} %collective-permute-done.2.refs_3_), channel_id=1, source_target_pairs={{0,2},{1,15},{2,4},{3,1},{4,6},{5,3},{6,8},{7,5},{8,10},{9,7},{10,... | collective-permute-start | bytes 786440 | tf_op jit(solution)/shard_map/ppermute | solution.py:350
  61.4 11.0 %copy-start.10 = (bf16[128,1024]{1,0:T(8,128)(2,1)}, bf16[128,1024]{1,0:T(8,128)(2,1)S(1)}, u32[]{:S(2)}) copy-start(bf16[128,1024]{1,0:T(8,128)(2,1)S(1)} %collective-permute-done.6.refs_4_) | copy-start | bytes 786436
  61.4 11.0 %collective-permute-start.7 = (bf16[128,1024]{1,0:T(8,128)(2,1)S(1)}, bf16[128,1024]{1,0:T(8,128)(2,1)S(1)}, u32[]{:S(2)}, u32[]{:S(2)}) collective-permute-start(bf16[128,1024]{1,0:T(8,128)(2,1)S(1)} %collective-permute-done.6.refs_4_), channel_id=1, source_target_pairs={{0,14},{1,3},{2,0},{3,5},{4,2},{5,7},{6,4},{7,9},{8,6},{9,11},{10,... | collective-permute-start | bytes 786440 | tf_op jit(solution)/shard_map/ppermute | solution.py:351
  67.1 12.8 %copy-start.5 = (bf16[128,1024]{1,0:T(8,128)(2,1)}, bf16[128,1024]{1,0:T(8,128)(2,1)S(1)}, u32[]{:S(2)}) copy-start(bf16[128,1024]{1,0:T(8,128)(2,1)S(1)} %collective-permute-done.3.refs_5_) | copy-start | bytes 786436
  67.1 7.5 %collective-permute-start.4 = (bf16[64,1024]{1,0:T(8,128)(2,1)S(1)}, bf16[64,1024]{1,0:T(8,128)(2,1)S(1)}, u32[]{:S(2)}, u32[]{:S(2)}) collective-permute-start(bf16[64,1024]{1,0:T(8,128)(2,1)S(1)} %slice.8), channel_id=1, source_target_pairs={{0,2},{1,15},{2,4},{3,1},{4,6},{5,3},{6,8},{7,5},{8,10},{9,7},{10,... | collective-permute-start | bytes 393224 | tf_op jit(solution)/shard_map/ppermute | solution.py:353
  72.4 7.5 %copy-start.6 = (bf16[128,1024]{1,0:T(8,128)(2,1)}, bf16[128,1024]{1,0:T(8,128)(2,1)S(1)}, u32[]{:S(2)}) copy-start(bf16[128,1024]{1,0:T(8,128)(2,1)S(1)} %collective-permute-done.7.refs_6_) | copy-start | bytes 786436
  72.4 17.5 %copy-start.2 = (s32[32,1,16]{0,2,1:T(8,128)S(1)}, s32[32,1,16]{0,2,1:T(8,128)}, u32[]{:S(2)}) copy-start(s32[32,1,16]{0,2,1:T(8,128)} %param.5) | copy-start | bytes 6148
  72.5 7.4 %collective-permute-start.8 = (bf16[64,1024]{1,0:T(8,128)(2,1)S(1)}, bf16[64,1024]{1,0:T(8,128)(2,1)S(1)}, u32[]{:S(2)}, u32[]{:S(2)}) collective-permute-start(bf16[64,1024]{1,0:T(8,128)(2,1)S(1)} %slice.9), channel_id=1, source_target_pairs={{0,14},{1,3},{2,0},{3,5},{4,2},{5,7},{6,4},{7,9},{8,6},{9,11},{10,... | collective-permute-start | bytes 393224 | tf_op jit(solution)/shard_map/ppermute | solution.py:353
  82.1 10.4 %collective-permute-start.9 = (f32[264,1024]{1,0:T(8,128)S(1)}, f32[264,1024]{1,0:T(8,128)}, u32[]{:S(2)}, u32[]{:S(2)}) collective-permute-start(f32[264,1024]{1,0:T(8,128)S(1)} %shard_map.49.sent_ref), channel_id=1, source_target_pairs={{0,1},{1,0},{2,3},{3,2},{4,5},{5,4},{6,7},{7,6},{8,9},{9,8},{10,11... | collective-permute-start | bytes 3244040 | tf_op jit(solution)/shard_map/ppermute | solution.py:373
  90.3 2.2 %copy-start.3 = (s32[1024]{0:T(1024)S(1)}, s32[1024]{0:T(1024)}, u32[]{:S(2)}) copy-start(s32[1024]{0:T(1024)} %param.6) | copy-start | bytes 12292
  92.6 23.3 %copy-start = (f32[256,256]{1,0:T(8,128)S(1)}, f32[256,256]{1,0:T(8,128)}, u32[]{:S(2)}) copy-start(f32[256,256]{1,0:T(8,128)} %pre_ref.3) | copy-start | bytes 786436

commit v7 on v6

--- a/solution.py
+++ b/solution.py
@@ -24,7 +24,7 @@
 WIDTH = N_PLANE * SLICE
 F = 2048
 N_Y = 8
-OFFSETS = (0, -1, 1, -2, 2, -3, 3, 4)
+OFFSETS = (0, -1, 1, -2, 2, -3, 3, -4)
 EXAMPLES = ROWS * N_EX
 
 EX = ("z", "xh")
@@ -73,36 +73,36 @@
     )(*args)
 
 
-def pick_kernel(spot_ref, index_ref, ft_hbm, out_ref, mine_ref, ft_ref, sem):
+def pick_kernel(own_ref, other_ref, ft_hbm, out_ref, ft_ref, sem):
     copy = pltpu.make_async_copy(ft_hbm, ft_ref, sem)
     copy.start()
-    core, base = spot_ref[3], spot_ref[4]
-    mine_ref[...] = (iota((4, 128), 1) == iota((4, 128), 0) + spot_ref[2] * 4).astype(F32)
     lane = iota((OWN, ROWS), 1)
-    index = index_ref[...]
-    blocks = iota((OWN, N_FEAT), 1)
-
-    def mask(block):
-        col = jnp.sum(jnp.where(blocks == block, index, 0), axis=1, keepdims=True) - base
-        return (lane == col).astype(F32).astype(BF16)
-
-    def chosen(side, table):
-        masks = jnp.concatenate([mask(2 * p + side) for p in range(N_PLANE)], axis=0)
-        return lax.dot_general(masks, table, LANES, preferred_element_type=F32)
-
+    pair = iota((OWN, N_FEAT), 1) >> 1
+
+    def masks(index_ref):
+        index = index_ref[...]
+        parts = []
+        for p in range(N_PLANE):
+            col = jnp.max(jnp.where(pair == p, index, -1), axis=1, keepdims=True)
+            parts.append((lane == col).astype(F32).astype(BF16))
+        return jnp.concatenate(parts, axis=0)
+
+    own, other = masks(own_ref), masks(other_ref)
     copy.wait()
     ft = ft_ref[...]
     zero = jnp.zeros_like(ft)
-    both = chosen(core, jnp.concatenate([ft, zero], axis=0)) + chosen(1 - core, jnp.concatenate([zero, ft], axis=0))
+    both = lax.dot_general(own, jnp.concatenate([ft, zero], axis=0), LANES, preferred_element_type=F32)
+    both += lax.dot_general(other, jnp.concatenate([zero, ft], axis=0), LANES, preferred_element_type=F32)
     out_ref[...] = both.astype(BF16).reshape(N_PLANE, OWN, 2 * SLICE)
 
 
-def spread_kernel(spot_ref, in_ref, out_ref):
+def spread_kernel(in_ref, out_ref, mine_ref):
+    side, y = lax.axis_index("xl"), lax.axis_index("y")
+    group = 2 * side + (y >> 2)
+    mine_ref[...] = (iota((4, 128), 1) == iota((4, 128), 0) + group * 4).astype(F32)
     low = iota((OWN, 128), 1) < SLICE
-    side, y = spot_ref[0], spot_ref[1]
-    sign = 1 - 2 * spot_ref[3]
     for t, offset in enumerate(OFFSETS):
-        row = lax.rem(y + N_Y + sign * offset, N_Y)
+        row = lax.rem(y + (offset + N_Y), N_Y)
         a = in_ref[side * N_Y + row].astype(F32)
         b = in_ref[(1 - side) * N_Y + row].astype(F32)
         own = jnp.where(low, a, pltpu.roll(b, SLICE, 1)).astype(BF16)
@@ -117,27 +117,31 @@
     return iota((BLOCK, BLOCK), 0) == iota((BLOCK, BLOCK), 1)
 
 
-def half_dots(ft, cen_ref, first):
-    block = cen_ref[:, first : first + OWN, :].reshape(BLOCK, WIDTH)
-    squares = jnp.sum(jnp.square(block.astype(F32)), axis=1, keepdims=True)
-    squares = jnp.sum(jnp.where(diagonal(), squares, 0.0), axis=0, keepdims=True)
-    return jnp.dot(block, ft, preferred_element_type=F32), squares
-
-
-def load_features(chunk_hbm, near_ref, far_ref, ft_ref, sems):
+def load_features(chunk_hbm, last_ref, ft_ref, sems):
     copies = []
     for i, chunk in enumerate(chunk_hbm):
         copies.append(pltpu.make_async_copy(chunk, ft_ref.at[128 * i : 128 * i + 128], sems.at[i]))
         copies[-1].start()
-    first = 128 * len(chunk_hbm)
-    ft_ref[first : first + SLICE] = near_ref[...]
-    ft_ref[first + SLICE : first + 2 * SLICE] = far_ref[...]
+    ft_ref[128 * len(chunk_hbm) :] = last_ref[...]
     return copies
 
 
-def other_kernel(near_ref, far_ref, cen_ref, *refs):
+def centre_squares(cen_ref, first):
+    block = cen_ref[:, first : first + OWN, :].reshape(BLOCK, WIDTH)
+    squares = jnp.sum(jnp.square(block.astype(F32)), axis=1, keepdims=True)
+    return jnp.sum(jnp.where(diagonal(), squares, 0.0), axis=0, keepdims=True)
+
+
+def centre_dots(cen_ref, first, ft_ref):
+    block = cen_ref[:, first : first + OWN, :].reshape(BLOCK, WIDTH)
+    return jnp.dot(block, ft_ref[...], preferred_element_type=F32)
+
+
+def other_kernel(last_ref, cen_ref, *refs):
     *chunk_hbm, out_ref, ft_ref, sems = refs
-    copies = load_features(chunk_hbm, near_ref, far_ref, ft_ref, sems)
+    copies = load_features(chunk_hbm, last_ref, ft_ref, sems)
+    out_ref[BLOCK : BLOCK + 8, :] = jnp.zeros((8, ROWS), F32)
+    out_ref[BLOCK + 1 : BLOCK + 2, 0:BLOCK] = centre_squares(cen_ref, OWN)
 
     def squares(start):
         return jnp.sum(jnp.square(ft_ref[start : start + 128].astype(F32)), axis=0, keepdims=True)
@@ -146,20 +150,17 @@
     for i, copy in enumerate(copies):
         copy.wait()
         row_sq += squares(128 * i)
-    out_ref[BLOCK : BLOCK + 8, :] = jnp.zeros((8, ROWS), F32)
     out_ref[BLOCK : BLOCK + 1, :] = row_sq
-    dots, squares = half_dots(ft_ref[...], cen_ref, OWN)
-    out_ref[0:BLOCK, :] = dots
-    out_ref[BLOCK + 1 : BLOCK + 2, 0:BLOCK] = squares
-
-
-def own_kernel(near_ref, far_ref, cen_ref, *refs):
+    out_ref[0:BLOCK, :] = centre_dots(cen_ref, OWN, ft_ref)
+
+
+def own_kernel(last_ref, cen_ref, *refs):
     *chunk_hbm, dots_ref, squares_ref, ft_ref, sems = refs
-    for copy in load_features(chunk_hbm, near_ref, far_ref, ft_ref, sems):
+    copies = load_features(chunk_hbm, last_ref, ft_ref, sems)
+    squares_ref[...] = jnp.broadcast_to(centre_squares(cen_ref, 0), (8, BLOCK))
+    for copy in copies:
         copy.wait()
-    dots, squares = half_dots(ft_ref[...], cen_ref, 0)
-    dots_ref[...] = dots
-    squares_ref[...] = jnp.broadcast_to(squares, (8, BLOCK))
+    dots_ref[...] = centre_dots(cen_ref, 0, ft_ref)
 
 
 def split2(x):
@@ -180,37 +181,42 @@
 
 
 def panel_kernel(
-    dots_ref, squares_ref, sent_ref, labels_ref, loc_ref, recv_hbm, high_ref, low_ref, place_ref, out_ref, recv_ref, sem
+    dots_ref, squares_ref, sent_ref, labels_ref, loc_ref, recv_hbm, high_ref, low_ref, place_ref, out_ref, recv_ref, sems
 ):
-    copy = pltpu.make_async_copy(recv_hbm, recv_ref, sem)
-    copy.start()
+    step = BLOCK // 4
+    spans = [slice(BLOCK, BLOCK + 8)] + [slice(step * t, step * t + step) for t in range(4)]
+    copies = [pltpu.make_async_copy(recv_hbm.at[r], recv_ref.at[r], sems.at[i]) for i, r in enumerate(spans)]
+    for copy in copies:
+        copy.start()
     place_ref[...] = (iota((BLOCK, ROWS), 1) == loc_ref[...]).astype(F32).astype(BF16)
     hit = iota((CLASSES, ROWS), 0) == labels_ref[...]
     targets = jnp.where(hit, CLASSES - 1.0, -1.0).astype(BF16)
-    copy.wait()
+    copies[0].wait()
     row_sq = sent_ref[BLOCK : BLOCK + 1, :] + recv_ref[BLOCK : BLOCK + 1, :]
     centre_sq = squares_ref[0:1, :] + recv_ref[BLOCK + 1 : BLOCK + 2, 0:BLOCK]
     centre_sq = jnp.sum(jnp.where(diagonal(), centre_sq, 0.0), axis=1, keepdims=True)
     row_scale = lax.rsqrt(row_sq / F + EPS)
     centre_scale = lax.rsqrt(centre_sq / F + EPS)
-    dots = dots_ref[...] + recv_ref[0:BLOCK, :]
-    cosine = jnp.clip(dots * row_scale * centre_scale, -1.0, 1.0)
-    high, low = split2(jnp.exp(GAMMA * (cosine - 1.0)))
-    high_ref[...] = high
-    low_ref[...] = low
-    rhs = (dot_t(targets, high, None) + dot_t(targets, low, None)) / EXAMPLES
+    for copy, r in zip(copies[1:], spans[1:]):
+        copy.wait()
+        dots = dots_ref[r] + recv_ref[r]
+        cosine = jnp.clip(dots * row_scale * centre_scale[r], -1.0, 1.0)
+        high, low = split2(jnp.exp(GAMMA * (cosine - 1.0)))
+        high_ref[r] = high
+        low_ref[r] = low
+    rhs = (dot_t(targets, high_ref[...], None) + dot_t(targets, low_ref[...], None)) / EXAMPLES
     for i in range(N_EX):
         out_ref[i] = rhs
 
 
-def apply_panel(vec, high_ref, low_ref, place_ref):
+def times(parts, matrix_ref):
+    return fold3(jnp.dot(parts, matrix_ref[...], preferred_element_type=F32))
+
+
+def apply_both(vec, high_ref, low_ref, place_ref):
     parts = split3(vec)
-
-    def times(matrix):
-        return fold3(jnp.dot(parts, matrix, preferred_element_type=F32))
-
-    k = times(high_ref[...]) + times(low_ref[...])
-    return k, k / EXAMPLES + LAMBDA * times(place_ref[...])
+    k = times(parts, high_ref) + times(parts, low_ref)
+    return k, k / EXAMPLES + LAMBDA * times(parts, place_ref)
 
 
 def apply_normal(k, high_ref, low_ref, place_ref):
@@ -253,7 +259,7 @@
     u = dot_t(rhs, pre_ref[...])
     rhs_ref[...] = rhs
     u_ref[...] = u
-    k, g = apply_panel(u, high_ref, low_ref, place_ref)
+    k, g = apply_both(u, high_ref, low_ref, place_ref)
     put_chunks(out_ref, k, 2, 0)
     put_chunks(out_ref, g, 2, 1)
 
@@ -278,7 +284,7 @@
     v = dot_t(image, pre_ref[...])
     image_ref[...] = image
     v_ref[...] = v
-    k, g = apply_panel(v, high_ref, low_ref, place_ref)
+    k, g = apply_both(v, high_ref, low_ref, place_ref)
     put_chunks(out_ref, k, 3, 0)
     put_chunks(out_ref, g, 3, 1)
     u = u_ref[...]
@@ -290,48 +296,53 @@
         out_ref[s * 3 + 2] = row
 
 
+def scalars(row):
+    rz = to_col(row, CLASSES, 0)
+    uu = to_col(row, CLASSES, CLASSES)
+    vu = to_col(row, CLASSES, 2 * CLASSES)
+    alpha = rz / uu
+    return rz, uu, vu, alpha, alpha * (vu / uu) - 1.0
+
+
 def step_kernel(mine_ref, recv_ref, chunk_ref, rhs_ref, u_ref, image_ref, v_ref, scal_ref, out_ref):
     row = sum_slot(recv_ref, 3, 2)[0:1]
     scal_ref[...] = jnp.broadcast_to(row, (8, 128))
-    alpha = to_col(row, CLASSES, 0) / to_col(row, CLASSES, CLASSES)
+    _, _, _, alpha, guess = scalars(row)
     residual = rhs_ref[...] - alpha * image_ref[...]
     z = u_ref[...] - alpha * v_ref[...]
     rz = to_row(jnp.sum(residual * z, axis=1, keepdims=True))
-    alpha_row = to_row(alpha)
     mine = mine_ref[...]
-    alpha_mine = jnp.sum(mine * alpha_row, axis=1, keepdims=True)
-    kz = chunk_ref[0] - alpha_mine * sum_slot(recv_ref, 3, 0)
-    gz = chunk_ref[1] - alpha_mine * sum_slot(recv_ref, 3, 1)
-    quad = jnp.sum(kz * gz, axis=1, keepdims=True)
+    alpha_mine = jnp.sum(mine * to_row(alpha), axis=1, keepdims=True)
+    guess_mine = jnp.sum(mine * to_row(guess), axis=1, keepdims=True)
+    k, g = chunk_ref[0], chunk_ref[1]
+    kd = (k - alpha_mine * sum_slot(recv_ref, 3, 0)) + guess_mine * k
+    gd = (g - alpha_mine * sum_slot(recv_ref, 3, 1)) + guess_mine * g
+    quad = jnp.sum(kd * gd, axis=1, keepdims=True)
     quad_row = jnp.sum(mine * quad, axis=0, keepdims=True)
     which = iota((4, 128), 0)
     tail = jnp.where(which == 0, rz, jnp.where(which == 1, quad_row, 0.0))
     for s in range(N_FEAT):
-        out_ref[s * 2] = kz
+        out_ref[s * 2] = kd
         out_ref[s * 2 + 1] = tail
 
 
-def gather_kernel(recv_ref, kz_ref, tail_ref, out_ref):
-    take_chunks(recv_ref, 2, kz_ref)
+def gather_kernel(recv_ref, kd_ref, tail_ref, out_ref):
+    take_chunks(recv_ref, 2, kd_ref)
     tail = sum_slot(recv_ref, 2, 1)
     tail_ref[...] = tail
     for i in range(N_EX):
         out_ref[i] = tail[1:2]
 
 
-def last_kernel(recv_ref, tail_ref, scal_ref, k_ref, kz_ref, out_ref):
+def last_kernel(recv_ref, tail_ref, scal_ref, k_ref, kd_ref, out_ref):
     quad = to_col(total(recv_ref), CLASSES)
     rz_next = to_col(tail_ref[0:1, :], CLASSES)
-    row = scal_ref[0:1, :]
-    rz = to_col(row, CLASSES, 0)
-    uu = to_col(row, CLASSES, CLASSES)
-    vu = to_col(row, CLASSES, 2 * CLASSES)
-    alpha = rz / uu
-    beta = rz_next / rz
-    cross = uu - alpha * vu
-    alpha_next = rz_next / (quad + 2.0 * beta * cross + beta * beta * uu)
+    rz, uu, vu, alpha, guess = scalars(scal_ref[0:1, :])
+    delta = rz_next / rz - guess
+    slope = (uu - alpha * vu) + guess * uu
+    alpha_next = rz_next / (quad + delta * (2.0 * slope + delta * uu))
     k = k_ref[...]
-    out_ref[...] = alpha * k + alpha_next * (kz_ref[...] + beta * k)
+    out_ref[...] = alpha * k + alpha_next * (kd_ref[...] + delta * k)
 
 
 def predict(features, centre_index, labels, precond):
@@ -342,23 +353,24 @@
     ft_local = features.T
     swapped = lax.ppermute(ft_local, "xl", [(0, 1), (1, 0)])
     here = jnp.concatenate([ft_local, swapped], axis=0)
-    up = [(2 * i + c, 2 * ((i + 1 - 2 * c) % N_Y) + c) for i in range(N_Y) for c in range(2)]
-    down = [(2 * i + c, 2 * ((i - 1 + 2 * c) % N_Y) + c) for i in range(N_Y) for c in range(2)]
+    up = [(i, (i + 1) % N_Y) for i in range(N_Y)]
+    down = [(i, (i - 1) % N_Y) for i in range(N_Y)]
     chunks = [here]
     below = above = here
     for _ in range(3):
-        below = lax.ppermute(below, ("y", "c"), up)
-        above = lax.ppermute(above, ("y", "c"), down)
+        below = lax.ppermute(below, "y", up)
+        above = lax.ppermute(above, "y", down)
         chunks += [below, above]
-    chunks += [lax.ppermute(below[:SLICE], ("y", "c"), up), lax.ppermute(above[SLICE:], ("y", "c"), down)]
-
-    spot = jnp.stack([lax.axis_index("xl"), lax.axis_index("y"), feat_index // 8, core, ex_index * ROWS])
-    picked, mine = call(
-        pick_kernel, [((N_PLANE, OWN, 2 * SLICE), BF16), ((4, 128), F32)], spot, centre_index[:, 0, :].T, ft_local, smem=1, hbm=1,
-        scratch=[pltpu.VMEM((SLICE, ROWS), BF16), pltpu.SemaphoreType.DMA],
+    chunks.append(lax.ppermute(below, "y", up))
+
+    index = centre_index[:, 0, :].T - ex_index * ROWS
+    ours = (iota((OWN, N_FEAT), 1) & 1) == core
+    picked = call(
+        pick_kernel, ((N_PLANE, OWN, 2 * SLICE), BF16), jnp.where(ours, index, -1), jnp.where(ours, -1, index), ft_local,
+        hbm=1, scratch=[pltpu.VMEM((SLICE, ROWS), BF16), pltpu.SemaphoreType.DMA],
     )
     picked = lax.all_to_all(picked, PLANE, 0, 0, tiled=True)
-    spread = call(spread_kernel, ((N_EX, 2 * OWN, WIDTH), BF16), spot, picked, smem=1)
+    spread, mine = call(spread_kernel, [((N_EX, 2 * OWN, WIDTH), BF16), ((4, 128), F32)], picked)
     cen = lax.all_to_all(spread, EX, 0, 0, tiled=True)
 
     own_rows = lax.dynamic_index_in_dim(local, feat_index, 0, keepdims=False)
@@ -366,8 +378,8 @@
     loc = jnp.where(slot, own_rows[None, :], -1).reshape(BLOCK, 1)
 
     dots_t = ((BLOCK, ROWS), F32)
-    operands = (*chunks[-2:], cen, *chunks[:-2])
-    still = len(chunks) - 2
+    operands = (chunks[-1], cen, *chunks[:-1])
+    still = len(chunks) - 1
     scratch = [pltpu.VMEM((WIDTH, ROWS), BF16), pltpu.SemaphoreType.DMA((still,))]
     sent = call(other_kernel, ((BLOCK + 8, ROWS), F32), *operands, hbm=still, scratch=scratch)
     got = lax.ppermute(sent, "c", [(0, 1), (1, 0)])
@@ -376,7 +388,7 @@
     high, low, place, part = call(
         panel_kernel, [half_t, half_t, half_t, ((N_EX, CLASSES, BLOCK), F32)],
         own, own_sq, sent, labels.reshape(1, ROWS), loc, got, hbm=1,
-        scratch=[pltpu.VMEM(sent.shape, F32), pltpu.SemaphoreType.DMA],
+        scratch=[pltpu.VMEM(sent.shape, F32), pltpu.SemaphoreType.DMA((5,))],
     )
     vec = ((CLASSES, BLOCK), F32)
     part = lax.all_to_all(part, EX, 0, 0, tiled=True)
@@ -396,9 +408,9 @@
         mine, part, chunk, rhs, u, image, v,
     )
     part = lax.all_to_all(part, FEAT, 0, 0, tiled=True)
-    kz, tail, part = call(gather_kernel, [((CLASSES, ROWS), F32), ((4, 128), F32), ((N_EX, 1, 128), F32)], part)
+    kd, tail, part = call(gather_kernel, [((CLASSES, ROWS), F32), ((4, 128), F32), ((N_EX, 1, 128), F32)], part)
     part = lax.all_to_all(part, EX, 0, 0, tiled=True)
-    out = call(last_kernel, ((CLASSES, ROWS), F32), part, tail, scal, k, kz, space=jax.ShapeDtypeStruct)
+    out = call(last_kernel, ((CLASSES, ROWS), F32), part, tail, scal, k, kd, space=jax.ShapeDtypeStruct)
     return out.T
 
 

time: 205 us -> 196 us (0.956)
  blocking collectives: 121 us -> 118 us
  starting transfers between devices: 47.9 us -> 45.4 us
  waiting for transfers between devices: 19 us -> 16.7 us
    ppermute x8 -> x7, starting transfers between devices: 25.7 us -> 21.4 us  [the longest x3 13 us: predict(): above = lax.ppermute(above, 'y', down)]
    all_to_all x4, blocking collectives: 58.1 us -> 55.6 us  [predict(): part = lax.all_to_all(part, FEAT, 0, 0, tiled=True)]
    ppermute x8 -> x7, waiting for transfers between devices: 15.2 us -> 12.9 us  [the longest x1 6.89 us: predict(): chunks.append(lax.ppermute(below, 'y', up))]
  transfers between devices with their start and end apart: 11 -> 10, of which waited for: 6 -> 5; matrix products, arithmetic and copies ran while one was open for 0% -> 0% of each run, Pallas kernels for 1% -> 1%
where the time goes in v7:
time: 196 us; the launch traced here: 195 us
  blocking collectives  118 us (60%)
  starting transfers between devices  45.4 us (23%)
  waiting for transfers between devices  16.7 us (9%)
  Pallas kernels  12.6 us (6%)
    all_to_all x4, blocking collectives, predict(): part = lax.all_to_all(part, FEAT, 0, 0, tiled=True)  55.6 us
    all_to_all x3, blocking collectives, predict(): part = lax.all_to_all(part, EX, 0, 0, tiled=True)  47 us
    all_to_all x1, blocking collectives, predict(): picked = lax.all_to_all(picked, PLANE, 0, 0, tiled=True)  15.8 us
    ppermute x3, starting transfers between devices, predict(): above = lax.ppermute(above, 'y', down)  13 us
    pallas_call x12, Pallas kernels, call(): pl.pallas_call(kernel, out_shape=[space(s, d) for s, d in outs] if many e...  12.6 us
    all_to_all x1, starting transfers between devices, predict(): cen = lax.all_to_all(spread, EX, 0, 0, tiled=True)  12.3 us
    ppermute x1, starting transfers between devices, predict(): got = lax.ppermute(sent, 'c', [(0, 1), (1, 0)])  9.77 us
    ppermute x1, waiting for transfers between devices, predict(): chunks.append(lax.ppermute(below, 'y', up))  6.89 us
  transfers between devices with their start and end apart: 10, of which 5 were waited for; matrix products, arithmetic and copies ran while one was open for 0% of the time, Pallas kernels for 1%

profile of v7, /device:TPU:1, one launch (start us, length us, event | category | flops | bytes accessed | tf_op | source)
XLA Modules:
  0.0 194.6 jit_solution(6337316819400625442)
XLA Ops:
  2.1 15.8 %all_to_all.45.in_ref = bf16[16,16,128]{2,1,0:T(8,128)(2,1)S(1)} all-to-all(bf16[16,16,128]{2,1,0:T(8,128)(2,1)S(1)} %shard_map.46), channel_id=1, replica_groups=mesh['z'=8,'xh'=2,'xl'=2,'y'=8,'c'=2] {'xl','y'}, dimensions={0} | all-to-all | bytes 131072 | tf_op jit(solution)/shard_map/all_to_all | solution.py:372
  19.3 12.3 %all-to-all-start.1 = ((bf16[16,32,1024]{2,1,0:T(8,128)(2,1)}), bf16[16,32,1024]{2,1,0:T(8,128)(2,1)S(1)}, u32[]{:S(2)}, u32[]{:S(2)}) async-start(bf16[16,32,1024]{2,1,0:T(8,128)(2,1)} %get-tuple-element.29), calls=%async_computation.1 | async-start | bytes 2097152 | tf_op jit(solution)/shard_map/all_to_all | solution.py:374
  31.6 1.9 collective-permute-start
  33.5 3.8 %collective-permute-done = bf16[64,1024]{1,0:T(8,128)(2,1)S(1)} collective-permute-done((bf16[64,1024]{1,0:T(8,128)(2,1)S(1)}, bf16[64,1024]{1,0:T(8,128)(2,1)S(1)}, u32[]{:S(2)}, u32[]{:S(2)}) %collective-permute-start) | collective-permute-done | bytes 131104 | tf_op jit(solution)/shard_map/ppermute | solution.py:354
  37.3 2.6 %collective-permute-start.1 = (bf16[128,1024]{1,0:T(8,128)(2,1)S(1)}, bf16[128,1024]{1,0:T(8,128)(2,1)S(1)}, u32[]{:S(2)}, u32[]{:S(2)}) collective-permute-start(bf16[128,1024]{1,0:T(8,128)(2,1)S(1)} %pad_maximum_fusion.refs_0_), channel_id=1, source_target_pairs={{0,2},{2,4},{4,6},{6,8},{8,10},{10,12},{12,14},{14,0},{1,3},{3,5},... | collective-permute-start | bytes 786440 | tf_op jit(solution)/shard_map/ppermute | solution.py:361
  40.0 3.9 %collective-permute-start.5 = (bf16[128,1024]{1,0:T(8,128)(2,1)S(1)}, bf16[128,1024]{1,0:T(8,128)(2,1)S(1)}, u32[]{:S(2)}, u32[]{:S(2)}) collective-permute-start(bf16[128,1024]{1,0:T(8,128)(2,1)S(1)} %pad_maximum_fusion.refs_0_), channel_id=1, source_target_pairs={{0,14},{2,0},{4,2},{6,4},{8,6},{10,8},{12,10},{14,12},{1,15},{3,1}... | collective-permute-start | bytes 786440 | tf_op jit(solution)/shard_map/ppermute | solution.py:362
  43.9 2.1 %collective-permute-done.1.refs_1_ = bf16[128,1024]{1,0:T(8,128)(2,1)S(1)} collective-permute-done((bf16[128,1024]{1,0:T(8,128)(2,1)S(1)}, bf16[128,1024]{1,0:T(8,128)(2,1)S(1)}, u32[]{:S(2)}, u32[]{:S(2)}) %collective-permute-start.1) | collective-permute-done | bytes 262176 | tf_op jit(solution)/shard_map/ppermute | solution.py:361
  46.0 1.9 collective-permute-start.2
  47.9 4.6 %collective-permute-start.6 = (bf16[128,1024]{1,0:T(8,128)(2,1)S(1)}, bf16[128,1024]{1,0:T(8,128)(2,1)S(1)}, u32[]{:S(2)}, u32[]{:S(2)}) collective-permute-start(bf16[128,1024]{1,0:T(8,128)(2,1)S(1)} %collective-permute-done.5.refs_2_), channel_id=1, source_target_pairs={{0,14},{2,0},{4,2},{6,4},{8,6},{10,8},{12,10},{14,12},{1,15},{3,1}... | collective-permute-start | bytes 786440 | tf_op jit(solution)/shard_map/ppermute | solution.py:362
  52.5 2.1 %collective-permute-done.2.refs_3_ = bf16[128,1024]{1,0:T(8,128)(2,1)S(1)} collective-permute-done((bf16[128,1024]{1,0:T(8,128)(2,1)S(1)}, bf16[128,1024]{1,0:T(8,128)(2,1)S(1)}, u32[]{:S(2)}, u32[]{:S(2)}) %collective-permute-start.2) | collective-permute-done | bytes 262176 | tf_op jit(solution)/shard_map/ppermute | solution.py:361
  54.6 1.9 collective-permute-start.3
  56.5 4.6 %collective-permute-start.7 = (bf16[128,1024]{1,0:T(8,128)(2,1)S(1)}, bf16[128,1024]{1,0:T(8,128)(2,1)S(1)}, u32[]{:S(2)}, u32[]{:S(2)}) collective-permute-start(bf16[128,1024]{1,0:T(8,128)(2,1)S(1)} %collective-permute-done.6.refs_4_), channel_id=1, source_target_pairs={{0,14},{2,0},{4,2},{6,4},{8,6},{10,8},{12,10},{14,12},{1,15},{3,1}... | collective-permute-start | bytes 786440 | tf_op jit(solution)/shard_map/ppermute | solution.py:362
  62.9 1.9 collective-permute-start.4
  64.8 6.9 %collective-permute-done.4.last_ref = bf16[128,1024]{1,0:T(8,128)(2,1)S(1)} collective-permute-done((bf16[128,1024]{1,0:T(8,128)(2,1)S(1)}, bf16[128,1024]{1,0:T(8,128)(2,1)S(1)}, u32[]{:S(2)}, u32[]{:S(2)}) %collective-permute-start.4) | collective-permute-done | bytes 262176 | tf_op jit(solution)/shard_map/ppermute | solution.py:364
  71.8 2.2 %shard_map.49.sent_ref = f32[264,1024]{1,0:T(8,128)S(1)} custom-call(bf16[128,1024]{1,0:T(8,128)(2,1)S(1)} %collective-permute-done.4.last_ref, bf16[16,32,1024]{2,1,0:T(8,128)(2,1)S(1)} %all-to-all-done.1.cen_ref, bf16[128,1024]{1,0:T(8,128)(2,1)} %copy-done.2, bf16[128,1024]{1,0:T(8,128)(2,1)} %copy-done.3, bf16[128,1024]{1,0:T(8,128)(2,1)} %copy-done.4, ...), custom_call_target="tpu_custom_call" | custom-call | tf_op jit(solution)/shard_map/pallas_call | solution.py:66
  74.0 9.8 %collective-permute-start.8 = (f32[264,1024]{1,0:T(8,128)S(1)}, f32[264,1024]{1,0:T(8,128)}, u32[]{:S(2)}, u32[]{:S(2)}) collective-permute-start(f32[264,1024]{1,0:T(8,128)S(1)} %shard_map.49.sent_ref), channel_id=1, source_target_pairs={{0,1},{1,0},{2,3},{3,2},{4,5},{5,4},{6,7},{7,6},{8,9},{9,8},{10,11... | collective-permute-start | bytes 3244040 | tf_op jit(solution)/shard_map/ppermute | solution.py:385
  84.2 2.2 %shard_map.48 = (f32[256,1024]{1,0:T(8,128)S(1)}, f32[8,256]{1,0:T(8,128)S(1)}) custom-call(bf16[128,1024]{1,0:T(8,128)(2,1)S(1)} %collective-permute-done.4.last_ref, bf16[16,32,1024]{2,1,0:T(8,128)(2,1)S(1)} %all-to-all-done.1.cen_ref, bf16[128,1024]{1,0:T(8,128)(2,1)} %copy-done.2, bf16[128,1024]{1,0:T(8,128)(2,1)} %copy-done.3, ...), custom_call_target="tpu_custom_call" | custom-call | tf_op jit(solution)/shard_map/pallas_call | solution.py:66
  88.2 21.3 %all_to_all.46.recv_ref = f32[16,16,256]{2,1,0:T(8,128)S(1)} all-to-all(f32[16,16,256]{2,1,0:T(8,128)S(1)} %get-tuple-element.32), channel_id=1, replica_groups=mesh['z'=8,'xh'=2,'xl'=2,'y'=8,'c'=2] {'z','xh'}, dimensions={0} | all-to-all | bytes 524288 | tf_op jit(solution)/shard_map/all_to_all | solution.py:394
  110.5 13.4 %all_to_all.47.recv_ref = f32[64,4,128]{2,1,0:T(4,128)S(1)} all-to-all(f32[64,4,128]{2,1,0:T(4,128)S(1)} %get-tuple-element.36), channel_id=1, replica_groups=mesh['z'=8,'xh'=2,'xl'=2,'y'=8,'c'=2] {'xl','y','c'}, dimensions={0} | all-to-all | bytes 262144 | tf_op jit(solution)/shard_map/all_to_all | solution.py:396
  123.9 12.5 %all_to_all.48.recv_ref = f32[32,4,128]{2,1,0:T(4,128)S(1)} all-to-all(f32[32,4,128]{2,1,0:T(4,128)S(1)} %get-tuple-element.37), channel_id=1, replica_groups=mesh['z'=8,'xh'=2,'xl'=2,'y'=8,'c'=2] {'xl','y','c'}, dimensions={0} | all-to-all | bytes 131072 | tf_op jit(solution)/shard_map/all_to_all | solution.py:398
  137.0 14.2 %all_to_all.49.recv_ref = f32[16,16,256]{2,1,0:T(8,128)S(1)} all-to-all(f32[16,16,256]{2,1,0:T(8,128)S(1)} %get-tuple-element.38), channel_id=1, replica_groups=mesh['z'=8,'xh'=2,'xl'=2,'y'=8,'c'=2] {'z','xh'}, dimensions={0} | all-to-all | bytes 524288 | tf_op jit(solution)/shard_map/all_to_all | solution.py:400
  152.3 16.2 %all_to_all.50.recv_ref = f32[96,4,128]{2,1,0:T(4,128)S(1)} all-to-all(f32[96,4,128]{2,1,0:T(4,128)S(1)} %get-tuple-element.41), channel_id=1, replica_groups=mesh['z'=8,'xh'=2,'xl'=2,'y'=8,'c'=2] {'xl','y','c'}, dimensions={0} | all-to-all | bytes 393216 | tf_op jit(solution)/shard_map/all_to_all | solution.py:405
  168.7 13.6 %all_to_all.51.recv_ref = f32[64,4,128]{2,1,0:T(4,128)S(1)} all-to-all(f32[64,4,128]{2,1,0:T(4,128)S(1)} %get-tuple-element.45), channel_id=1, replica_groups=mesh['z'=8,'xh'=2,'xl'=2,'y'=8,'c'=2] {'xl','y','c'}, dimensions={0} | all-to-all | bytes 262144 | tf_op jit(solution)/shard_map/all_to_all | solution.py:410
  182.4 11.4 %all_to_all.52.recv_ref = f32[16,1,128]{2,1,0:T(1,128)S(1)} all-to-all(f32[16,1,128]{2,1,0:T(1,128)S(1)} %get-tuple-element.46), channel_id=1, replica_groups=mesh['z'=8,'xh'=2,'xl'=2,'y'=8,'c'=2] {'z','xh'}, dimensions={0} | all-to-all | bytes 16384 | tf_op jit(solution)/shard_map/all_to_all | solution.py:412
  (44 shorter events, 11.2 us)
Async XLA Ops:
  17.9 13.7 %copy-start.9 = (bf16[1024,64]{0,1:T(8,128)(2,1)S(1)}, bf16[1024,64]{0,1:T(8,128)(2,1)}, u32[]{:S(2)}) copy-start(bf16[1024,64]{0,1:T(8,128)(2,1)} %param.4) | copy-start | bytes 393220
  19.3 52.5 %all-to-all-start.1 = ((bf16[16,32,1024]{2,1,0:T(8,128)(2,1)}), bf16[16,32,1024]{2,1,0:T(8,128)(2,1)S(1)}, u32[]{:S(2)}, u32[]{:S(2)}) async-start(bf16[16,32,1024]{2,1,0:T(8,128)(2,1)} %get-tuple-element.29), calls=%async_computation.1 | async-start | bytes 2097152 | tf_op jit(solution)/shard_map/all_to_all | solution.py:374
  31.6 5.7 %collective-permute-start = (bf16[64,1024]{1,0:T(8,128)(2,1)S(1)}, bf16[64,1024]{1,0:T(8,128)(2,1)S(1)}, u32[]{:S(2)}, u32[]{:S(2)}) collective-permute-start(bf16[64,1024]{1,0:T(8,128)(2,1)S(1)} %bitcast.16), channel_id=1, source_target_pairs={{0,16},{16,0},{1,17},{17,1},{2,18},{18,2},{3,19},{19,3},{4,20},{20... | collective-permute-start | bytes 393224 | tf_op jit(solution)/shard_map/ppermute | solution.py:354
  37.3 34.4 %copy-start.2 = (bf16[128,1024]{1,0:T(8,128)(2,1)}, bf16[128,1024]{1,0:T(8,128)(2,1)S(1)}, u32[]{:S(2)}) copy-start(bf16[128,1024]{1,0:T(8,128)(2,1)S(1)} %pad_maximum_fusion.refs_0_) | copy-start | bytes 786436
  37.3 8.6 %collective-permute-start.1 = (bf16[128,1024]{1,0:T(8,128)(2,1)S(1)}, bf16[128,1024]{1,0:T(8,128)(2,1)S(1)}, u32[]{:S(2)}, u32[]{:S(2)}) collective-permute-start(bf16[128,1024]{1,0:T(8,128)(2,1)S(1)} %pad_maximum_fusion.refs_0_), channel_id=1, source_target_pairs={{0,2},{2,4},{4,6},{6,8},{8,10},{10,12},{12,14},{14,0},{1,3},{3,5},... | collective-permute-start | bytes 786440 | tf_op jit(solution)/shard_map/ppermute | solution.py:361
  40.0 7.9 %collective-permute-start.5 = (bf16[128,1024]{1,0:T(8,128)(2,1)S(1)}, bf16[128,1024]{1,0:T(8,128)(2,1)S(1)}, u32[]{:S(2)}, u32[]{:S(2)}) collective-permute-start(bf16[128,1024]{1,0:T(8,128)(2,1)S(1)} %pad_maximum_fusion.refs_0_), channel_id=1, source_target_pairs={{0,14},{2,0},{4,2},{6,4},{8,6},{10,8},{12,10},{14,12},{1,15},{3,1}... | collective-permute-start | bytes 786440 | tf_op jit(solution)/shard_map/ppermute | solution.py:362
  46.0 25.8 %copy-start.3 = (bf16[128,1024]{1,0:T(8,128)(2,1)}, bf16[128,1024]{1,0:T(8,128)(2,1)S(1)}, u32[]{:S(2)}) copy-start(bf16[128,1024]{1,0:T(8,128)(2,1)S(1)} %collective-permute-done.1.refs_1_) | copy-start | bytes 786436
  46.0 8.6 %collective-permute-start.2 = (bf16[128,1024]{1,0:T(8,128)(2,1)S(1)}, bf16[128,1024]{1,0:T(8,128)(2,1)S(1)}, u32[]{:S(2)}, u32[]{:S(2)}) collective-permute-start(bf16[128,1024]{1,0:T(8,128)(2,1)S(1)} %collective-permute-done.1.refs_1_), channel_id=1, source_target_pairs={{0,2},{2,4},{4,6},{6,8},{8,10},{10,12},{12,14},{14,0},{1,3},{3,5},... | collective-permute-start | bytes 786440 | tf_op jit(solution)/shard_map/ppermute | solution.py:361
  47.9 23.9 %copy-start.4 = (bf16[128,1024]{1,0:T(8,128)(2,1)}, bf16[128,1024]{1,0:T(8,128)(2,1)S(1)}, u32[]{:S(2)}) copy-start(bf16[128,1024]{1,0:T(8,128)(2,1)S(1)} %collective-permute-done.5.refs_2_) | copy-start | bytes 786436
  47.9 8.6 %collective-permute-start.6 = (bf16[128,1024]{1,0:T(8,128)(2,1)S(1)}, bf16[128,1024]{1,0:T(8,128)(2,1)S(1)}, u32[]{:S(2)}, u32[]{:S(2)}) collective-permute-start(bf16[128,1024]{1,0:T(8,128)(2,1)S(1)} %collective-permute-done.5.refs_2_), channel_id=1, source_target_pairs={{0,14},{2,0},{4,2},{6,4},{8,6},{10,8},{12,10},{14,12},{1,15},{3,1}... | collective-permute-start | bytes 786440 | tf_op jit(solution)/shard_map/ppermute | solution.py:362
  54.6 17.1 %copy-start.5 = (bf16[128,1024]{1,0:T(8,128)(2,1)}, bf16[128,1024]{1,0:T(8,128)(2,1)S(1)}, u32[]{:S(2)}) copy-start(bf16[128,1024]{1,0:T(8,128)(2,1)S(1)} %collective-permute-done.2.refs_3_) | copy-start | bytes 786436
  54.6 8.3 %collective-permute-start.3 = (bf16[128,1024]{1,0:T(8,128)(2,1)S(1)}, bf16[128,1024]{1,0:T(8,128)(2,1)S(1)}, u32[]{:S(2)}, u32[]{:S(2)}) collective-permute-start(bf16[128,1024]{1,0:T(8,128)(2,1)S(1)} %collective-permute-done.2.refs_3_), channel_id=1, source_target_pairs={{0,2},{2,4},{4,6},{6,8},{8,10},{10,12},{12,14},{14,0},{1,3},{3,5},... | collective-permute-start | bytes 786440 | tf_op jit(solution)/shard_map/ppermute | solution.py:361
  56.5 15.2 %copy-start.6 = (bf16[128,1024]{1,0:T(8,128)(2,1)}, bf16[128,1024]{1,0:T(8,128)(2,1)S(1)}, u32[]{:S(2)}) copy-start(bf16[128,1024]{1,0:T(8,128)(2,1)S(1)} %collective-permute-done.6.refs_4_) | copy-start | bytes 786436
  56.5 8.3 %collective-permute-start.7 = (bf16[128,1024]{1,0:T(8,128)(2,1)S(1)}, bf16[128,1024]{1,0:T(8,128)(2,1)S(1)}, u32[]{:S(2)}, u32[]{:S(2)}) collective-permute-start(bf16[128,1024]{1,0:T(8,128)(2,1)S(1)} %collective-permute-done.6.refs_4_), channel_id=1, source_target_pairs={{0,14},{2,0},{4,2},{6,4},{8,6},{10,8},{12,10},{14,12},{1,15},{3,1}... | collective-permute-start | bytes 786440 | tf_op jit(solution)/shard_map/ppermute | solution.py:362
  62.9 8.8 %copy-start.7 = (bf16[128,1024]{1,0:T(8,128)(2,1)}, bf16[128,1024]{1,0:T(8,128)(2,1)S(1)}, u32[]{:S(2)}) copy-start(bf16[128,1024]{1,0:T(8,128)(2,1)S(1)} %collective-permute-done.3.refs_5_) | copy-start | bytes 786436
  62.9 8.8 %collective-permute-start.4 = (bf16[128,1024]{1,0:T(8,128)(2,1)S(1)}, bf16[128,1024]{1,0:T(8,128)(2,1)S(1)}, u32[]{:S(2)}, u32[]{:S(2)}) collective-permute-start(bf16[128,1024]{1,0:T(8,128)(2,1)S(1)} %collective-permute-done.3.refs_5_), channel_id=1, source_target_pairs={{0,2},{2,4},{4,6},{6,8},{8,10},{10,12},{12,14},{14,0},{1,3},{3,5},... | collective-permute-start | bytes 786440 | tf_op jit(solution)/shard_map/ppermute | solution.py:364
  64.8 6.9 %copy-start.8 = (bf16[128,1024]{1,0:T(8,128)(2,1)}, bf16[128,1024]{1,0:T(8,128)(2,1)S(1)}, u32[]{:S(2)}) copy-start(bf16[128,1024]{1,0:T(8,128)(2,1)S(1)} %collective-permute-done.7.refs_6_) | copy-start | bytes 786436
  74.0 12.4 %collective-permute-start.8 = (f32[264,1024]{1,0:T(8,128)S(1)}, f32[264,1024]{1,0:T(8,128)}, u32[]{:S(2)}, u32[]{:S(2)}) collective-permute-start(f32[264,1024]{1,0:T(8,128)S(1)} %shard_map.49.sent_ref), channel_id=1, source_target_pairs={{0,1},{1,0},{2,3},{3,2},{4,5},{5,4},{6,7},{7,6},{8,9},{9,8},{10,11... | collective-permute-start | bytes 3244040 | tf_op jit(solution)/shard_map/ppermute | solution.py:385
  84.1 2.2 %copy-start.1 = (s32[1024]{0:T(1024)S(1)}, s32[1024]{0:T(1024)}, u32[]{:S(2)}) copy-start(s32[1024]{0:T(1024)} %param.6) | copy-start | bytes 12292
  86.4 23.1 %copy-start = (f32[256,256]{1,0:T(8,128)S(1)}, f32[256,256]{1,0:T(8,128)}, u32[]{:S(2)}) copy-start(f32[256,256]{1,0:T(8,128)} %pre_ref.3) | copy-start | bytes 786436
